TPU v7x, 128 devices: a whole 4x4x4 slice. The times are simulated.
128 devices in a mesh: aa: 16 (over y, x), ba: 8 (over z, core).
Axes of the slice: x: 4, y: 4, z: 4, core: 2. Of those that a mesh axis runs over, the one named last changes fastest.
Arguments:
- queries: bfloat16 [8, 128, 8192], P('ba', None, 'aa'), may hold values from -10 to 10
- new_kv: bfloat16 [8, 128, 2, 512], P('ba', 'aa'), may hold values from -4 to 4
- pool: bfloat16 [8, 192, 32, 2, 512], P('ba', 'aa'), may hold values from -4 to 4
- page_table: int32 [8, 64], P('ba', 'aa'), may hold values from 0 to 11, as said below
- ctx_len: int32 [8, 16], P('ba', 'aa'), may hold values from 1 to 128, as said below
- move_page: int32 [8, 112], P('ba', 'aa'), may hold values from 0 to 11, as said below
- move_dest: int32 [8, 112], P('ba', 'aa'), may hold values from 0 to 7, as said below
- append_page: int32 [8, 16], P('ba', 'aa'), may hold values from 0 to 11
Outputs:
- attended: bfloat16 [8, 128, 8192], P('ba', None, 'aa')
- pool_out: bfloat16 [8, 192, 32, 2, 512], P('ba', 'aa')
Inputs may be any that keep to these rules, and one draw needn't show every extreme that they name: `page_table`: the entries of one device are distinct pages of its pool and differ from its leaving pages and its append page. `ctx_len`: for each instance some index of aa holds exactly 128 live rows. `move_page`: the 7 entries of one device are distinct pages of its pool. `move_dest`: A device never names its own instance and names any one instance at most 2 times; for each index of aa one instance is named exactly 2 times by the device of every other instance.
All inputs are finite; a program needn't handle non-finite values.
Results may differ from a plain program's by a relative error of at most 0.0017.
Values may be sent and summed in bfloat16 or wider, within the bound.
No kernel may reach another device: no remote copies, remote signals or barrier semaphores. Data moves between devices by JAX's collectives and lax.ppermute only.
A program may use at most 64 MiB of HBM per device.

v0:
```python
import math

import jax
import jax.numpy as jnp
from jax import lax
from jax.sharding import PartitionSpec as P

HEAD_DIM = 128
MOST = 2


NEG_LARGE = -1e30


def in_one_piece(arrays, axis, split_dim, concat_dim, along):
    widths = [math.prod(a.shape[along:]) for a in arrays]
    both = jnp.concatenate(
        [a.reshape(*a.shape[:along], w) for a, w in zip(arrays, widths)], axis=along
    )
    filled = lax.all_to_all(both, axis, split_axis=split_dim, concat_axis=concat_dim, tiled=True)
    blocks = jnp.split(filled, [sum(widths[:k]) for k in range(1, len(widths))], axis=along)
    return tuple(
        (b.reshape(*filled.shape[:along], *a.shape[along:]) for a, b in zip(arrays, blocks))
    )


def from_everyone(value, axis):
    length = lax.axis_size(axis)
    return lax.all_to_all(
        jnp.broadcast_to(value[None], (length, *value.shape)), axis, 0, 0, tiled=True
    )


def taken_together(value, axis):
    return from_everyone(value, axis).max(axis=0)


def split_up(value, dim, length):
    lengths = value.shape
    blocks = value.reshape(*lengths[:dim], length, lengths[dim] // length, *lengths[dim + 1 :])
    return jnp.moveaxis(blocks, dim, 0)


def sum_at_owner(value, axis, dim):
    length = lax.axis_size(axis)
    blocks = lax.all_to_all(split_up(value, dim, length), axis, 0, 0, tiled=True)
    return jnp.sum(blocks, axis=0)


def in_one_piece_2(arrays, axis, dim, along):
    widths = [math.prod(a.shape[along:]) for a in arrays]
    both = jnp.concatenate(
        [a.reshape(*a.shape[:along], w) for a, w in zip(arrays, widths)], axis=along
    )
    filled = sum_at_owner(both, axis, dim)
    blocks = jnp.split(filled, [sum(widths[:k]) for k in range(1, len(widths))], axis=along)
    return tuple(
        (b.reshape(*filled.shape[:along], *a.shape[along:]) for a, b in zip(arrays, blocks))
    )


def block_plan(total_rows):
    counted = max(1, total_rows // 512)
    length = -(-total_rows // counted)
    length = -(-length // 8) * 8
    return (counted, length)


def combine_parts(former, latter):
    former_max, former_sum, former_out = former
    latter_max, latter_sum, latter_out = latter
    joint_max = jnp.maximum(former_max, latter_max)
    former_scale = jnp.exp(former_max - joint_max)
    latter_scale = jnp.exp(latter_max - joint_max)
    joint_sum = former_sum * former_scale + latter_sum * latter_scale
    joint_out = former_out * former_scale[..., None] + latter_out * latter_scale[..., None]
    return (joint_max, joint_sum, joint_out)


def attend_rows(query_heads, key_rows, visible):
    total_rows = key_rows.shape[0]
    counted, length = block_plan(total_rows)
    query_count, kv_heads, group_size, head_dim = query_heads.shape
    blocked_keys = key_rows.reshape(counted, length, 2, kv_heads, head_dim)
    blocked_mask = visible.reshape(query_count, counted, length).transpose(1, 0, 2)
    scale = 1.0 / math.sqrt(head_dim)

    def block_step(state_now, inputs):
        run_max, run_sum, run_out = state_now
        block_keys, block_mask = inputs
        scores = (
            jnp.einsum(
                "qkgd,rkd->qkgr", query_heads, block_keys[:, 0], preferred_element_type=jnp.float32
            )
            * scale
        )
        allowed = block_mask[:, None, None, :]
        scores = jnp.where(allowed, scores, NEG_LARGE)
        new_max = jnp.maximum(run_max, jnp.max(scores, axis=-1))
        weights = jnp.where(allowed, jnp.exp(scores - new_max[..., None]), 0.0)
        shrink = jnp.exp(run_max - new_max)
        new_sum = run_sum * shrink + jnp.sum(weights, axis=-1)
        block_values = block_keys[:, 1].astype(jnp.float32)
        new_out = run_out * shrink[..., None] + jnp.einsum(
            "qkgr,rkd->qkgd", weights, block_values, precision=lax.Precision.HIGHEST
        )
        return ((new_max, new_sum, new_out), None)

    start_state = (
        jnp.full((query_count, kv_heads, group_size), NEG_LARGE, jnp.float32),
        jnp.zeros((query_count, kv_heads, group_size), jnp.float32),
        jnp.zeros((query_count, kv_heads, group_size, head_dim), jnp.float32),
    )
    finished, _ = lax.scan(block_step, start_state, (blocked_keys, blocked_mask))
    return finished


def local(queries, new_kv, pool, page_table, ctx_len, move_page, move_dest, append_page):
    instances = lax.axis_size("ba")
    position = lax.axis_index("aa")
    pool_pages = pool[0]
    page_rows = pool_pages.shape[1]
    kv_width = pool_pages.shape[-1]
    kv_heads = kv_width // HEAD_DIM
    gathered = lax.all_gather(queries[0], "aa", axis=1, tiled=True)
    query_count = gathered.shape[0]
    query_heads = gathered.reshape(query_count, kv_heads, -1, HEAD_DIM)
    moved_ids = move_page[0]
    targets = move_dest[0]
    move_count = moved_ids.shape[0]
    counter = jnp.arange(move_count, dtype=jnp.int32)
    earlier = (counter[None, :] < counter[:, None]) & (targets[None, :] == targets[:, None])
    slot_index = targets * MOST + jnp.sum(earlier, axis=1)
    select = (jnp.arange(instances * MOST, dtype=jnp.int32)[:, None] == slot_index[None, :]).astype(
        jnp.bfloat16
    )
    picked = jnp.take(pool_pages, moved_ids, axis=0).reshape(move_count, -1)
    outgoing = jnp.dot(select, picked, preferred_element_type=jnp.float32).astype(jnp.bfloat16)
    outgoing = outgoing.reshape(instances, MOST, page_rows, 2, kv_width)
    occupied = (
        jnp.sum(select.astype(jnp.float32), axis=1).astype(jnp.bfloat16).reshape(instances, MOST)
    )
    incoming, arrived = in_one_piece((outgoing, occupied), "ba", 0, 0, 2)
    moved_rows = incoming.reshape(-1, 2, kv_width)
    moved_live = jnp.broadcast_to(
        (arrived > 0.5)[:, :, None], (instances, MOST, page_rows)
    ).reshape(-1)
    resident = jnp.take(pool_pages, page_table[0], axis=0).reshape(-1, 2, kv_width)
    resident_live = jnp.arange(resident.shape[0], dtype=jnp.int32) < ctx_len[0, 0]
    fresh_rows = new_kv[0]
    fresh_count = fresh_rows.shape[0]
    fresh_place = position * fresh_count + jnp.arange(fresh_count, dtype=jnp.int32)
    fresh_visible = fresh_place[None, :] <= jnp.arange(query_count, dtype=jnp.int32)[:, None]
    resident_visible = jnp.broadcast_to(
        resident_live[None, :], (query_count, resident_live.shape[0])
    )
    moved_visible = jnp.broadcast_to(moved_live[None, :], (query_count, moved_live.shape[0]))
    local_part = attend_rows(
        query_heads,
        jnp.concatenate([resident, fresh_rows], axis=0),
        jnp.concatenate([resident_visible, fresh_visible], axis=1),
    )
    moved_part = attend_rows(query_heads, moved_rows, moved_visible)
    partials = combine_parts(local_part, moved_part)
    run_max, run_sum, run_out = partials
    top_max = taken_together(run_max, "aa")
    rescale = jnp.exp(run_max - top_max)
    numerator = (run_out * rescale[..., None]).reshape(query_count, -1, HEAD_DIM)
    denominator = (run_sum * rescale).reshape(query_count, -1)
    numerator, denominator = in_one_piece_2((numerator, denominator), "aa", 1, 2)
    result = numerator / denominator[..., None]
    attended = result.reshape(1, query_count, -1).astype(jnp.bfloat16)
    zero = jnp.zeros((), jnp.int32)
    updated = lax.dynamic_update_slice(
        pool_pages, fresh_rows[None], (append_page[0, 0], zero, zero, zero)
    )
    return (attended, updated[None])


def solution(mesh):
    return jax.shard_map(
        local,
        mesh=mesh,
        in_specs=(
            P("ba", None, "aa"),
            P("ba", "aa", None, None),
            P("ba", "aa", None, None, None),
            P("ba", "aa"),
            P("ba", "aa"),
            P("ba", "aa"),
            P("ba", "aa"),
            P("ba", "aa"),
        ),
        out_specs=(P("ba", None, "aa"), P("ba", "aa", None, None, None)),
        check_vma=False,
    )
```

profile of v0, /device:TPU:0, one launch (start us, length us, event | category | flops | bytes accessed | tf_op | source)
XLA Modules:
  0.0 190.3 jit_solution(174172654630481055)
XLA Ops:
  7.2 1.1 copy.173
  8.3 1.7 copy.132
  11.4 0.9 convert_reduce_fusion
  13.1 1.5 gather_fusion.1
  16.2 1.9 %pad_maximum_fusion = bf16[8,2,32769]{2,1,0:T(2,128)(2,1)} fusion(bf16[8,2,1]{2,1,0:T(2,128)(2,1)S(1)} %reshape_reshape.9, bf16[8,2,32768]{2,1,0:T(2,128)(2,1)S(1)} %reshape_reshape.7), kind=kLoop, calls=%fused_computation.33 | loop fusion | flops 2097216 | bytes 2097216 | tf_op jit(solution)/shard_map/concatenate | solution.py:17
  18.2 5.4 %all-to-all-start = ((bf16[8,2,32769]{2,1,0:T(2,128)(2,1)}), bf16[8,2,32769]{2,1,0:T(2,128)(2,1)S(1)}, u32[]{:S(2)}, u32[]{:S(2)}) async-start(bf16[8,2,32769]{2,1,0:T(2,128)(2,1)} %pad_maximum_fusion), calls=%async_computation | async-start | bytes 2105344 | tf_op jit(solution)/shard_map/all_to_all | solution.py:20
  24.5 1.1 gather_fusion
  26.0 13.6 %all-to-all-done = bf16[8,2,32769]{2,1,0:T(2,128)(2,1)S(1)} async-done(((bf16[8,2,32769]{2,1,0:T(2,128)(2,1)}), bf16[8,2,32769]{2,1,0:T(2,128)(2,1)S(1)}, u32[]{:S(2)}, u32[]{:S(2)}) %all-to-all-start) | async-done | bytes 1048640 | tf_op jit(solution)/shard_map/all_to_all | solution.py:20
  40.4 0.8 squeeze.63
  41.6 1.1 copy.158
  43.0 15.0 %all-gather.3.cloned.1.call-done = bf16[1,128,8192]{1,2,0:T(8,128)(2,1)} async-done(((bf16[1,128,512]{1,2,0:T(8,128)(2,1)}), bf16[1,128,8192]{1,2,0:T(8,128)(2,1)}) %all-gather.3.cloned.1.call-update) | async-done | bytes 2097168 | tf_op jit(solution)/shard_map/all_gather | solution.py:125
  58.1 8.9 %bitcast_reduce_fusion = (f32[128,4,16]{0,2,1:T(8,128)S(1)}, f32[4,512,128,16]{2,1,3,0:T(8,128)}) fusion(pred[512]{0:T(512)(128)(4,1)S(1)} %broadcast_in_dim.133, bf16[128,4,16,128]{0,3,2,1:T(8,128)(2,1)} %bitcast.111, bf16[512,1,4,128]{3,2,1,0:T(4,128)(2,1)S(1)} %get-tuple-element.59), kind=kOutput, calls=%fused_computation.4 | convolution fusion | flops 1086316544 | bytes 19431936 | tf_op jit(solution)/shard_map/while/body/eval_jaxpr/qkgd,rkd->qkgr/dot_general | solution.py:92
  66.9 2.9 %fusion.15 = (f32[128,4,16]{0,2,1:T(8,128)S(1)}, f32[4,136,128,16]{2,1,3,0:T(8,128)}) fusion(pred[128,136]{0,1:T(8,128)(4,1)S(1)} %pad_add_fusion, bf16[128,4,16,128]{0,3,2,1:T(8,128)(2,1)S(1)} %bitcast.112, bf16[128,2,4,128]{3,0,2,1:T(8,128)(2,1)S(1)} %copy_select_fusion, bf16[8,2,4,128]{3,0,2,1:T(8,128)(2,1)S(1)} %copy.131), kind=kOutput, calls=%fused_computation.25 | convolution fusion | flops 288825344 | bytes 6882304 | tf_op jit(solution)/shard_map/while/body/eval_jaxpr/qkgd,rkd->qkgr/dot_general | solution.py:92
  69.8 0.8 broadcast_in_dim.138
  70.7 5.1 %all-to-all-start.1 = ((f32[16,128,4,16]{1,3,2,0:T(8,128)}), f32[16,128,4,16]{1,3,2,0:T(8,128)S(1)}, u32[]{:S(2)}, u32[]{:S(2)}) async-start(f32[16,128,4,16]{1,3,2,0:T(8,128)} %broadcast_in_dim.138), calls=%async_computation.1 | async-start | bytes 1048576 | tf_op jit(solution)/shard_map/all_to_all | solution.py:29
  75.8 8.5 %fusion.2 = f32[128,4,16]{0,2,1:T(8,128)S(1)} fusion(f32[4,512,128,16]{2,1,3,0:T(8,128)} %get-tuple-element.69, f32[128,4,16]{0,2,1:T(8,128)S(1)} %get-tuple-element.62, pred[512]{0:T(512)(128)(4,1)S(1)} %broadcast_in_dim.133), kind=kLoop, calls=%fused_computation.8 | loop fusion | flops 20963328 | bytes 16843264 | tf_op jit(solution)/shard_map/while/body/eval_jaxpr/reduce_sum | solution.py:102
  84.3 1.3 fusion.16
  85.7 5.3 %fusion.17 = f32[4,128,128,16]{2,1,3,0:T(8,128)} fusion(f32[4,136,128,16]{2,1,3,0:T(8,128)S(1)} %bitcast.110, f32[128,4,16]{0,2,1:T(8,128)S(1)} %get-tuple-element.65, pred[128,136]{0,1:T(8,128)(4,1)S(1)} %pad_add_fusion, bf16[8,2,4,128]{3,0,2,1:T(8,128)(2,1)S(1)} %copy.131, bf16[128,2,4,128]{3,0,2,1:T(8,128)(2,1)S(1)} %copy_select_fusion), kind=kOutput, calls=%fused_computation.27 | convolution fusion | flops 1716011008 | bytes 8979456 | tf_op jit(solution)/shard_map/while/body/eval_jaxpr/qkgr,rkd->qkgd/dot_general | solution.py:104
  91.0 15.8 %fusion.13 = f32[128,4,16,128]{0,3,2,1:T(8,128)S(1)} fusion(f32[4,128,128,16]{2,1,3,0:T(8,128)} %fusion.17, f32[4,512,128,16]{2,1,3,0:T(8,128)} %get-tuple-element.69, f32[128,4,16]{0,2,1:T(8,128)S(1)} %get-tuple-element.62, pred[512]{0:T(512)(128)(4,1)S(1)} %broadcast_in_dim.133, f32[128,4,16]{0,2,1:T(8,128)S(1)} %get-tuple-element.64, ...), kind=kOutput, calls=%fused_computation.22 | convolution fusion | flops 6465519616 | bytes 25887232 | tf_op jit(solution)/shard_map/while/body/eval_jaxpr/qkgr,rkd->qkgd/dot_general | solution.py:104
  106.8 2.8 %copy.141 = f32[128,16,4,128]{0,2,3,1:T(4,128)S(1)} copy(f32[128,16,4,128]{0,3,2,1:T(8,128)S(1)} %bitcast.113) | data formatting | bytes 8388608 | tf_op jit(solution)/shard_map/concatenate | solution.py:52
  109.6 3.0 %maximum_bitcast_fusion = f32[16,128,4,129]{1,2,3,0:T(4,128)} fusion(f32[128,16,4,1]{0,2,3,1:T(4,128)S(1)} %exponential_multiply_fusion, f32[128,16,4,128]{0,2,3,1:T(4,128)S(1)} %copy.141), kind=kLoop, calls=%fused_computation.18 | loop fusion | flops 1056768 | bytes 8454144 | tf_op jit(solution)/shard_map/transpose | solution.py:41
  112.6 7.3 %all-to-all-start.2 = ((f32[16,128,4,129]{1,2,3,0:T(4,128)}), f32[16,128,4,129]{1,2,3,0:T(4,128)}, u32[]{:S(2)}, u32[]{:S(2)}) async-start(f32[16,128,4,129]{1,2,3,0:T(4,128)} %maximum_bitcast_fusion), calls=%async_computation.2 | async-start | bytes 8454144 | tf_op jit(solution)/shard_map/all_to_all | solution.py:46
  120.5 59.2 %all-to-all-done.2 = f32[16,128,4,129]{1,2,3,0:T(4,128)} async-done(((f32[16,128,4,129]{1,2,3,0:T(4,128)}), f32[16,128,4,129]{1,2,3,0:T(4,128)}, u32[]{:S(2)}, u32[]{:S(2)}) %all-to-all-start.2) | async-done | bytes 4227104 | tf_op jit(solution)/shard_map/all_to_all | solution.py:46
  179.7 2.9 %reduce_sum.63 = f32[128,4,129]{0,1,2:T(4,128)S(1)} reduce(f32[16,128,4,129]{1,2,3,0:T(4,128)} %all-to-all-done.2, f32[]{:T(128)} %constant.52.clone.1), dimensions={0}, to_apply=%region_7.8 | reduce | flops 990720 | bytes 4491268 | tf_op jit(solution)/shard_map/reduce_sum | solution.py:47
  (58 shorter events, 7.0 us)
Async XLA Ops:
  7.2 50.9 %all-gather.3.cloned.1.call-start = ((), (), s32[]{:S(2)}) async-start(), calls=%async_computation.3 | async-start | bytes 2228224 | tf_op jit(solution)/shard_map/all_gather | solution.py:125
  14.6 9.0 %copy-start.4 = (s32[1,4]{1,0:T(1,128)S(1)}, s32[1,4]{1,0:T(1,128)}, u32[]{:S(2)}) copy-start(s32[1,4]{1,0:T(1,128)} %param.11) | copy-start | bytes 52
  14.6 9.8 %copy-start.3 = (bf16[1,8,2,512]{3,2,1,0:T(2,128)(2,1)S(1)}, bf16[1,8,2,512]{3,2,1,0:T(2,128)(2,1)}, u32[]{:S(2)}) copy-start(bf16[1,8,2,512]{3,2,1,0:T(2,128)(2,1)} %param.9) | copy-start | bytes 49156
  18.2 21.4 %all-to-all-start = ((bf16[8,2,32769]{2,1,0:T(2,128)(2,1)}), bf16[8,2,32769]{2,1,0:T(2,128)(2,1)S(1)}, u32[]{:S(2)}, u32[]{:S(2)}) async-start(bf16[8,2,32769]{2,1,0:T(2,128)(2,1)} %pad_maximum_fusion), calls=%async_computation | async-start | bytes 2105344 | tf_op jit(solution)/shard_map/all_to_all | solution.py:20
  58.0 8.9 %copy-start = (bf16[1,128,8192]{1,2,0:T(8,128)(2,1)S(1)}, bf16[1,128,8192]{1,2,0:T(8,128)(2,1)}, u32[]{:S(2)}) copy-start(bf16[1,128,8192]{1,2,0:T(8,128)(2,1)} %all-gather.3.cloned.1.call-done) | copy-start | bytes 6291460
  70.7 13.6 %slice-start = ((s8[4456448]{0:T(1024)(128)(4,1)}), s8[262144]{0:T(1024)(128)(4,1)S(1)}, s32[]{:S(2)}) async-start(s8[4456448]{0:T(1024)(128)(4,1)} %bitcast.109), calls=%async_computation.4 | async-start | bytes 524288
  70.7 20.2 %all-to-all-start.1 = ((f32[16,128,4,16]{1,3,2,0:T(8,128)}), f32[16,128,4,16]{1,3,2,0:T(8,128)S(1)}, u32[]{:S(2)}, u32[]{:S(2)}) async-start(f32[16,128,4,16]{1,3,2,0:T(8,128)} %broadcast_in_dim.138), calls=%async_computation.1 | async-start | bytes 1048576 | tf_op jit(solution)/shard_map/all_to_all | solution.py:29
  75.8 8.6 %slice-start.1 = ((s8[4456448]{0:T(1024)(128)(4,1)}), s8[4194304]{0:T(1024)(128)(4,1)S(1)}, s32[]{:S(2)}) async-start(s8[4456448]{0:T(1024)(128)(4,1)} %bitcast.109), calls=%async_computation.5 | async-start | bytes 8388608
  85.6 5.3 %copy-start.2 = (bf16[512,1,4,128]{0,3,2,1:T(8,128)(2,1)S(1)}, bf16[512,1,4,128]{0,3,2,1:T(8,128)(2,1)}, u32[]{:S(2)}) copy-start(bf16[512,1,4,128]{0,3,2,1:T(8,128)(2,1)} %copy.158) | copy-start | bytes 1572868
  112.6 67.1 %all-to-all-start.2 = ((f32[16,128,4,129]{1,2,3,0:T(4,128)}), f32[16,128,4,129]{1,2,3,0:T(4,128)}, u32[]{:S(2)}, u32[]{:S(2)}) async-start(f32[16,128,4,129]{1,2,3,0:T(4,128)} %maximum_bitcast_fusion), calls=%async_computation.2 | async-start | bytes 8454144 | tf_op jit(solution)/shard_map/all_to_all | solution.py:46
  120.5 62.9 %copy-start.1 = (bf16[1,12,32,2,512]{4,3,2,1,0:T(2,128)(2,1)}, bf16[1,12,32,2,512]{4,3,2,1,0:T(2,128)(2,1)S(1)}, u32[]{:S(2)}) copy-start(bf16[1,12,32,2,512]{4,3,2,1,0:T(2,128)(2,1)S(1)} %bitcast_dynamic-update-slice_fusion) | copy-start | bytes 2359300
Sparse Core Ops, SparseCore 0:
  10.7 47.2 all-gather.2
where the time goes:
time: 191 us; the launch traced here: 190 us
  waiting for transfers between devices  87.8 us (46%)
  matrix products  33.4 us (17%)
  other arithmetic  21 us (11%)
  starting transfers between devices  17.8 us (9%)
  between operations  15.6 us (8%)
  local copies, waits for them, and re-layouts  14.7 us (8%)
    all_to_all x1, waiting for transfers between devices, sum_at_owner(): lax.all_to_all(split_up(value, dim, length), axis, 0, 0, tiled=True)  59.2 us
    dot_general x2, matrix products, block_step(): jnp.einsum('qkgr,rkd->qkgd', weights, block_values, precision=lax.Precisi...  21 us
    all_gather x1, waiting for transfers between devices, local(): gathered = lax.all_gather(queries[0], 'aa', axis=1, tiled=True)  15 us
    all_to_all x1, waiting for transfers between devices, in_one_piece(): lax.all_to_all(both, axis, split_axis=split_dim, concat_axis=concat_dim,...  13.6 us
    dot_general x2, matrix products, block_step(): jnp.einsum('qkgd,rkd->qkgr', query_heads, block_keys[:, 0], preferred_ele...  11.8 us
    reduce_sum x2, other arithmetic, block_step(): new_sum = run_sum * shrink + jnp.sum(weights, axis=-1)  9.83 us
    all_to_all x1, starting transfers between devices, sum_at_owner(): lax.all_to_all(split_up(value, dim, length), axis, 0, 0, tiled=True)  7.25 us
    all_to_all x1, starting transfers between devices, in_one_piece(): lax.all_to_all(both, axis, split_axis=split_dim, concat_axis=concat_dim,...  5.39 us
  transfers between devices with their start and end apart: 4, of which 3 were waited for; matrix products, arithmetic and copies ran while one was open for 15% of the time, Pallas kernels for 0%

commit v1 on v0

v1 whole, which is shorter than its diff:
```python
import functools
import math

import jax
import jax.numpy as jnp
import numpy as np
from jax import lax
from jax.experimental import pallas as pl
from jax.experimental.pallas import tpu as pltpu
from jax.sharding import Mesh, PartitionSpec as P

D = 128
KVH = 4
MOST = 2
PAGE = 32
TABLE = 4
MOVES = 7
INST = 8
NEW_DEV = 8
NQ = 128
RES = TABLE * PAGE + NEW_DEV
DEAD = 128.0
BIG = -1e30
BF = jnp.bfloat16
F32 = jnp.float32
LOG_SCALE = math.log2(math.e) / math.sqrt(D)
MIG_BLOCKS = INST * KVH * MOST * PAGE // 128
RES_BLOCKS = TABLE * PAGE * KVH // 128
BLOCKS = MIG_BLOCKS + RES_BLOCKS + 1
ROWS = BLOCKS * 128


def pack_kernel(table, ctx, page, dest, pool, new, mig, res, dead, sem_m, sem_r):
    dead[...] = jnp.full_like(dead, DEAD)
    for y in range(KVH):
        lanes = pl.ds(y * D, D)
        for j in range(TABLE):
            pltpu.make_async_copy(
                pool.at[table[0, j], :, :, lanes], res.at[y, pl.ds(j * PAGE, PAGE)], sem_r
            ).start()
        pltpu.make_async_copy(
            new.at[:, :, lanes], res.at[y, pl.ds(TABLE * PAGE, NEW_DEV)], sem_r
        ).start()
    for m in range(MOVES):
        rank = jnp.int32(0)
        for e in range(m):
            rank += (dest[0, e] == dest[0, m]).astype(jnp.int32)
        for y in range(KVH):
            pltpu.make_async_copy(
                pool.at[page[0, m], :, :, pl.ds(y * D, D)], mig.at[dest[0, m], y, rank], sem_m
            ).start()
    for d in range(INST):
        count = jnp.int32(0)
        for m in range(MOVES):
            count += (dest[0, m] == d).astype(jnp.int32)
        for s in range(MOST):

            @pl.when(count <= s)
            def _():
                pltpu.make_async_copy(dead, mig.at[d, :, s], sem_m).start()

    pltpu.make_async_copy(res, res, sem_r).wait()
    index = lax.broadcasted_iota(jnp.int32, (TABLE * PAGE, 2, D), 0)
    alive = index < ctx[0, 0]
    for y in range(KVH):
        part = res[y, : TABLE * PAGE].astype(F32)
        res[y, : TABLE * PAGE] = jnp.where(alive, part, DEAD).astype(BF)
    pltpu.make_async_copy(mig, mig, sem_m).wait()


def pack(table, ctx, page, dest, pool, new):
    smem = pl.BlockSpec(memory_space=pltpu.SMEM)
    hbm = pl.BlockSpec(memory_space=pl.ANY)
    vmem = pl.BlockSpec(memory_space=pltpu.VMEM)
    return pl.pallas_call(
        pack_kernel,
        in_specs=[smem] * 4 + [hbm] * 2,
        out_specs=[hbm, vmem],
        out_shape=[
            jax.ShapeDtypeStruct((INST, KVH, MOST, PAGE, 2, D), BF),
            jax.ShapeDtypeStruct((KVH, RES, 2, D), BF),
        ],
        scratch_shapes=[
            pltpu.VMEM((KVH, PAGE, 2, D), BF),
            pltpu.SemaphoreType.DMA,
            pltpu.SemaphoreType.DMA,
        ],
        compiler_params=pltpu.CompilerParams(vmem_limit_bytes=16 << 20),
    )(table, ctx, page, dest, pool, new)


def attend_kernel(
    place, q0, q1, q2, q3, mig, res, new, o_ref, n_ref, d_ref, kt, vv, sc, aug
):
    row = lax.broadcasted_iota(jnp.int32, (256, 256), 0)
    col = lax.broadcasted_iota(jnp.int32, (256, 256), 1)
    pick = (row == jnp.where(col < 128, 2 * col, 2 * col - 255)).astype(BF)
    sub = lax.broadcasted_iota(jnp.int32, (128, 128), 0)
    lane = lax.broadcasted_iota(jnp.int32, (128, 128), 1)

    def put(b, x):
        both = lax.dot_general(x, pick, (((0,), (0,)), ((), ())), preferred_element_type=F32)
        keys = both[:, :128]
        cols = pl.ds(pl.multiple_of(b * 128, 128), 128)
        kt[0:128, cols] = keys.astype(BF)
        kt[128:256, cols] = jnp.where((sub == 0) & (keys > 64.0), BIG, 0.0).astype(BF)
        vals = lax.dot_general(
            pick[:, 128:], x, (((0,), (0,)), ((), ())), preferred_element_type=F32
        )
        rows = pl.ds(pl.multiple_of(b * 128, 128), 128)
        vv[rows, 0:128] = vals.astype(BF)
        vv[rows, 128:256] = jnp.ones((128, 128), BF)

    def mig_step(b, c):
        put(b, mig[b])
        return c

    lax.fori_loop(0, MIG_BLOCKS, mig_step, 0)

    def res_step(b, c):
        put(MIG_BLOCKS + b, res[b])
        return c

    lax.fori_loop(0, RES_BLOCKS, res_step, 0)
    last = BLOCKS - 1
    put(last, jnp.concatenate([new[...], jnp.zeros((192, 128), BF)], axis=0))
    hot = jnp.where((sub == 1 + lane) & (lane < 32), 1.0, 0.0)
    kt[128:256, last * 128 :] = jnp.where((sub == 0) & (lane >= 32), BIG, hot).astype(BF)
    j = lane - 1
    pos = (j // 8) * 32 + place[0] * 8 + j % 8
    bar = jnp.where((lane >= 1) & (lane < 33) & (pos > sub), BIG, 0.0)
    aug[...] = jnp.where(lane == 0, 1.0, bar).astype(BF)

    qs = (q0, q1, q2, q3)
    for k in range(4):
        num = jnp.zeros((128, 128), F32)
        den = jnp.zeros((128, 128), F32)
        for h in range(4):
            lanes = slice(h * D, h * D + D)
            q = jnp.concatenate([qs[k][:, lanes], aug[...]], axis=1)
            s = jnp.dot(q, kt[...], preferred_element_type=F32)
            top = jnp.max(s, axis=1, keepdims=True)
            p = jnp.exp2((s - top) * LOG_SCALE)
            high = p.astype(BF)
            low = (p - high.astype(F32)).astype(BF)
            o = jnp.dot(high, vv[...], preferred_element_type=F32)
            o += jnp.dot(low, vv[...], preferred_element_type=F32)
            total = o[:, 128:]
            mean = o[:, :128] / total
            most = jnp.maximum(jnp.max(jnp.abs(mean), axis=1, keepdims=True), 1e-30)
            o_ref[k, :, lanes] = mean / most
            lse = jnp.log2(total) + top * LOG_SCALE
            den = jnp.where(lane == h, lse, den)
            num = jnp.where(lane == h, lse + jnp.log2(most), num)
        n_ref[k] = num
        d_ref[k] = den


def attend(place, qs, mig, res, new):
    vmem = pl.BlockSpec(memory_space=pltpu.VMEM)
    return pl.pallas_call(
        attend_kernel,
        in_specs=[pl.BlockSpec(memory_space=pltpu.SMEM)] + [vmem] * 7,
        out_specs=[vmem] * 3,
        out_shape=[
            jax.ShapeDtypeStruct((4, 128, 512), F32),
            jax.ShapeDtypeStruct((4, 128, 128), F32),
            jax.ShapeDtypeStruct((4, 128, 128), F32),
        ],
        scratch_shapes=[
            pltpu.VMEM((256, ROWS), BF),
            pltpu.VMEM((ROWS, 256), BF),
            pltpu.VMEM((128, ROWS), F32),
            pltpu.VMEM((128, 128), BF),
        ],
        compiler_params=pltpu.CompilerParams(vmem_limit_bytes=56 << 20),
    )(place, *qs, mig, res, new)


def local(queries, new_kv, pool, page_table, ctx_len, move_page, move_dest, append_page):
    pool_pages = pool[0]
    fresh = new_kv[0]
    q = queries[0]
    mig, res = pack(page_table, ctx_len, move_page, move_dest, pool_pages, fresh)
    mig = mig.reshape(INST * KVH, MOST * PAGE * 2, D)
    mig = lax.all_to_all(mig, ("ba", "y"), 0, 0, tiled=True)
    res = lax.all_to_all(res.reshape(KVH, RES * 2, D), "y", 0, 0, tiled=True)
    qs = [q] + [
        lax.ppermute(q, "x", [(i, (i + k) % 4) for i in range(4)]) for k in range(1, 4)
    ]
    old = res[:, : TABLE * PAGE * 2].reshape(RES_BLOCKS, 256, D)
    new = res[:, TABLE * PAGE * 2 :].reshape(KVH * NEW_DEV * 2, D)
    place = lax.axis_index("x").astype(jnp.int32).reshape(1)
    out, num, den = attend(place, qs, mig.reshape(MIG_BLOCKS, 256, D), old, new)
    outs, nums, dens = [out[0]], [num[0, :, :4]], [den[0, :, :4]]
    for k in range(1, 4):
        stats = jnp.concatenate([num[k, :, :4], den[k, :, :4]], axis=1)
        high = lax.reduce_precision(stats, 5, 10)
        low = (stats - high).astype(jnp.float16)
        high = high.astype(jnp.float16)
        extra = jnp.concatenate([high, low], axis=1).reshape(4, 512)
        sent = jnp.concatenate([out[k].astype(jnp.float16), extra], axis=0)
        got = lax.ppermute(sent, "x", [(i, (i - k) % 4) for i in range(4)])
        extra = got[128:].reshape(128, 16).astype(F32)
        stats = extra[:, :8] + extra[:, 8:]
        outs.append(got[:128].astype(F32))
        nums.append(stats[:, :4])
        dens.append(stats[:, 4:])
    top = functools.reduce(jnp.maximum, dens)
    total = sum(jnp.exp2(x - top) for x in dens)
    result = sum(
        o.reshape(128, 4, D) * (jnp.exp2(n - top) / total)[:, :, None] for o, n in zip(outs, nums)
    )
    attended = result.reshape(1, NQ, 4 * D).astype(BF)
    zero = jnp.zeros((), jnp.int32)
    updated = lax.dynamic_update_slice(
        pool_pages, fresh[None], (append_page[0, 0], zero, zero, zero)
    )
    return attended, updated[None]


def solution(mesh):
    grid = Mesh(np.asarray(mesh.devices).reshape(4, 4, 8), ("y", "x", "ba"))
    aa = ("y", "x")
    return jax.shard_map(
        local,
        mesh=grid,
        in_specs=(
            P("ba", None, aa),
            P("ba", aa, None, None),
            P("ba", aa, None, None, None),
            P("ba", aa),
            P("ba", aa),
            P("ba", aa),
            P("ba", aa),
            P("ba", aa),
        ),
        out_specs=(P("ba", None, aa), P("ba", aa, None, None, None)),
        check_vma=False,
    )
```

time: 191 us -> 76 us (0.40)
  waiting for transfers between devices: 87.8 us -> 13.4 us
  matrix products: 33.4 us -> 0 us
  Pallas kernels: 0 us -> 21 us
  other arithmetic: 21 us -> 2.74 us
  between operations: 15.6 us -> 2.18 us
  blocking collectives: 0 us -> 11.2 us
  local copies, waits for them, and re-layouts: 14.7 us -> 7.59 us
    all_to_all x3 -> x1, waiting for transfers between devices: 72.7 us -> 4.5 us  [local(): mig = lax.all_to_all(mig, ('ba', 'y'), 0, 0, tiled=True)]
    dot_general x5 -> x0, matrix products: 33.4 us -> none  [the longest x2 21 us: block_step(): jnp.einsum('qkgr,rkd->qkgd', weights, block_values, precision=lax.Precisi...]
    pallas_call x0 -> x2, Pallas kernels: none -> 21 us  [the longest x1 19.1 us: attend(): pl.pallas_call(attend_kernel, in_specs=[pl.BlockSpec(memory_space=pltpu.S...]
    all_gather x1 -> x0, waiting for transfers between devices: 15 us -> none  [local(): gathered = lax.all_gather(queries[0], 'aa', axis=1, tiled=True)]
    reduce_sum x5 -> x0, other arithmetic: 13.7 us -> none  [the longest x2 9.83 us: block_step(): new_sum = run_sum * shrink + jnp.sum(weights, axis=-1)]
    all_to_all x3 -> x1, starting transfers between devices: 17.7 us -> 6.44 us  [local(): mig = lax.all_to_all(mig, ('ba', 'y'), 0, 0, tiled=True)]
    all_to_all x0 -> x1, blocking collectives: none -> 11.2 us  [local(): res = lax.all_to_all(res.reshape(KVH, RES * 2, D), 'y', 0, 0, tiled=True)]
    ppermute x0 -> x6, starting transfers between devices: none -> 11 us  [the longest x3 6.48 us: local(): got = lax.ppermute(sent, 'x', [(i, (i - k) % 4) for i in range(4)])]
  transfers between devices with their start and end apart: 4 -> 7, of which waited for: 3 -> 6; matrix products, arithmetic and copies ran while one was open for 15% -> 3% of each run, Pallas kernels for 0% -> 0%
where the time goes in v1:
time: 76 us; the launch traced here: 75.5 us
  Pallas kernels  21 us (28%)
  starting transfers between devices  17.4 us (23%)
  waiting for transfers between devices  13.4 us (18%)
  blocking collectives  11.2 us (15%)
  local copies, waits for them, and re-layouts  7.59 us (10%)
  other arithmetic  2.74 us (4%)
  between operations  2.18 us (3%)
    pallas_call x1, Pallas kernels, attend(): pl.pallas_call(attend_kernel, in_specs=[pl.BlockSpec(memory_space=pltpu.S...  19.1 us
    all_to_all x1, blocking collectives, local(): res = lax.all_to_all(res.reshape(KVH, RES * 2, D), 'y', 0, 0, tiled=True)  11.2 us
    ppermute x3, starting transfers between devices, local(): got = lax.ppermute(sent, 'x', [(i, (i - k) % 4) for i in range(4)])  6.48 us
    all_to_all x1, starting transfers between devices, local(): mig = lax.all_to_all(mig, ('ba', 'y'), 0, 0, tiled=True)  6.44 us
    ppermute x3, waiting for transfers between devices, local(): lax.ppermute(q, 'x', [(i, (i + k) % 4) for i in range(4)])  5.98 us
    ppermute x3, starting transfers between devices, local(): lax.ppermute(q, 'x', [(i, (i + k) % 4) for i in range(4)])  4.51 us
    all_to_all x1, waiting for transfers between devices, local(): mig = lax.all_to_all(mig, ('ba', 'y'), 0, 0, tiled=True)  4.5 us
    ppermute x3, waiting for transfers between devices, local(): got = lax.ppermute(sent, 'x', [(i, (i - k) % 4) for i in range(4)])  2.96 us
  transfers between devices with their start and end apart: 7, of which 6 were waited for; matrix products, arithmetic and copies ran while one was open for 3% of the time, Pallas kernels for 0%

profile of v1, /device:TPU:0, one launch (start us, length us, event | category | flops | bytes accessed | tf_op | source)
XLA Modules:
  0.0 75.5 jit_solution(8569448218232366598)
XLA Ops:
  0.6 1.1 %copy.48 = bf16[1,12,32,2,512]{4,3,2,1,0:T(2,128)(2,1)S(1)} copy(bf16[1,12,32,2,512]{4,3,2,1,0:T(2,128)(2,1)} %param.10) | data formatting | bytes 1572864
  2.5 0.6 copy-done.2
  3.1 1.9 %shard_map.95 = (bf16[8,4,2,32,2,128]{5,4,3,2,1,0:T(2,128)(2,1)}, bf16[4,136,2,128]{3,2,1,0:T(2,128)(2,1)S(1)}) custom-call(s32[1,4]{1,0:T(1,128)S(1)} %copy-done.2, s32[1,1]{1,0:T(1,128)S(6)} %copy.46.ctx, s32[1,7]{1,0:T(1,128)S(1)} %copy-done.3, s32[1,7]{1,0:T(1,128)S(1)} %copy-done.4, bf16[12,32,2,512]{3,2,1,0:T(2,128)(2,1)S(1)} %bitcast.99, ...), custom_call_target="tpu_custom_call" | custom-call | tf_op jit(solution)/shard_map/pallas_call | solution.py:75
  5.0 11.2 %all_to_all.10 = bf16[4,272,128]{2,1,0:T(8,128)(2,1)S(1)} all-to-all(bf16[4,272,128]{2,1,0:T(8,128)(2,1)S(1)} %bitcast.100), channel_id=1, replica_groups=mesh['y'=4,'x'=4,'ba'=8] {'y'}, dimensions={0} | all-to-all | bytes 557056 | tf_op jit(solution)/shard_map/all_to_all | solution.py:187
  16.2 6.4 %all-to-all-start = ((bf16[32,128,128]{2,1,0:T(8,128)(2,1)}), bf16[32,128,128]{2,1,0:T(8,128)(2,1)S(1)}, u32[]{:S(2)}, u32[]{:S(2)}) async-start(bf16[32,128,128]{2,1,0:T(8,128)(2,1)} %bitcast.4), calls=%async_computation | async-start | bytes 2097152 | tf_op jit(solution)/shard_map/all_to_all | solution.py:186
  22.7 2.8 %collective-permute-start.2 = (bf16[128,512]{1,0:T(8,128)(2,1)S(1)}, bf16[128,512]{1,0:T(8,128)(2,1)S(1)}, u32[]{:S(2)}, u32[]{:S(2)}) collective-permute-start(bf16[128,512]{1,0:T(8,128)(2,1)S(1)} %bitcast.108), channel_id=1, source_target_pairs={{0,24},{8,0},{16,8},{24,16},{1,25},{9,1},{17,9},{25,17},{2,26},{10... | collective-permute-start | bytes 393224 | tf_op jit(solution)/shard_map/ppermute | solution.py:189
  25.5 0.8 %collective-permute-start.1 = (bf16[128,512]{1,0:T(8,128)(2,1)S(1)}, bf16[128,512]{1,0:T(8,128)(2,1)S(1)}, u32[]{:S(2)}, u32[]{:S(2)}) collective-permute-start(bf16[128,512]{1,0:T(8,128)(2,1)S(1)} %bitcast.109), channel_id=1, source_target_pairs={{0,16},{8,24},{16,0},{24,8},{1,17},{9,25},{17,1},{25,9},{2,18},{10... | collective-permute-start | bytes 393224 | tf_op jit(solution)/shard_map/ppermute | solution.py:189
  26.3 0.9 %collective-permute-start = (bf16[128,512]{1,0:T(8,128)(2,1)S(1)}, bf16[128,512]{1,0:T(8,128)(2,1)S(1)}, u32[]{:S(2)}, u32[]{:S(2)}) collective-permute-start(bf16[128,512]{1,0:T(8,128)(2,1)S(1)} %bitcast.110), channel_id=1, source_target_pairs={{0,8},{8,16},{16,24},{24,0},{1,9},{9,17},{17,25},{25,1},{2,10},{10... | collective-permute-start | bytes 393224 | tf_op jit(solution)/shard_map/ppermute | solution.py:189
  27.9 0.6 slice.132
  28.5 0.7 slice.131.res
  29.2 2.3 %collective-permute-done.2.q3 = bf16[128,512]{1,0:T(8,128)(2,1)S(1)} collective-permute-done((bf16[128,512]{1,0:T(8,128)(2,1)S(1)}, bf16[128,512]{1,0:T(8,128)(2,1)S(1)}, u32[]{:S(2)}, u32[]{:S(2)}) %collective-permute-start.2) | collective-permute-done | bytes 131104 | tf_op jit(solution)/shard_map/ppermute | solution.py:189
  31.5 1.8 %collective-permute-done.1.q2 = bf16[128,512]{1,0:T(8,128)(2,1)S(1)} collective-permute-done((bf16[128,512]{1,0:T(8,128)(2,1)S(1)}, bf16[128,512]{1,0:T(8,128)(2,1)S(1)}, u32[]{:S(2)}, u32[]{:S(2)}) %collective-permute-start.1) | collective-permute-done | bytes 131104 | tf_op jit(solution)/shard_map/ppermute | solution.py:189
  33.4 1.8 %collective-permute-done.q1 = bf16[128,512]{1,0:T(8,128)(2,1)S(1)} collective-permute-done((bf16[128,512]{1,0:T(8,128)(2,1)S(1)}, bf16[128,512]{1,0:T(8,128)(2,1)S(1)}, u32[]{:S(2)}, u32[]{:S(2)}) %collective-permute-start) | collective-permute-done | bytes 131104 | tf_op jit(solution)/shard_map/ppermute | solution.py:189
  35.2 4.5 %all-to-all-done = bf16[32,128,128]{2,1,0:T(8,128)(2,1)S(1)} async-done(((bf16[32,128,128]{2,1,0:T(8,128)(2,1)}), bf16[32,128,128]{2,1,0:T(8,128)(2,1)S(1)}, u32[]{:S(2)}, u32[]{:S(2)}) %all-to-all-start) | async-done | bytes 1048608 | tf_op jit(solution)/shard_map/all_to_all | solution.py:186
  39.7 1.0 %copy-done.5 = bf16[32,128,128]{2,1,0:T(8,128)(2,1)} copy-done((bf16[32,128,128]{2,1,0:T(8,128)(2,1)}, bf16[32,128,128]{2,1,0:T(8,128)(2,1)S(1)}, u32[]{:S(2)}) %copy-start.5) | copy-done | bytes 1048600
  40.7 19.1 %shard_map.96 = (f32[4,128,512]{2,1,0:T(8,128)}, f32[4,128,128]{2,1,0:T(8,128)}, f32[4,128,128]{2,1,0:T(8,128)}) custom-call(s32[1]{0:T(128)} %bitcast.place, bf16[128,512]{1,0:T(8,128)(2,1)} %bitcast.107, bf16[128,512]{1,0:T(8,128)(2,1)} %copy-done.10, bf16[128,512]{1,0:T(8,128)(2,1)} %copy-done.9, bf16[128,512]{1,0:T(8,128)(2,1)} %copy-done.8, ...), custom_call_target="tpu_custom_call" | custom-call | tf_op jit(solution)/shard_map/pallas_call | solution.py:161
  59.8 1.1 %slice_bitcast_fusion.7 = (f32[128,4]{1,0:T(8,128)S(1)}, f32[128,4]{1,0:T(8,128)S(1)}, f32[128,4]{1,0:T(8,128)S(1)}, f32[128,4]{1,0:T(8,128)S(1)}, f32[128,4]{1,0:T(8,128)S(1)}, /*index=5*/f32[128,4]{1,0:T(8,128)S(1)}) fusion(f32[4,128,128]{2,1,0:T(8,128)} %get-tuple-element.11, f32[4,128,128]{2,1,0:T(8,128)} %get-tuple-element.10), kind=kLoop, calls=%fused_computation.47 | loop fusion | bytes 24576 | tf_op jit(solution)/shard_map/squeeze | solution.py:197
  62.4 3.1 %collective-permute-start.4 = (f16[132,512]{1,0:T(8,128)(2,1)S(1)}, f16[132,512]{1,0:T(8,128)(2,1)S(1)}, u32[]{:S(2)}, u32[]{:S(2)}) collective-permute-start(f16[132,512]{1,0:T(8,128)(2,1)S(1)} %pad_maximum_fusion.1), channel_id=1, source_target_pairs={{0,16},{8,24},{16,0},{24,8},{1,17},{9,25},{17,1},{25,9},{2,18},{10... | collective-permute-start | bytes 405512 | tf_op jit(solution)/shard_map/ppermute | solution.py:203
  65.8 0.7 collective-permute-start.5
  66.5 2.7 %collective-permute-start.3 = (f16[132,512]{1,0:T(8,128)(2,1)S(1)}, f16[132,512]{1,0:T(8,128)(2,1)S(1)}, u32[]{:S(2)}, u32[]{:S(2)}) collective-permute-start(f16[132,512]{1,0:T(8,128)(2,1)S(1)} %pad_maximum_fusion), channel_id=1, source_target_pairs={{0,24},{8,0},{16,8},{24,16},{1,25},{9,1},{17,9},{25,17},{2,26},{10... | collective-permute-start | bytes 405512 | tf_op jit(solution)/shard_map/ppermute | solution.py:203
  69.2 0.9 %collective-permute-done.4 = f16[132,512]{1,0:T(8,128)(2,1)S(1)} collective-permute-done((f16[132,512]{1,0:T(8,128)(2,1)S(1)}, f16[132,512]{1,0:T(8,128)(2,1)S(1)}, u32[]{:S(2)}, u32[]{:S(2)}) %collective-permute-start.4) | collective-permute-done | bytes 135200 | tf_op jit(solution)/shard_map/ppermute | solution.py:203
  70.3 2.0 %collective-permute-done.5 = f16[132,512]{1,0:T(8,128)(2,1)S(1)} collective-permute-done((f16[132,512]{1,0:T(8,128)(2,1)S(1)}, f16[132,512]{1,0:T(8,128)(2,1)S(1)}, u32[]{:S(2)}, u32[]{:S(2)}) %collective-permute-start.5) | collective-permute-done | bytes 135200 | tf_op jit(solution)/shard_map/ppermute | solution.py:203
  72.8 1.0 %fusion.23 = (f32[128,4]{1,0:T(8,128)S(1)}, f32[128,4]{1,0:T(8,128)S(1)}, f32[128,4]{1,0:T(8,128)S(1)}) fusion(f32[4,128,128]{2,1,0:T(8,128)} %get-tuple-element.10, f32[128,8]{1,0:T(8,128)S(1)} %slice_add_fusion, f32[128,8]{1,0:T(8,128)S(1)} %slice_add_fusion.1, f32[128,8]{1,0:T(8,128)S(1)} %slice_add_fusion.2, f32[4,128,128]{2,1,0:T(8,128)} %get-tuple-element.11), kind=kLoop, calls=%fused_computation.42 | loop fusion | flops 8704 | bytes 16384 | tf_op jit(solution)/shard_map/div | solution.py:212
  74.7 0.9 %fusion.4 = bf16[1,128,512]{2,1,0:T(8,128)(2,1)} fusion(f32[16,8,4,128]{3,2,1,0:T(4,128)S(1)} %bitcast.106, f16[132,512]{1,0:T(8,128)(2,1)S(1)} %collective-permute-done.5, f32[16,8,4,128]{3,2,1,0:T(4,128)S(1)} %bitcast.105, f16[132,512]{1,0:T(8,128)(2,1)S(1)} %collective-permute-done.4, f32[16,8,4,128]{3,2,1,0:T(4,128)S(1)} %bitcast.103, ...), kind=kLoop, calls=%fused_computation.14 | loop fusion | flops 720896 | bytes 1835008 | tf_op jit(solution)/shard_map/convert_element_type | solution.py:214
  (59 shorter events, 3.2 us)
Async XLA Ops:
  0.6 1.8 %copy-start.1 = (bf16[1,8,2,512]{3,2,1,0:T(2,128)(2,1)S(1)}, bf16[1,8,2,512]{3,2,1,0:T(2,128)(2,1)}, u32[]{:S(2)}) copy-start(bf16[1,8,2,512]{3,2,1,0:T(2,128)(2,1)} %param.9) | copy-start | bytes 49156
  2.4 0.7 copy-start.2
  2.4 0.7 copy-start.3
  2.5 0.7 copy-start.4
  16.2 6.5 %copy-start.7 = (bf16[1,128,512]{2,1,0:T(8,128)(2,1)S(1)}, bf16[1,128,512]{2,1,0:T(8,128)(2,1)}, u32[]{:S(2)}) copy-start(bf16[1,128,512]{2,1,0:T(8,128)(2,1)} %param.8) | copy-start | bytes 393220
  16.2 23.5 %all-to-all-start = ((bf16[32,128,128]{2,1,0:T(8,128)(2,1)}), bf16[32,128,128]{2,1,0:T(8,128)(2,1)S(1)}, u32[]{:S(2)}, u32[]{:S(2)}) async-start(bf16[32,128,128]{2,1,0:T(8,128)(2,1)} %bitcast.4), calls=%async_computation | async-start | bytes 2097152 | tf_op jit(solution)/shard_map/all_to_all | solution.py:186
  22.7 8.9 %collective-permute-start.2 = (bf16[128,512]{1,0:T(8,128)(2,1)S(1)}, bf16[128,512]{1,0:T(8,128)(2,1)S(1)}, u32[]{:S(2)}, u32[]{:S(2)}) collective-permute-start(bf16[128,512]{1,0:T(8,128)(2,1)S(1)} %bitcast.108), channel_id=1, source_target_pairs={{0,24},{8,0},{16,8},{24,16},{1,25},{9,1},{17,9},{25,17},{2,26},{10... | collective-permute-start | bytes 393224 | tf_op jit(solution)/shard_map/ppermute | solution.py:189
  25.5 7.9 %collective-permute-start.1 = (bf16[128,512]{1,0:T(8,128)(2,1)S(1)}, bf16[128,512]{1,0:T(8,128)(2,1)S(1)}, u32[]{:S(2)}, u32[]{:S(2)}) collective-permute-start(bf16[128,512]{1,0:T(8,128)(2,1)S(1)} %bitcast.109), channel_id=1, source_target_pairs={{0,16},{8,24},{16,0},{24,8},{1,17},{9,25},{17,1},{25,9},{2,18},{10... | collective-permute-start | bytes 393224 | tf_op jit(solution)/shard_map/ppermute | solution.py:189
  26.3 8.9 %collective-permute-start = (bf16[128,512]{1,0:T(8,128)(2,1)S(1)}, bf16[128,512]{1,0:T(8,128)(2,1)S(1)}, u32[]{:S(2)}, u32[]{:S(2)}) collective-permute-start(bf16[128,512]{1,0:T(8,128)(2,1)S(1)} %bitcast.110), channel_id=1, source_target_pairs={{0,8},{8,16},{16,24},{24,0},{1,9},{9,17},{17,25},{25,1},{2,10},{10... | collective-permute-start | bytes 393224 | tf_op jit(solution)/shard_map/ppermute | solution.py:189
  27.9 31.9 %copy-start = (bf16[1,12,32,2,512]{4,3,2,1,0:T(2,128)(2,1)}, bf16[1,12,32,2,512]{4,3,2,1,0:T(2,128)(2,1)S(1)}, u32[]{:S(2)}) copy-start(bf16[1,12,32,2,512]{4,3,2,1,0:T(2,128)(2,1)S(1)} %bitcast_dynamic-update-slice_fusion) | copy-start | bytes 2359300
  31.5 8.2 %copy-start.8 = (bf16[128,512]{1,0:T(8,128)(2,1)}, bf16[128,512]{1,0:T(8,128)(2,1)S(1)}, u32[]{:S(2)}) copy-start(bf16[128,512]{1,0:T(8,128)(2,1)S(1)} %collective-permute-done.2.q3) | copy-start | bytes 393220
  33.4 6.3 %copy-start.9 = (bf16[128,512]{1,0:T(8,128)(2,1)}, bf16[128,512]{1,0:T(8,128)(2,1)S(1)}, u32[]{:S(2)}) copy-start(bf16[128,512]{1,0:T(8,128)(2,1)S(1)} %collective-permute-done.1.q2) | copy-start | bytes 393220
  35.2 4.5 %copy-start.10 = (bf16[128,512]{1,0:T(8,128)(2,1)}, bf16[128,512]{1,0:T(8,128)(2,1)S(1)}, u32[]{:S(2)}) copy-start(bf16[128,512]{1,0:T(8,128)(2,1)S(1)} %collective-permute-done.q1) | copy-start | bytes 393220
  39.7 1.0 %copy-start.5 = (bf16[32,128,128]{2,1,0:T(8,128)(2,1)}, bf16[32,128,128]{2,1,0:T(8,128)(2,1)S(1)}, u32[]{:S(2)}) copy-start(bf16[32,128,128]{2,1,0:T(8,128)(2,1)S(1)} %all-to-all-done) | copy-start | bytes 3145732
  59.8 2.4 %copy-start.6 = (f32[4,128,512]{2,1,0:T(8,128)S(1)}, f32[4,128,512]{2,1,0:T(8,128)}, u32[]{:S(2)}) copy-start(f32[4,128,512]{2,1,0:T(8,128)} %get-tuple-element.9) | copy-start | bytes 3145732
  62.4 7.7 %collective-permute-start.4 = (f16[132,512]{1,0:T(8,128)(2,1)S(1)}, f16[132,512]{1,0:T(8,128)(2,1)S(1)}, u32[]{:S(2)}, u32[]{:S(2)}) collective-permute-start(f16[132,512]{1,0:T(8,128)(2,1)S(1)} %pad_maximum_fusion.1), channel_id=1, source_target_pairs={{0,16},{8,24},{16,0},{24,8},{1,17},{9,25},{17,1},{25,9},{2,18},{10... | collective-permute-start | bytes 405512 | tf_op jit(solution)/shard_map/ppermute | solution.py:203
  65.8 6.6 %collective-permute-start.5 = (f16[132,512]{1,0:T(8,128)(2,1)S(1)}, f16[132,512]{1,0:T(8,128)(2,1)S(1)}, u32[]{:S(2)}, u32[]{:S(2)}) collective-permute-start(f16[132,512]{1,0:T(8,128)(2,1)S(1)} %pad_maximum_fusion.2), channel_id=1, source_target_pairs={{0,8},{8,16},{16,24},{24,0},{1,9},{9,17},{17,25},{25,1},{2,10},{10... | collective-permute-start | bytes 405512 | tf_op jit(solution)/shard_map/ppermute | solution.py:203
  66.5 6.1 %collective-permute-start.3 = (f16[132,512]{1,0:T(8,128)(2,1)S(1)}, f16[132,512]{1,0:T(8,128)(2,1)S(1)}, u32[]{:S(2)}, u32[]{:S(2)}) collective-permute-start(f16[132,512]{1,0:T(8,128)(2,1)S(1)} %pad_maximum_fusion), channel_id=1, source_target_pairs={{0,24},{8,0},{16,8},{24,16},{1,25},{9,1},{17,9},{25,17},{2,26},{10... | collective-permute-start | bytes 405512 | tf_op jit(solution)/shard_map/ppermute | solution.py:203

commit v2 on v1

v2 whole, which is shorter than its diff:
```python
import functools
import math

import jax
import jax.numpy as jnp
import numpy as np
from jax import lax
from jax.experimental import pallas as pl
from jax.experimental.pallas import tpu as pltpu
from jax.sharding import Mesh, PartitionSpec as P

D = 128
KVH = 4
MOST = 2
PAGE = 32
TABLE = 4
MOVES = 7
INST = 8
NEW_DEV = 8
NQ = 128
RES = TABLE * PAGE + NEW_DEV
DEAD = 128.0
BIG = -1e30
BF = jnp.bfloat16
F32 = jnp.float32
F16 = jnp.float16
LOG_SCALE = math.log2(math.e) / math.sqrt(D)
HALF = MOST * PAGE
REST = RES - HALF
MIG_ROWS = INST * KVH * MOST * PAGE
OLD_ROWS = (TABLE - MOST) * PAGE * KVH
ROWS = MIG_ROWS + OLD_ROWS + 128
CHUNK = 256

SMEM = pl.BlockSpec(memory_space=pltpu.SMEM)
HBM = pl.BlockSpec(memory_space=pltpu.HBM)
VMEM = pl.BlockSpec(memory_space=pltpu.VMEM)


def here():
    return (
        lax.axis_index("x").astype(jnp.int32),
        lax.axis_index("y").astype(jnp.int32),
        lax.axis_index("ba").astype(jnp.int32),
    )


def pack_kernel(
    table_in, ctx_in, page_in, dest_in, source, new, mig, r0, r1, r2, r3, table, ctx, page, dest,
    pool, dead, sem_s, sem_p, sem_m, sem_r
):
    fetch = pltpu.make_async_copy(source, pool, sem_p)
    fetch.start()
    scalars = [
        pltpu.make_async_copy(a, b, sem_s.at[i])
        for i, (a, b) in enumerate(
            ((table_in, table), (ctx_in, ctx), (page_in, page), (dest_in, dest))
        )
    ]
    for copy in scalars:
        copy.start()
    dead[...] = jnp.full_like(dead, DEAD)
    _, y_here, b_here = here()
    for copy in scalars:
        copy.wait()
    for d in range(INST):
        count = jnp.int32(0)
        for m in range(MOVES):
            count += (dest[0, m] == d).astype(jnp.int32)
        for s in range(MOST):

            @pl.when((count <= s) & (b_here != d))
            def _():
                pltpu.make_async_copy(dead, mig.at[d, :, s], sem_m).start()

    fetch.wait()
    for m in range(MOVES):
        rank = jnp.int32(0)
        for e in range(m):
            rank += (dest[0, e] == dest[0, m]).astype(jnp.int32)
        for y in range(KVH):
            pltpu.make_async_copy(
                pool.at[page[0, m], :, :, pl.ds(y * D, D)], mig.at[dest[0, m], y, rank], sem_m
            ).start()
    index = lax.broadcasted_iota(jnp.int32, (PAGE, 2, KVH * D), 0)
    for j in range(TABLE):
        page_j = table[0, j]

        @pl.when(ctx[0, 0] < (j + 1) * PAGE)
        def _():
            rows = pool[page_j].astype(F32)
            alive = index < ctx[0, 0] - j * PAGE
            pool[page_j] = jnp.where(alive, rows, DEAD).astype(BF)

    outs = (r0, r1, r2, r3)
    for k in range(4):
        lanes = pl.ds(pl.multiple_of(lax.rem(y_here + k, 4) * D, D), D)
        for j in range(MOST, TABLE):
            pltpu.make_async_copy(
                pool.at[table[0, j], :, :, lanes],
                outs[k].at[pl.ds((j - MOST) * PAGE, PAGE)],
                sem_r.at[k],
            ).start()
        pltpu.make_async_copy(
            new.at[:, :, lanes], outs[k].at[pl.ds((TABLE - MOST) * PAGE, NEW_DEV)], sem_r.at[k]
        ).start()
    for j in range(MOST):
        for y in range(KVH):
            pltpu.make_async_copy(
                pool.at[table[0, j], :, :, pl.ds(y * D, D)], mig.at[b_here, y, j], sem_m
            ).start()
    for k in range(4):
        pltpu.make_async_copy(outs[k], outs[k], sem_r.at[k]).wait()
    pltpu.make_async_copy(mig, mig, sem_m).wait()


def pack(table, ctx, page, dest, pool, new):
    return pl.pallas_call(
        pack_kernel,
        in_specs=[HBM] * 5 + [VMEM],
        out_specs=[HBM] * 5,
        out_shape=[jax.ShapeDtypeStruct((INST, KVH, MOST, PAGE, 2, D), BF)]
        + [jax.ShapeDtypeStruct((REST, 2, D), BF)] * 4,
        scratch_shapes=[pltpu.SMEM(a.shape, jnp.int32) for a in (table, ctx, page, dest)]
        + [
            pltpu.VMEM(pool.shape, BF),
            pltpu.VMEM((KVH, PAGE, 2, D), BF),
            pltpu.SemaphoreType.DMA((4,)),
            pltpu.SemaphoreType.DMA,
            pltpu.SemaphoreType.DMA,
            pltpu.SemaphoreType.DMA((4,)),
        ],
        compiler_params=pltpu.CompilerParams(vmem_limit_bytes=60 << 20),
        name="pack",
    )(table, ctx, page, dest, pool, new)


def append_kernel(page_in, after, source, new, target, page, pool, sem):
    copy = pltpu.make_async_copy(source, pool, sem.at[0])
    copy.start()
    scalar = pltpu.make_async_copy(page_in, page, sem.at[1])
    scalar.start()
    scalar.wait()
    copy.wait()
    last = pltpu.make_async_copy(new, pool.at[page[0, 0], pl.ds(0, NEW_DEV)], sem.at[1])
    last.start()
    last.wait()
    copy = pltpu.make_async_copy(pool, target, sem.at[0])
    copy.start()
    copy.wait()


def append(page, after, pool, new):
    return pl.pallas_call(
        append_kernel,
        in_specs=[HBM] * 4,
        out_specs=HBM,
        out_shape=jax.ShapeDtypeStruct(pool.shape, BF),
        scratch_shapes=[
            pltpu.SMEM((1, 1), jnp.int32),
            pltpu.VMEM(pool.shape, BF),
            pltpu.SemaphoreType.DMA((2,)),
        ],
        compiler_params=pltpu.CompilerParams(vmem_limit_bytes=8 << 20),
        name="append",
    )(page, after, pool, new)


def pickers():
    row = lax.broadcasted_iota(jnp.int32, (256, 128), 0)
    col = lax.broadcasted_iota(jnp.int32, (256, 128), 1)
    keys = (row == 2 * col).astype(BF)
    row = lax.broadcasted_iota(jnp.int32, (128, 256), 0)
    col = lax.broadcasted_iota(jnp.int32, (128, 256), 1)
    return keys, (col == 2 * row + 1).astype(BF)


def put(x, pick, kt, vv, at):
    keys = lax.dot_general(x, pick[0], (((0,), (0,)), ((), ())), preferred_element_type=F32)
    kt[0:128, at] = keys.astype(BF)
    sub = lax.broadcasted_iota(jnp.int32, (128, 128), 0)
    kt[128:256, at] = jnp.where((sub == 0) & (keys > 64.0), BIG, 0.0).astype(BF)
    vals = jnp.dot(pick[1], x, preferred_element_type=F32)
    vv[at, 0:128] = vals.astype(BF)
    vv[at, 128:256] = jnp.ones((128, 128), BF)


def fill(mig, parts, kt, vv, aug):
    x_here, y_here, _ = here()
    pick = pickers()
    for i in range(MIG_ROWS // 128):
        put(mig[i], pick, kt, vv, slice(i * 128, i * 128 + 128))
    for i in range(2):
        x = jnp.concatenate([parts[2 * i][0:128], parts[2 * i + 1][0:128]], axis=0)
        at = MIG_ROWS + i * 128
        put(x, pick, kt, vv, slice(at, at + 128))
    at = MIG_ROWS + OLD_ROWS
    fresh = [r[128:144] for r in parts] + [jnp.zeros((192, 128), BF)]
    put(jnp.concatenate(fresh, axis=0), pick, kt, vv, slice(at, at + 128))
    sub = lax.broadcasted_iota(jnp.int32, (128, 128), 0)
    lane = lax.broadcasted_iota(jnp.int32, (128, 128), 1)
    hot = jnp.where((sub == 1 + lane) & (lane < 32), 1.0, 0.0)
    kt[128:256, at : at + 128] = jnp.where((sub == 0) & (lane >= 32), BIG, hot).astype(BF)
    j = lane - 1
    source = (y_here + 4 - (j >> 3)) & 3
    pos = source * 32 + x_here * 8 + (j & 7)
    bar = jnp.where((lane >= 1) & (lane < 33) & (pos > sub), BIG, 0.0)
    aug[...] = jnp.where(lane == 0, 1.0, bar).astype(BF)


def rows_of(qs, outs, kt, vv, aug, s_ref):
    per = CHUNK // 128
    units = [(i, c) for i in range(len(qs)) for c in range(512 // CHUNK)]
    lane = lax.broadcasted_iota(jnp.int32, (128, 128), 1)
    stats = [jnp.zeros((128, 128), F32) for _ in qs]

    def score(u):
        i, c = units[u]
        q = [
            jnp.concatenate([qs[i][:, (c * per + h) * 128 : (c * per + h + 1) * 128], aug[...]], 1)
            for h in range(per)
        ]
        s_ref[u % 2] = jnp.dot(jnp.concatenate(q, 0), kt[...], preferred_element_type=F32)

    score(0)
    for u, (i, c) in enumerate(units):
        if u + 1 < len(units):
            score(u + 1)
        s = s_ref[u % 2]
        top = jnp.max(s, axis=1, keepdims=True)
        p = jnp.exp2((s - top) * LOG_SCALE)
        high = p.astype(BF)
        low = (p - high.astype(F32)).astype(BF)
        o = jnp.dot(high, vv[...], preferred_element_type=F32)
        o += jnp.dot(low, vv[...], preferred_element_type=F32)
        total = o[:, 128:]
        mean = o[:, :128] / total
        most = jnp.maximum(jnp.max(jnp.abs(mean), axis=1, keepdims=True), 1e-30)
        mean = mean / most
        lse = jnp.log2(total) + top * LOG_SCALE
        num = lse + jnp.log2(most)
        for h in range(per):
            part = slice(h * 128, h * 128 + 128)
            at = c * per + h
            outs[i][0:128, at * 128 : at * 128 + 128] = mean[part]
            stats[i] = jnp.where(lane == at, lse[part], stats[i])
            stats[i] = jnp.where(lane == 4 + at, num[part], stats[i])
    for i, out in enumerate(outs):
        rows = stats[i].T[0:8]
        high = jnp.floor(rows * 2.0 + 0.5) * 0.5
        out[128:136, 0:128] = high
        out[128:136, 128:256] = rows - high
        out[128:136, 256:512] = jnp.zeros((8, 256), F32)


def first_kernel(q, mig, r0, r1, r2, r3, out, kt, vv, aug, s_ref):
    fill(mig, (r0, r1, r2, r3), kt, vv, aug)
    rows_of((q,), (out,), kt, vv, aug, s_ref)


def more_kernel(*refs):
    *pairs, kt, vv, aug = refs[: len(refs) // 2 + 1]
    outs = refs[len(refs) // 2 + 1 : -1]
    rows_of(pairs, outs, kt, vv, aug, refs[-1])


def cost(count):
    return pl.CostEstimate(
        flops=3 * 2 * 512 * ROWS * 256 * count,
        transcendentals=512 * ROWS * count,
        bytes_accessed=(2 << 20) * count,
    )


PART = jax.ShapeDtypeStruct((136, 512), F32)
SCORES = pltpu.VMEM((2, CHUNK, ROWS), F32)


def first(q, mig, parts):
    return pl.pallas_call(
        first_kernel,
        in_specs=[VMEM] * 6,
        out_specs=[VMEM] * 4,
        out_shape=[
            PART,
            jax.ShapeDtypeStruct((256, ROWS), BF),
            jax.ShapeDtypeStruct((ROWS, 256), BF),
            jax.ShapeDtypeStruct((128, 128), BF),
        ],
        scratch_shapes=[SCORES],
        compiler_params=pltpu.CompilerParams(vmem_limit_bytes=28 << 20),
        cost_estimate=cost(1),
        name="first",
    )(q, mig, *parts)


def more(qs, kt, vv, aug):
    return pl.pallas_call(
        more_kernel,
        in_specs=[VMEM] * (len(qs) + 3),
        out_specs=[VMEM] * len(qs),
        out_shape=[PART] * len(qs),
        scratch_shapes=[SCORES],
        compiler_params=pltpu.CompilerParams(vmem_limit_bytes=28 << 20),
        cost_estimate=cost(len(qs)),
        name="more",
    )(*qs, kt, vv, aug)


def combine_kernel(g0, g1, g2, g3, out):
    parts = (g0, g1, g2, g3)
    stats = [g[128:136, 0:128] + g[128:136, 128:256] for g in parts]
    cols = jnp.concatenate(stats + [jnp.zeros((96, 128), F32)], axis=0).T
    for h in range(4):
        dens = [cols[:, 8 * k + h : 8 * k + h + 1] for k in range(4)]
        nums = [cols[:, 8 * k + 4 + h : 8 * k + 5 + h] for k in range(4)]
        top = functools.reduce(jnp.maximum, dens)
        total = sum(jnp.exp2(x - top) for x in dens)
        lanes = slice(h * 128, h * 128 + 128)
        result = sum(g[0:128, lanes] * (jnp.exp2(n - top) / total) for g, n in zip(parts, nums))
        out[:, lanes] = result.astype(BF)


def combine(parts):
    return pl.pallas_call(
        combine_kernel,
        in_specs=[VMEM] * 4,
        out_specs=VMEM,
        out_shape=jax.ShapeDtypeStruct((128, 512), BF),
        compiler_params=pltpu.CompilerParams(vmem_limit_bytes=8 << 20),
        name="combine",
    )(*parts)


def shift(value, axis, k):
    return lax.ppermute(value, axis, [(i, (i + k) % 4) for i in range(4)])


def back(out, k):
    return shift(out.astype(F16), "x", -k).astype(F32)


def local(queries, new_kv, pool, page_table, ctx_len, move_page, move_dest, append_page):
    fresh = new_kv[0]
    q = queries[0]
    mig, *parts = pack(page_table, ctx_len, move_page, move_dest, pool[0], fresh)
    mig = mig.reshape(INST * KVH, MOST * PAGE * 2, D)
    mig = lax.all_to_all(mig, ("ba", "y"), 0, 0, tiled=True)
    parts = [r.reshape(REST * 2, D) for r in parts]
    parts = [parts[0]] + [shift(parts[k], "y", k) for k in range(1, 4)]
    qs = [q] + [shift(q, "x", k) for k in range(1, 4)]
    out2, *shared = first(qs[2], mig.reshape(MIG_ROWS // 128, 256, D), parts)
    got2 = back(out2, 2)
    out1, out3 = more((qs[1], qs[3]), *shared)
    got1, got3 = back(out1, 1), back(out3, 3)
    (out0,) = more((q,), *shared)
    updated = append(append_page, out3, pool[0], fresh)
    return combine([out0, got1, got2, got3])[None], updated[None]


def solution(mesh):
    grid = Mesh(np.asarray(mesh.devices).reshape(4, 4, 8), ("y", "x", "ba"))
    aa = ("y", "x")
    return jax.shard_map(
        local,
        mesh=grid,
        in_specs=(
            P("ba", None, aa),
            P("ba", aa, None, None),
            P("ba", aa, None, None, None),
            P("ba", aa),
            P("ba", aa),
            P("ba", aa),
            P("ba", aa),
            P("ba", aa),
        ),
        out_specs=(P("ba", None, aa), P("ba", aa, None, None, None)),
        check_vma=False,
    )
```

time: 76 us -> 53.2 us (0.70)
  blocking collectives: 11.2 us -> 0 us
  starting transfers between devices: 17.4 us -> 25.3 us
  local copies, waits for them, and re-layouts: 7.59 us -> 0.03 us
  waiting for transfers between devices: 13.4 us -> 7.93 us
  Pallas kernels: 21 us -> 17.3 us
  other arithmetic: 2.74 us -> 0.14 us
    all_to_all x1 -> x0, blocking collectives: 11.2 us -> none  [local(): res = lax.all_to_all(res.reshape(KVH, RES * 2, D), 'y', 0, 0, tiled=True)]
    ppermute x6 -> x9, starting transfers between devices: 11 us -> 16.6 us  [shift(): return lax.ppermute(value, axis, [(i, (i + k) % 4) for i in range(4)])]
    all_to_all x1, waiting for transfers between devices: 4.5 us -> 0.01 us  [local(): mig = lax.all_to_all(mig, ('ba', 'y'), 0, 0, tiled=True)]
    pallas_call x2 -> x6, Pallas kernels: 21 us -> 17.3 us  [the longest x2 7.93 us: more(): pl.pallas_call(more_kernel, in_specs=[VMEM] * (len(qs) + 3), out_specs=[V...]
    unnamed x23 -> x14, local copies, waits for them, and re-layouts: 2.83 us -> 0.03 us
    all_to_all x1, starting transfers between devices: 6.44 us -> 8.67 us  [local(): mig = lax.all_to_all(mig, ('ba', 'y'), 0, 0, tiled=True)]
    squeeze x7 -> x0, local copies, waits for them, and re-layouts: 1.57 us -> none  [local(): stats = jnp.concatenate([num[k, :, :4], den[k, :, :4]], axis=1)]
    slice x2 -> x0, local copies, waits for them, and re-layouts: 1.34 us -> none  [the longest x1 0.71 us: local(): old = res[:, :TABLE * PAGE * 2].reshape(RES_BLOCKS, 256, D)]
  transfers between devices with their start and end apart: 7 -> 10, of which waited for: 6 -> 2; matrix products, arithmetic and copies ran while one was open for 3% -> 0% of each run, Pallas kernels for 0% -> 15%
where the time goes in v2:
time: 53.2 us; the launch traced here: 52.8 us
  starting transfers between devices  25.3 us (48%)
  Pallas kernels  17.3 us (33%)
  waiting for transfers between devices  7.93 us (15%)
  between operations  2.1 us (4%)
    ppermute x9, starting transfers between devices, shift(): return lax.ppermute(value, axis, [(i, (i + k) % 4) for i in range(4)])  16.6 us
    all_to_all x1, starting transfers between devices, local(): mig = lax.all_to_all(mig, ('ba', 'y'), 0, 0, tiled=True)  8.67 us
    pallas_call x2, Pallas kernels, more(): pl.pallas_call(more_kernel, in_specs=[VMEM] * (len(qs) + 3), out_specs=[V...  7.93 us
    ppermute x9, waiting for transfers between devices, shift(): return lax.ppermute(value, axis, [(i, (i + k) % 4) for i in range(4)])  7.92 us
    pallas_call x1, Pallas kernels, first(): pl.pallas_call(first_kernel, in_specs=[VMEM] * 6, out_specs=[VMEM] * 4, o...  3.63 us
    pallas_call x1, Pallas kernels, pack(): pl.pallas_call(pack_kernel, in_specs=[HBM] * 5 + [VMEM], out_specs=[HBM]...  2.83 us
    pallas_call x1, Pallas kernels, append(): pl.pallas_call(append_kernel, in_specs=[HBM] * 4, out_specs=HBM, out_shap...  1.52 us
    pallas_call x1, Pallas kernels, combine(): pl.pallas_call(combine_kernel, in_specs=[VMEM] * 4, out_specs=VMEM, out_s...  1.44 us
  transfers between devices with their start and end apart: 10, of which 2 were waited for; matrix products, arithmetic and copies ran while one was open for 0% of the time, Pallas kernels for 15%

profile of v2, /device:TPU:0, one launch (start us, length us, event | category | flops | bytes accessed | tf_op | source)
XLA Modules:
  0.0 52.8 jit_solution(9524654508231938530)
XLA Ops:
  1.3 2.8 %pack.1 = (bf16[8,4,2,32,2,128]{5,4,3,2,1,0:T(2,128)(2,1)}, bf16[72,2,128]{2,1,0:T(2,128)(2,1)}, bf16[72,2,128]{2,1,0:T(2,128)(2,1)}, bf16[72,2,128]{2,1,0:T(2,128)(2,1)}, bf16[72,2,128]{2,1,0:T(2,128)(2,1)}) custom-call(s32[1,4]{1,0:T(1,128)} %table_in.1, s32[1,1]{1,0:T(1,128)S(6)} %copy.10.ctx_in, s32[1,7]{1,0:T(1,128)} %page_in.2, s32[1,7]{1,0:T(1,128)} %dest_in.1, ...), custom_call_target="tpu_custom_call" | custom-call | tf_op jit(solution)/shard_map/pack/pallas_call | solution.py:118
  4.1 0.0 copy-start.2
  4.1 0.0 copy-start.6
  4.2 0.0 copy-start.3
  4.2 8.7 %all-to-all-start = ((bf16[32,128,128]{2,1,0:T(8,128)(2,1)}), bf16[32,128,128]{2,1,0:T(8,128)(2,1)S(1)}, u32[]{:S(2)}, u32[]{:S(2)}) async-start(bf16[32,128,128]{2,1,0:T(8,128)(2,1)} %bitcast.21), calls=%async_computation | async-start | bytes 2097152 | tf_op jit(solution)/shard_map/all_to_all | solution.py:348
  12.9 3.0 %collective-permute-start = (bf16[128,512]{1,0:T(8,128)(2,1)S(1)}, bf16[128,512]{1,0:T(8,128)(2,1)S(1)}, u32[]{:S(2)}, u32[]{:S(2)}) collective-permute-start(bf16[128,512]{1,0:T(8,128)(2,1)S(1)} %bitcast.16), channel_id=1, source_target_pairs={{0,16},{8,24},{16,0},{24,8},{1,17},{9,25},{17,1},{25,9},{2,18},{10... | collective-permute-start | bytes 393224 | tf_op jit(solution)/shard_map/ppermute | solution.py:336
  15.8 1.8 %collective-permute-start.1 = (bf16[144,128]{1,0:T(8,128)(2,1)S(1)}, bf16[144,128]{1,0:T(8,128)(2,1)S(1)}, u32[]{:S(2)}, u32[]{:S(2)}) collective-permute-start(bf16[144,128]{1,0:T(8,128)(2,1)S(1)} %bitcast.26), channel_id=1, source_target_pairs={{0,32},{32,64},{64,96},{96,0},{1,33},{33,65},{65,97},{97,1},{2,34}... | collective-permute-start | bytes 110600 | tf_op jit(solution)/shard_map/ppermute | solution.py:336
  17.6 2.7 %collective-permute-start.2 = (bf16[144,128]{1,0:T(8,128)(2,1)S(1)}, bf16[144,128]{1,0:T(8,128)(2,1)S(1)}, u32[]{:S(2)}, u32[]{:S(2)}) collective-permute-start(bf16[144,128]{1,0:T(8,128)(2,1)S(1)} %bitcast.25), channel_id=1, source_target_pairs={{0,64},{32,96},{64,0},{96,32},{1,65},{33,97},{65,1},{97,33},{2,66}... | collective-permute-start | bytes 110600 | tf_op jit(solution)/shard_map/ppermute | solution.py:336
  20.3 1.5 %collective-permute-start.3 = (bf16[144,128]{1,0:T(8,128)(2,1)S(1)}, bf16[144,128]{1,0:T(8,128)(2,1)S(1)}, u32[]{:S(2)}, u32[]{:S(2)}) collective-permute-start(bf16[144,128]{1,0:T(8,128)(2,1)S(1)} %bitcast.24), channel_id=1, source_target_pairs={{0,96},{32,0},{64,32},{96,64},{1,97},{33,1},{65,33},{97,65},{2,98}... | collective-permute-start | bytes 110600 | tf_op jit(solution)/shard_map/ppermute | solution.py:336
  21.8 0.6 %collective-permute-start.4 = (bf16[128,512]{1,0:T(8,128)(2,1)S(1)}, bf16[128,512]{1,0:T(8,128)(2,1)S(1)}, u32[]{:S(2)}, u32[]{:S(2)}) collective-permute-start(bf16[128,512]{1,0:T(8,128)(2,1)S(1)} %bitcast.17), channel_id=1, source_target_pairs={{0,8},{8,16},{16,24},{24,0},{1,9},{9,17},{17,25},{25,1},{2,10},{10... | collective-permute-start | bytes 393224 | tf_op jit(solution)/shard_map/ppermute | solution.py:336
  23.1 6.1 %collective-permute-done.1.r1 = bf16[144,128]{1,0:T(8,128)(2,1)S(1)} collective-permute-done((bf16[144,128]{1,0:T(8,128)(2,1)S(1)}, bf16[144,128]{1,0:T(8,128)(2,1)S(1)}, u32[]{:S(2)}, u32[]{:S(2)}) %collective-permute-start.1) | collective-permute-done | bytes 36896 | tf_op jit(solution)/shard_map/ppermute | solution.py:336
  29.1 2.7 %collective-permute-start.5 = (bf16[128,512]{1,0:T(8,128)(2,1)S(1)}, bf16[128,512]{1,0:T(8,128)(2,1)S(1)}, u32[]{:S(2)}, u32[]{:S(2)}) collective-permute-start(bf16[128,512]{1,0:T(8,128)(2,1)S(1)} %bitcast.18), channel_id=1, source_target_pairs={{0,24},{8,0},{16,8},{24,16},{1,25},{9,1},{17,9},{25,17},{2,26},{10... | collective-permute-start | bytes 393224 | tf_op jit(solution)/shard_map/ppermute | solution.py:336
  31.8 0.0 collective-permute-done.2.r2
  31.8 0.0 collective-permute-done.3.r3
  31.9 0.0 all-to-all-done
  31.9 3.6 %first.1 = (f32[136,512]{1,0:T(8,128)S(1)}, bf16[256,2432]{1,0:T(8,128)(2,1)S(1)}, bf16[2432,256]{1,0:T(8,128)(2,1)S(1)}, bf16[128,128]{1,0:T(8,128)(2,1)S(1)}) custom-call(bf16[128,512]{1,0:T(8,128)(2,1)S(1)} %collective-permute-done.q, bf16[16,256,128]{2,1,0:T(8,128)(2,1)S(1)} %bitcast.13, bf16[144,128]{1,0:T(8,128)(2,1)S(1)} %bitcast.20, ...), custom_call_target="tpu_custom_call" | custom-call | flops 1912602624 | bytes 2097152 | tf_op jit(solution)/shard_map/first/pallas_call | solution.py:280
  35.5 5.1 %more.3 = (f32[136,512]{1,0:T(8,128)S(1)}, f32[136,512]{1,0:T(8,128)S(1)}) custom-call(bf16[128,512]{1,0:T(8,128)(2,1)S(1)} %collective-permute-done.4.refs_0_, bf16[128,512]{1,0:T(8,128)(2,1)S(1)} %collective-permute-done.5.refs_1_, bf16[256,2432]{1,0:T(8,128)(2,1)S(1)} %get-tuple-element.18.refs_1_.refs_2_, ...), custom_call_target="tpu_custom_call" | custom-call | flops 3825205248 | bytes 4194304 | tf_op jit(solution)/shard_map/more/pallas_call | solution.py:298
  40.7 2.6 %collective-permute-start.6 = (f16[136,512]{1,0:T(8,128)(2,1)S(1)}, f16[136,512]{1,0:T(8,128)(2,1)S(1)}, u32[]{:S(2)}, u32[]{:S(2)}) collective-permute-start(f16[136,512]{1,0:T(8,128)(2,1)S(1)} %convert_element_type.18), channel_id=1, source_target_pairs={{0,24},{8,0},{16,8},{24,16},{1,25},{9,1},{17,9},{25,17},{2,26},{10... | collective-permute-start | bytes 417800 | tf_op jit(solution)/shard_map/ppermute | solution.py:336
  43.3 0.3 collective-permute-start.8
  43.6 1.5 %collective-permute-start.7 = (f16[136,512]{1,0:T(8,128)(2,1)S(1)}, f16[136,512]{1,0:T(8,128)(2,1)S(1)}, u32[]{:S(2)}, u32[]{:S(2)}) collective-permute-start(f16[136,512]{1,0:T(8,128)(2,1)S(1)} %convert_element_type.20), channel_id=1, source_target_pairs={{0,16},{8,24},{16,0},{24,8},{1,17},{9,25},{17,1},{25,9},{2,18},{10... | collective-permute-start | bytes 417800 | tf_op jit(solution)/shard_map/ppermute | solution.py:336
  45.1 1.5 %append.1 = bf16[12,32,2,512]{3,2,1,0:T(2,128)(2,1)} custom-call(s32[1,1]{1,0:T(1,128)S(6)} %copy.11.page_in, f32[136,512]{1,0:T(8,128)S(1)} %get-tuple-element.23.after, bf16[12,32,2,512]{3,2,1,0:T(2,128)(2,1)S(1)} %bitcast.12, bf16[8,2,512]{2,1,0:T(2,128)(2,1)S(1)} %bitcast.15), custom_call_target="tpu_custom_call" | custom-call | tf_op jit(solution)/shard_map/append/pallas_call | solution.py:154
  46.6 2.8 %more.2.g0 = f32[136,512]{1,0:T(8,128)S(1)} custom-call(bf16[128,512]{1,0:T(8,128)(2,1)S(1)} %bitcast.19, bf16[256,2432]{1,0:T(8,128)(2,1)S(1)} %get-tuple-element.18.refs_1_.refs_2_, bf16[2432,256]{1,0:T(8,128)(2,1)S(1)} %get-tuple-element.19.refs_2_.refs_3_, bf16[128,128]{1,0:T(8,128)(2,1)S(1)} %get-tuple-element.20.refs_3_.refs_4_), custom_call_target="tpu_custom_call" | custom-call | flops 1912602624 | bytes 2097152 | tf_op jit(solution)/shard_map/more/pallas_call | solution.py:298
  49.5 1.8 %collective-permute-done.8 = f16[136,512]{1,0:T(8,128)(2,1)S(1)} collective-permute-done((f16[136,512]{1,0:T(8,128)(2,1)S(1)}, f16[136,512]{1,0:T(8,128)(2,1)S(1)}, u32[]{:S(2)}, u32[]{:S(2)}) %collective-permute-start.8) | collective-permute-done | bytes 139296 | tf_op jit(solution)/shard_map/ppermute | solution.py:336
  51.4 1.4 %combine.1 = bf16[128,512]{1,0:T(8,128)(2,1)} custom-call(f32[136,512]{1,0:T(8,128)S(1)} %more.2.g0, f32[136,512]{1,0:T(8,128)S(1)} %convert_element_type.19.g1, f32[136,512]{1,0:T(8,128)S(1)} %convert_element_type.21.g2, f32[136,512]{1,0:T(8,128)S(1)} %convert_element_type.23.g3), custom_call_target="tpu_custom_call" | custom-call | tf_op jit(solution)/shard_map/combine/pallas_call | solution.py:325
  (22 shorter events, 0.2 us)
Async XLA Ops:
  4.1 8.7 %copy-start.2 = (bf16[1,128,512]{2,1,0:T(8,128)(2,1)S(1)}, bf16[1,128,512]{2,1,0:T(8,128)(2,1)}, u32[]{:S(2)}) copy-start(bf16[1,128,512]{2,1,0:T(8,128)(2,1)} %param.8) | copy-start | bytes 393220
  4.1 11.7 %copy-start.6 = (bf16[72,2,128]{2,1,0:T(2,128)(2,1)S(1)}, bf16[72,2,128]{2,1,0:T(2,128)(2,1)}, u32[]{:S(2)}) copy-start(bf16[72,2,128]{2,1,0:T(2,128)(2,1)} %get-tuple-element.15) | copy-start | bytes 110596
  4.1 13.5 %copy-start.5 = (bf16[72,2,128]{2,1,0:T(2,128)(2,1)S(1)}, bf16[72,2,128]{2,1,0:T(2,128)(2,1)}, u32[]{:S(2)}) copy-start(bf16[72,2,128]{2,1,0:T(2,128)(2,1)} %get-tuple-element.16) | copy-start | bytes 110596
  4.1 16.2 %copy-start.4 = (bf16[72,2,128]{2,1,0:T(2,128)(2,1)S(1)}, bf16[72,2,128]{2,1,0:T(2,128)(2,1)}, u32[]{:S(2)}) copy-start(bf16[72,2,128]{2,1,0:T(2,128)(2,1)} %get-tuple-element.17) | copy-start | bytes 110596
  4.2 27.7 %copy-start.3 = (bf16[72,2,128]{2,1,0:T(2,128)(2,1)S(1)}, bf16[72,2,128]{2,1,0:T(2,128)(2,1)}, u32[]{:S(2)}) copy-start(bf16[72,2,128]{2,1,0:T(2,128)(2,1)} %get-tuple-element.14) | copy-start | bytes 110596
  4.2 27.7 %all-to-all-start = ((bf16[32,128,128]{2,1,0:T(8,128)(2,1)}), bf16[32,128,128]{2,1,0:T(8,128)(2,1)S(1)}, u32[]{:S(2)}, u32[]{:S(2)}) async-start(bf16[32,128,128]{2,1,0:T(8,128)(2,1)} %bitcast.21), calls=%async_computation | async-start | bytes 2097152 | tf_op jit(solution)/shard_map/all_to_all | solution.py:348
  12.9 19.0 %collective-permute-start = (bf16[128,512]{1,0:T(8,128)(2,1)S(1)}, bf16[128,512]{1,0:T(8,128)(2,1)S(1)}, u32[]{:S(2)}, u32[]{:S(2)}) collective-permute-start(bf16[128,512]{1,0:T(8,128)(2,1)S(1)} %bitcast.16), channel_id=1, source_target_pairs={{0,16},{8,24},{16,0},{24,8},{1,17},{9,25},{17,1},{25,9},{2,18},{10... | collective-permute-start | bytes 393224 | tf_op jit(solution)/shard_map/ppermute | solution.py:336
  15.8 13.3 %collective-permute-start.1 = (bf16[144,128]{1,0:T(8,128)(2,1)S(1)}, bf16[144,128]{1,0:T(8,128)(2,1)S(1)}, u32[]{:S(2)}, u32[]{:S(2)}) collective-permute-start(bf16[144,128]{1,0:T(8,128)(2,1)S(1)} %bitcast.26), channel_id=1, source_target_pairs={{0,32},{32,64},{64,96},{96,0},{1,33},{33,65},{65,97},{97,1},{2,34}... | collective-permute-start | bytes 110600 | tf_op jit(solution)/shard_map/ppermute | solution.py:336
  17.6 14.2 %collective-permute-start.2 = (bf16[144,128]{1,0:T(8,128)(2,1)S(1)}, bf16[144,128]{1,0:T(8,128)(2,1)S(1)}, u32[]{:S(2)}, u32[]{:S(2)}) collective-permute-start(bf16[144,128]{1,0:T(8,128)(2,1)S(1)} %bitcast.25), channel_id=1, source_target_pairs={{0,64},{32,96},{64,0},{96,32},{1,65},{33,97},{65,1},{97,33},{2,66}... | collective-permute-start | bytes 110600 | tf_op jit(solution)/shard_map/ppermute | solution.py:336
  20.3 11.5 %collective-permute-start.3 = (bf16[144,128]{1,0:T(8,128)(2,1)S(1)}, bf16[144,128]{1,0:T(8,128)(2,1)S(1)}, u32[]{:S(2)}, u32[]{:S(2)}) collective-permute-start(bf16[144,128]{1,0:T(8,128)(2,1)S(1)} %bitcast.24), channel_id=1, source_target_pairs={{0,96},{32,0},{64,32},{96,64},{1,97},{33,1},{65,33},{97,65},{2,98}... | collective-permute-start | bytes 110600 | tf_op jit(solution)/shard_map/ppermute | solution.py:336
  21.8 13.7 %collective-permute-start.4 = (bf16[128,512]{1,0:T(8,128)(2,1)S(1)}, bf16[128,512]{1,0:T(8,128)(2,1)S(1)}, u32[]{:S(2)}, u32[]{:S(2)}) collective-permute-start(bf16[128,512]{1,0:T(8,128)(2,1)S(1)} %bitcast.17), channel_id=1, source_target_pairs={{0,8},{8,16},{16,24},{24,0},{1,9},{9,17},{17,25},{25,1},{2,10},{10... | collective-permute-start | bytes 393224 | tf_op jit(solution)/shard_map/ppermute | solution.py:336
  29.1 6.4 %collective-permute-start.5 = (bf16[128,512]{1,0:T(8,128)(2,1)S(1)}, bf16[128,512]{1,0:T(8,128)(2,1)S(1)}, u32[]{:S(2)}, u32[]{:S(2)}) collective-permute-start(bf16[128,512]{1,0:T(8,128)(2,1)S(1)} %bitcast.18), channel_id=1, source_target_pairs={{0,24},{8,0},{16,8},{24,16},{1,25},{9,1},{17,9},{25,17},{2,26},{10... | collective-permute-start | bytes 393224 | tf_op jit(solution)/shard_map/ppermute | solution.py:336
  40.6 4.5 %copy-start = (bf16[1,12,32,2,512]{4,3,2,1,0:T(2,128)(2,1)S(1)}, bf16[1,12,32,2,512]{4,3,2,1,0:T(2,128)(2,1)}, u32[]{:S(2)}) copy-start(bf16[1,12,32,2,512]{4,3,2,1,0:T(2,128)(2,1)} %param.10) | copy-start | bytes 2359300
  40.6 4.5 %copy-start.1 = (bf16[1,8,2,512]{3,2,1,0:T(2,128)(2,1)S(1)}, bf16[1,8,2,512]{3,2,1,0:T(2,128)(2,1)}, u32[]{:S(2)}) copy-start(bf16[1,8,2,512]{3,2,1,0:T(2,128)(2,1)} %param.9) | copy-start | bytes 49156
  40.7 8.8 %collective-permute-start.6 = (f16[136,512]{1,0:T(8,128)(2,1)S(1)}, f16[136,512]{1,0:T(8,128)(2,1)S(1)}, u32[]{:S(2)}, u32[]{:S(2)}) collective-permute-start(f16[136,512]{1,0:T(8,128)(2,1)S(1)} %convert_element_type.18), channel_id=1, source_target_pairs={{0,24},{8,0},{16,8},{24,16},{1,25},{9,1},{17,9},{25,17},{2,26},{10... | collective-permute-start | bytes 417800 | tf_op jit(solution)/shard_map/ppermute | solution.py:336
  43.3 8.1 %collective-permute-start.8 = (f16[136,512]{1,0:T(8,128)(2,1)S(1)}, f16[136,512]{1,0:T(8,128)(2,1)S(1)}, u32[]{:S(2)}, u32[]{:S(2)}) collective-permute-start(f16[136,512]{1,0:T(8,128)(2,1)S(1)} %convert_element_type.22), channel_id=1, source_target_pairs={{0,8},{8,16},{16,24},{24,0},{1,9},{9,17},{17,25},{25,1},{2,10},{10... | collective-permute-start | bytes 417800 | tf_op jit(solution)/shard_map/ppermute | solution.py:336
  43.6 7.8 %collective-permute-start.7 = (f16[136,512]{1,0:T(8,128)(2,1)S(1)}, f16[136,512]{1,0:T(8,128)(2,1)S(1)}, u32[]{:S(2)}, u32[]{:S(2)}) collective-permute-start(f16[136,512]{1,0:T(8,128)(2,1)S(1)} %convert_element_type.20), channel_id=1, source_target_pairs={{0,16},{8,24},{16,0},{24,8},{1,17},{9,25},{17,1},{25,9},{2,18},{10... | collective-permute-start | bytes 417800 | tf_op jit(solution)/shard_map/ppermute | solution.py:336

commit v3 on v2

--- a/solution.py
+++ b/solution.py
@@ -117,7 +117,7 @@
 def pack(table, ctx, page, dest, pool, new):
     return pl.pallas_call(
         pack_kernel,
-        in_specs=[HBM] * 5 + [VMEM],
+        in_specs=[HBM, VMEM, HBM, HBM, HBM, VMEM],
         out_specs=[HBM] * 5,
         out_shape=[jax.ShapeDtypeStruct((INST, KVH, MOST, PAGE, 2, D), BF)]
         + [jax.ShapeDtypeStruct((REST, 2, D), BF)] * 4,
@@ -162,6 +162,7 @@
             pltpu.SemaphoreType.DMA((2,)),
         ],
         compiler_params=pltpu.CompilerParams(vmem_limit_bytes=8 << 20),
+        cost_estimate=cost(1),
         name="append",
     )(page, after, pool, new)
 
@@ -258,17 +259,14 @@
     rows_of((q,), (out,), kt, vv, aug, s_ref)
 
 
-def more_kernel(*refs):
-    *pairs, kt, vv, aug = refs[: len(refs) // 2 + 1]
-    outs = refs[len(refs) // 2 + 1 : -1]
-    rows_of(pairs, outs, kt, vv, aug, refs[-1])
+def more_kernel(count, *refs):
+    *qs, kt, vv, aug = refs[: count + 3]
+    rows_of(qs, refs[-1 - count : -1], kt, vv, aug, refs[-1])
 
 
 def cost(count):
     return pl.CostEstimate(
-        flops=3 * 2 * 512 * ROWS * 256 * count,
-        transcendentals=512 * ROWS * count,
-        bytes_accessed=(2 << 20) * count,
+        flops=count << 20, transcendentals=count << 10, bytes_accessed=count << 16
     )
 
 
@@ -294,37 +292,40 @@
     )(q, mig, *parts)
 
 
-def more(qs, kt, vv, aug):
-    return pl.pallas_call(
-        more_kernel,
-        in_specs=[VMEM] * (len(qs) + 3),
+def more(qs, kt, vv, aug, after=None):
+    late = () if after is None else (after,)
+    return pl.pallas_call(
+        functools.partial(more_kernel, len(qs)),
+        in_specs=[VMEM] * (len(qs) + 3) + [HBM] * len(late),
         out_specs=[VMEM] * len(qs),
         out_shape=[PART] * len(qs),
         scratch_shapes=[SCORES],
         compiler_params=pltpu.CompilerParams(vmem_limit_bytes=28 << 20),
         cost_estimate=cost(len(qs)),
         name="more",
-    )(*qs, kt, vv, aug)
-
-
-def combine_kernel(g0, g1, g2, g3, out):
-    parts = (g0, g1, g2, g3)
+    )(*qs, kt, vv, aug, *late)
+
+
+def combine_kernel(g0, g2, g, out):
+    parts = (g0, g2, g.at[0], g.at[1])
     stats = [g[128:136, 0:128] + g[128:136, 128:256] for g in parts]
-    cols = jnp.concatenate(stats + [jnp.zeros((96, 128), F32)], axis=0).T
+    dens = [x[0:4] for x in stats]
+    top = functools.reduce(jnp.maximum, dens)
+    share = 1.0 / sum(jnp.exp2(x - top) for x in dens)
+    rows = [jnp.exp2(x[4:8] - top) * share for x in stats]
+    cols = jnp.concatenate(rows + [jnp.zeros((112, 128), F32)], axis=0).T
     for h in range(4):
-        dens = [cols[:, 8 * k + h : 8 * k + h + 1] for k in range(4)]
-        nums = [cols[:, 8 * k + 4 + h : 8 * k + 5 + h] for k in range(4)]
-        top = functools.reduce(jnp.maximum, dens)
-        total = sum(jnp.exp2(x - top) for x in dens)
         lanes = slice(h * 128, h * 128 + 128)
-        result = sum(g[0:128, lanes] * (jnp.exp2(n - top) / total) for g, n in zip(parts, nums))
+        result = sum(
+            g[0:128, lanes] * cols[:, 4 * k + h : 4 * k + h + 1] for k, g in enumerate(parts)
+        )
         out[:, lanes] = result.astype(BF)
 
 
-def combine(parts):
+def combine(*parts):
     return pl.pallas_call(
         combine_kernel,
-        in_specs=[VMEM] * 4,
+        in_specs=[VMEM] * 3,
         out_specs=VMEM,
         out_shape=jax.ShapeDtypeStruct((128, 512), BF),
         compiler_params=pltpu.CompilerParams(vmem_limit_bytes=8 << 20),
@@ -336,8 +337,8 @@
     return lax.ppermute(value, axis, [(i, (i + k) % 4) for i in range(4)])
 
 
-def back(out, k):
-    return shift(out.astype(F16), "x", -k).astype(F32)
+def swap(value, k):
+    return lax.ppermute(value, "x", [(i, i ^ k) for i in range(4)])
 
 
 def local(queries, new_kv, pool, page_table, ctx_len, move_page, move_dest, append_page):
@@ -348,14 +349,17 @@
     mig = lax.all_to_all(mig, ("ba", "y"), 0, 0, tiled=True)
     parts = [r.reshape(REST * 2, D) for r in parts]
     parts = [parts[0]] + [shift(parts[k], "y", k) for k in range(1, 4)]
-    qs = [q] + [shift(q, "x", k) for k in range(1, 4)]
+    q2 = swap(q, 2)
+    pair = swap(jnp.concatenate([q, q2], axis=0), 1)
+    qs = [q, pair[:128], q2, pair[128:]]
     out2, *shared = first(qs[2], mig.reshape(MIG_ROWS // 128, 256, D), parts)
-    got2 = back(out2, 2)
+    got2 = swap(out2.astype(F16), 2).astype(F32)
     out1, out3 = more((qs[1], qs[3]), *shared)
-    got1, got3 = back(out1, 1), back(out3, 3)
-    (out0,) = more((q,), *shared)
+    sent = [swap(out.astype(F16), k) for k, out in ((1, out1), (3, out3))]
+    got = jnp.stack(sent).astype(F32)
+    (out0,) = more((q,), *shared, after=got2)
     updated = append(append_page, out3, pool[0], fresh)
-    return combine([out0, got1, got2, got3])[None], updated[None]
+    return combine(out0, got2, got)[None], updated[None]
 
 
 def solution(mesh):

time: 53.2 us -> 50.5 us (0.949)
  starting transfers between devices: 25.3 us -> 23.4 us
  waiting for transfers between devices: 7.93 us -> 6.91 us
    ppermute x9 -> x3, starting transfers between devices: 16.6 us -> 5.8 us  [shift(): return lax.ppermute(value, axis, [(i, (i + k) % 4) for i in range(4)])]
    ppermute x0 -> x5, starting transfers between devices: none -> 8.93 us  [swap(): return lax.ppermute(value, 'x', [(i, i ^ k) for i in range(4)])]
    ppermute x9 -> x3, waiting for transfers between devices: 7.92 us -> 2.14 us  [shift(): return lax.ppermute(value, axis, [(i, (i + k) % 4) for i in range(4)])]
    ppermute x0 -> x5, waiting for transfers between devices: none -> 4.77 us  [swap(): return lax.ppermute(value, 'x', [(i, i ^ k) for i in range(4)])]
  transfers between devices with their start and end apart: 10 -> 9, of which waited for: 2 -> 4; matrix products, arithmetic and copies ran while one was open for 0% -> 0% of each run, Pallas kernels for 15% -> 19%
where the time goes in v3:
time: 50.5 us; the launch traced here: 49.7 us
  starting transfers between devices  23.4 us (46%)
  Pallas kernels  17.1 us (34%)
  waiting for transfers between devices  6.91 us (14%)
  between operations  2.09 us (4%)
    ppermute x5, starting transfers between devices, swap(): return lax.ppermute(value, 'x', [(i, i ^ k) for i in range(4)])  8.93 us
    all_to_all x1, starting transfers between devices, local(): mig = lax.all_to_all(mig, ('ba', 'y'), 0, 0, tiled=True)  8.67 us
    pallas_call x2, Pallas kernels, more(): pl.pallas_call(functools.partial(more_kernel, len(qs)), in_specs=[VMEM] *...  7.96 us
    ppermute x3, starting transfers between devices, shift(): return lax.ppermute(value, axis, [(i, (i + k) % 4) for i in range(4)])  5.8 us
    ppermute x5, waiting for transfers between devices, swap(): return lax.ppermute(value, 'x', [(i, i ^ k) for i in range(4)])  4.77 us
    pallas_call x1, Pallas kernels, first(): pl.pallas_call(first_kernel, in_specs=[VMEM] * 6, out_specs=[VMEM] * 4, o...  3.63 us
    pallas_call x1, Pallas kernels, pack(): pl.pallas_call(pack_kernel, in_specs=[HBM, VMEM, HBM, HBM, HBM, VMEM], ou...  2.83 us
    ppermute x3, waiting for transfers between devices, shift(): return lax.ppermute(value, axis, [(i, (i + k) % 4) for i in range(4)])  2.14 us
  transfers between devices with their start and end apart: 9, of which 4 were waited for; matrix products, arithmetic and copies ran while one was open for 0% of the time, Pallas kernels for 19%

profile of v3, /device:TPU:0, one launch (start us, length us, event | category | flops | bytes accessed | tf_op | source)
XLA Modules:
  0.0 49.7 jit_solution(15983314284859040596)
XLA Ops:
  1.3 2.8 %pack.1 = (bf16[8,4,2,32,2,128]{5,4,3,2,1,0:T(2,128)(2,1)}, bf16[72,2,128]{2,1,0:T(2,128)(2,1)}, bf16[72,2,128]{2,1,0:T(2,128)(2,1)}, bf16[72,2,128]{2,1,0:T(2,128)(2,1)}, bf16[72,2,128]{2,1,0:T(2,128)(2,1)}) custom-call(s32[1,4]{1,0:T(1,128)} %table_in.1, s32[1,1]{1,0:T(1,128)S(6)} %copy.10.ctx_in, s32[1,7]{1,0:T(1,128)} %page_in.2, s32[1,7]{1,0:T(1,128)} %dest_in.1, ...), custom_call_target="tpu_custom_call" | custom-call | tf_op jit(solution)/shard_map/pack/pallas_call | solution.py:118
  4.1 0.0 copy-start.1
  4.1 0.0 copy-start.6
  4.2 0.0 copy-start.3
  4.2 8.7 %all-to-all-start = ((bf16[32,128,128]{2,1,0:T(8,128)(2,1)}), bf16[32,128,128]{2,1,0:T(8,128)(2,1)S(1)}, u32[]{:S(2)}, u32[]{:S(2)}) async-start(bf16[32,128,128]{2,1,0:T(8,128)(2,1)} %bitcast.22), calls=%async_computation | async-start | bytes 2097152 | tf_op jit(solution)/shard_map/all_to_all | solution.py:349
  12.9 3.0 %collective-permute-start = (bf16[128,512]{1,0:T(8,128)(2,1)S(1)}, bf16[128,512]{1,0:T(8,128)(2,1)S(1)}, u32[]{:S(2)}, u32[]{:S(2)}) collective-permute-start(bf16[128,512]{1,0:T(8,128)(2,1)S(1)} %bitcast.16), channel_id=1, source_target_pairs={{0,16},{8,24},{16,0},{24,8},{1,17},{9,25},{17,1},{25,9},{2,18},{10... | collective-permute-start | bytes 393224 | tf_op jit(solution)/shard_map/ppermute | solution.py:341
  15.8 4.3 %collective-permute-done.q = bf16[128,512]{1,0:T(8,128)(2,1)S(1)} collective-permute-done((bf16[128,512]{1,0:T(8,128)(2,1)S(1)}, bf16[128,512]{1,0:T(8,128)(2,1)S(1)}, u32[]{:S(2)}, u32[]{:S(2)}) %collective-permute-start) | collective-permute-done | bytes 131104 | tf_op jit(solution)/shard_map/ppermute | solution.py:341
  20.1 1.5 %collective-permute-start.5 = (bf16[256,512]{1,0:T(8,128)(2,1)S(1)}, bf16[256,512]{1,0:T(8,128)(2,1)S(1)}, u32[]{:S(2)}, u32[]{:S(2)}) collective-permute-start(bf16[256,512]{1,0:T(8,128)(2,1)S(1)} %pad_maximum_fusion), channel_id=1, source_target_pairs={{0,8},{8,0},{16,24},{24,16},{1,9},{9,1},{17,25},{25,17},{2,10},{10... | collective-permute-start | bytes 786440 | tf_op jit(solution)/shard_map/ppermute | solution.py:341
  21.6 1.7 %collective-permute-start.1 = (bf16[144,128]{1,0:T(8,128)(2,1)S(1)}, bf16[144,128]{1,0:T(8,128)(2,1)S(1)}, u32[]{:S(2)}, u32[]{:S(2)}) collective-permute-start(bf16[144,128]{1,0:T(8,128)(2,1)S(1)} %bitcast.29), channel_id=1, source_target_pairs={{0,32},{32,64},{64,96},{96,0},{1,33},{33,65},{65,97},{97,1},{2,34}... | collective-permute-start | bytes 110600 | tf_op jit(solution)/shard_map/ppermute | solution.py:337
  23.3 2.7 %collective-permute-start.2 = (bf16[144,128]{1,0:T(8,128)(2,1)S(1)}, bf16[144,128]{1,0:T(8,128)(2,1)S(1)}, u32[]{:S(2)}, u32[]{:S(2)}) collective-permute-start(bf16[144,128]{1,0:T(8,128)(2,1)S(1)} %bitcast.28), channel_id=1, source_target_pairs={{0,64},{32,96},{64,0},{96,32},{1,65},{33,97},{65,1},{97,33},{2,66}... | collective-permute-start | bytes 110600 | tf_op jit(solution)/shard_map/ppermute | solution.py:337
  25.9 1.5 %collective-permute-start.3 = (bf16[144,128]{1,0:T(8,128)(2,1)S(1)}, bf16[144,128]{1,0:T(8,128)(2,1)S(1)}, u32[]{:S(2)}, u32[]{:S(2)}) collective-permute-start(bf16[144,128]{1,0:T(8,128)(2,1)S(1)} %bitcast.27), channel_id=1, source_target_pairs={{0,96},{32,0},{64,32},{96,64},{1,97},{33,1},{65,33},{97,65},{2,98}... | collective-permute-start | bytes 110600 | tf_op jit(solution)/shard_map/ppermute | solution.py:337
  27.4 0.5 collective-permute-done.5
  27.9 1.2 %collective-permute-done.1.r1 = bf16[144,128]{1,0:T(8,128)(2,1)S(1)} collective-permute-done((bf16[144,128]{1,0:T(8,128)(2,1)S(1)}, bf16[144,128]{1,0:T(8,128)(2,1)S(1)}, u32[]{:S(2)}, u32[]{:S(2)}) %collective-permute-start.1) | collective-permute-done | bytes 36896 | tf_op jit(solution)/shard_map/ppermute | solution.py:337
  29.1 0.9 %collective-permute-done.2.r2 = bf16[144,128]{1,0:T(8,128)(2,1)S(1)} collective-permute-done((bf16[144,128]{1,0:T(8,128)(2,1)S(1)}, bf16[144,128]{1,0:T(8,128)(2,1)S(1)}, u32[]{:S(2)}, u32[]{:S(2)}) %collective-permute-start.2) | collective-permute-done | bytes 36896 | tf_op jit(solution)/shard_map/ppermute | solution.py:337
  30.1 0.0 all-to-all-done
  30.1 3.6 %first.1 = (f32[136,512]{1,0:T(8,128)S(1)}, bf16[256,2432]{1,0:T(8,128)(2,1)S(1)}, bf16[2432,256]{1,0:T(8,128)(2,1)S(1)}, bf16[128,128]{1,0:T(8,128)(2,1)S(1)}) custom-call(bf16[128,512]{1,0:T(8,128)(2,1)S(1)} %collective-permute-done.q, bf16[16,256,128]{2,1,0:T(8,128)(2,1)S(1)} %bitcast.13, bf16[144,128]{1,0:T(8,128)(2,1)S(1)} %bitcast.21, ...), custom_call_target="tpu_custom_call" | custom-call | flops 1048576 | bytes 65536 | tf_op jit(solution)/shard_map/first/pallas_call | solution.py:278
  33.7 3.0 %collective-permute-start.4 = (f16[136,512]{1,0:T(8,128)(2,1)S(1)}, f16[136,512]{1,0:T(8,128)(2,1)S(1)}, u32[]{:S(2)}, u32[]{:S(2)}) collective-permute-start(f16[136,512]{1,0:T(8,128)(2,1)S(1)} %convert_element_type.15), channel_id=1, source_target_pairs={{0,16},{8,24},{16,0},{24,8},{1,17},{9,25},{17,1},{25,9},{2,18},{10... | collective-permute-start | bytes 417800 | tf_op jit(solution)/shard_map/ppermute | solution.py:341
  36.7 5.1 %more.3 = (f32[136,512]{1,0:T(8,128)S(1)}, f32[136,512]{1,0:T(8,128)S(1)}) custom-call(bf16[128,512]{1,0:T(8,128)(2,1)S(1)} %get-tuple-element.25.refs_0_, bf16[128,512]{1,0:T(8,128)(2,1)S(1)} %get-tuple-element.24.refs_1_, bf16[256,2432]{1,0:T(8,128)(2,1)S(1)} %get-tuple-element.18.refs_1_.refs_2_, bf16[2432,256]{1,0:T(8,128)(2,1)S(1)} %get-tuple-element.19.refs_2_.refs_3_, ...), custom_call_target="tpu_custom_call" | custom-call | flops 2097152 | bytes 131072 | tf_op jit(solution)/shard_map/more/pallas_call | solution.py:297
  41.9 1.2 %collective-permute-start.7 = (f16[136,512]{1,0:T(8,128)(2,1)S(1)}, f16[136,512]{1,0:T(8,128)(2,1)S(1)}, u32[]{:S(2)}, u32[]{:S(2)}) collective-permute-start(f16[136,512]{1,0:T(8,128)(2,1)S(1)} %convert_element_type.18), channel_id=1, source_target_pairs={{0,24},{8,16},{16,8},{24,0},{1,25},{9,17},{17,9},{25,1},{2,26},{10... | collective-permute-start | bytes 417800 | tf_op jit(solution)/shard_map/ppermute | solution.py:341
  43.2 0.3 collective-permute-start.6
  44.1 1.5 %append.1 = bf16[12,32,2,512]{3,2,1,0:T(2,128)(2,1)} custom-call(s32[1,1]{1,0:T(1,128)S(6)} %copy.11.page_in, f32[136,512]{1,0:T(8,128)S(1)} %get-tuple-element.23.after, bf16[12,32,2,512]{3,2,1,0:T(2,128)(2,1)S(1)} %bitcast.15, bf16[8,2,512]{2,1,0:T(2,128)(2,1)S(1)} %bitcast.20), custom_call_target="tpu_custom_call" | custom-call | flops 1048576 | bytes 65536 | tf_op jit(solution)/shard_map/append/pallas_call | solution.py:154
  45.7 2.8 %more.2.g0 = f32[136,512]{1,0:T(8,128)S(1)} custom-call(bf16[128,512]{1,0:T(8,128)(2,1)S(1)} %bitcast.18, bf16[256,2432]{1,0:T(8,128)(2,1)S(1)} %get-tuple-element.18.refs_1_.refs_2_, bf16[2432,256]{1,0:T(8,128)(2,1)S(1)} %get-tuple-element.19.refs_2_.refs_3_, bf16[128,128]{1,0:T(8,128)(2,1)S(1)} %get-tuple-element.20.refs_3_.refs_4_, ...), custom_call_target="tpu_custom_call" | custom-call | flops 1048576 | bytes 65536 | tf_op jit(solution)/shard_map/more/pallas_call | solution.py:297
  48.5 0.1 maximum_convert_fusion.g
  48.6 1.2 %combine.1 = bf16[128,512]{1,0:T(8,128)(2,1)} custom-call(f32[136,512]{1,0:T(8,128)S(1)} %more.2.g0, f32[136,512]{1,0:T(8,128)S(1)} %convert_element_type.16.refs_4_.g2, f32[2,136,512]{2,1,0:T(8,128)S(1)} %maximum_convert_fusion.g), custom_call_target="tpu_custom_call" | custom-call | tf_op jit(solution)/shard_map/combine/pallas_call | solution.py:326
  (21 shorter events, 0.2 us)
Async XLA Ops:
  4.1 8.7 %copy-start.1 = (bf16[1,128,512]{2,1,0:T(8,128)(2,1)S(1)}, bf16[1,128,512]{2,1,0:T(8,128)(2,1)}, u32[]{:S(2)}) copy-start(bf16[1,128,512]{2,1,0:T(8,128)(2,1)} %param.8) | copy-start | bytes 393220
  4.1 17.5 %copy-start.6 = (bf16[72,2,128]{2,1,0:T(2,128)(2,1)S(1)}, bf16[72,2,128]{2,1,0:T(2,128)(2,1)}, u32[]{:S(2)}) copy-start(bf16[72,2,128]{2,1,0:T(2,128)(2,1)} %get-tuple-element.15) | copy-start | bytes 110596
  4.1 19.1 %copy-start.5 = (bf16[72,2,128]{2,1,0:T(2,128)(2,1)S(1)}, bf16[72,2,128]{2,1,0:T(2,128)(2,1)}, u32[]{:S(2)}) copy-start(bf16[72,2,128]{2,1,0:T(2,128)(2,1)} %get-tuple-element.16) | copy-start | bytes 110596
  4.1 21.8 %copy-start.4 = (bf16[72,2,128]{2,1,0:T(2,128)(2,1)S(1)}, bf16[72,2,128]{2,1,0:T(2,128)(2,1)}, u32[]{:S(2)}) copy-start(bf16[72,2,128]{2,1,0:T(2,128)(2,1)} %get-tuple-element.17) | copy-start | bytes 110596
  4.2 25.9 %copy-start.3 = (bf16[72,2,128]{2,1,0:T(2,128)(2,1)S(1)}, bf16[72,2,128]{2,1,0:T(2,128)(2,1)}, u32[]{:S(2)}) copy-start(bf16[72,2,128]{2,1,0:T(2,128)(2,1)} %get-tuple-element.14) | copy-start | bytes 110596
  4.2 25.9 %all-to-all-start = ((bf16[32,128,128]{2,1,0:T(8,128)(2,1)}), bf16[32,128,128]{2,1,0:T(8,128)(2,1)S(1)}, u32[]{:S(2)}, u32[]{:S(2)}) async-start(bf16[32,128,128]{2,1,0:T(8,128)(2,1)} %bitcast.22), calls=%async_computation | async-start | bytes 2097152 | tf_op jit(solution)/shard_map/all_to_all | solution.py:349
  12.9 7.3 %collective-permute-start = (bf16[128,512]{1,0:T(8,128)(2,1)S(1)}, bf16[128,512]{1,0:T(8,128)(2,1)S(1)}, u32[]{:S(2)}, u32[]{:S(2)}) collective-permute-start(bf16[128,512]{1,0:T(8,128)(2,1)S(1)} %bitcast.16), channel_id=1, source_target_pairs={{0,16},{8,24},{16,0},{24,8},{1,17},{9,25},{17,1},{25,9},{2,18},{10... | collective-permute-start | bytes 393224 | tf_op jit(solution)/shard_map/ppermute | solution.py:341
  20.1 7.8 %collective-permute-start.5 = (bf16[256,512]{1,0:T(8,128)(2,1)S(1)}, bf16[256,512]{1,0:T(8,128)(2,1)S(1)}, u32[]{:S(2)}, u32[]{:S(2)}) collective-permute-start(bf16[256,512]{1,0:T(8,128)(2,1)S(1)} %pad_maximum_fusion), channel_id=1, source_target_pairs={{0,8},{8,0},{16,24},{24,16},{1,9},{9,1},{17,25},{25,17},{2,10},{10... | collective-permute-start | bytes 786440 | tf_op jit(solution)/shard_map/ppermute | solution.py:341
  21.6 7.5 %collective-permute-start.1 = (bf16[144,128]{1,0:T(8,128)(2,1)S(1)}, bf16[144,128]{1,0:T(8,128)(2,1)S(1)}, u32[]{:S(2)}, u32[]{:S(2)}) collective-permute-start(bf16[144,128]{1,0:T(8,128)(2,1)S(1)} %bitcast.29), channel_id=1, source_target_pairs={{0,32},{32,64},{64,96},{96,0},{1,33},{33,65},{65,97},{97,1},{2,34}... | collective-permute-start | bytes 110600 | tf_op jit(solution)/shard_map/ppermute | solution.py:337
  23.3 6.8 %collective-permute-start.2 = (bf16[144,128]{1,0:T(8,128)(2,1)S(1)}, bf16[144,128]{1,0:T(8,128)(2,1)S(1)}, u32[]{:S(2)}, u32[]{:S(2)}) collective-permute-start(bf16[144,128]{1,0:T(8,128)(2,1)S(1)} %bitcast.28), channel_id=1, source_target_pairs={{0,64},{32,96},{64,0},{96,32},{1,65},{33,97},{65,1},{97,33},{2,66}... | collective-permute-start | bytes 110600 | tf_op jit(solution)/shard_map/ppermute | solution.py:337
  25.9 4.1 %collective-permute-start.3 = (bf16[144,128]{1,0:T(8,128)(2,1)S(1)}, bf16[144,128]{1,0:T(8,128)(2,1)S(1)}, u32[]{:S(2)}, u32[]{:S(2)}) collective-permute-start(bf16[144,128]{1,0:T(8,128)(2,1)S(1)} %bitcast.27), channel_id=1, source_target_pairs={{0,96},{32,0},{64,32},{96,64},{1,97},{33,1},{65,33},{97,65},{2,98}... | collective-permute-start | bytes 110600 | tf_op jit(solution)/shard_map/ppermute | solution.py:337
  33.7 11.9 %collective-permute-start.4 = (f16[136,512]{1,0:T(8,128)(2,1)S(1)}, f16[136,512]{1,0:T(8,128)(2,1)S(1)}, u32[]{:S(2)}, u32[]{:S(2)}) collective-permute-start(f16[136,512]{1,0:T(8,128)(2,1)S(1)} %convert_element_type.15), channel_id=1, source_target_pairs={{0,16},{8,24},{16,0},{24,8},{1,17},{9,25},{17,1},{25,9},{2,18},{10... | collective-permute-start | bytes 417800 | tf_op jit(solution)/shard_map/ppermute | solution.py:341
  36.7 7.4 %copy-start = (bf16[1,12,32,2,512]{4,3,2,1,0:T(2,128)(2,1)S(1)}, bf16[1,12,32,2,512]{4,3,2,1,0:T(2,128)(2,1)}, u32[]{:S(2)}) copy-start(bf16[1,12,32,2,512]{4,3,2,1,0:T(2,128)(2,1)} %param.10) | copy-start | bytes 2359300
  36.7 7.4 %copy-start.2 = (bf16[1,8,2,512]{3,2,1,0:T(2,128)(2,1)S(1)}, bf16[1,8,2,512]{3,2,1,0:T(2,128)(2,1)}, u32[]{:S(2)}) copy-start(bf16[1,8,2,512]{3,2,1,0:T(2,128)(2,1)} %param.9) | copy-start | bytes 49156
  41.9 6.6 %collective-permute-start.7 = (f16[136,512]{1,0:T(8,128)(2,1)S(1)}, f16[136,512]{1,0:T(8,128)(2,1)S(1)}, u32[]{:S(2)}, u32[]{:S(2)}) collective-permute-start(f16[136,512]{1,0:T(8,128)(2,1)S(1)} %convert_element_type.18), channel_id=1, source_target_pairs={{0,24},{8,16},{16,8},{24,0},{1,25},{9,17},{17,9},{25,1},{2,26},{10... | collective-permute-start | bytes 417800 | tf_op jit(solution)/shard_map/ppermute | solution.py:341
  43.2 5.3 %collective-permute-start.6 = (f16[136,512]{1,0:T(8,128)(2,1)S(1)}, f16[136,512]{1,0:T(8,128)(2,1)S(1)}, u32[]{:S(2)}, u32[]{:S(2)}) collective-permute-start(f16[136,512]{1,0:T(8,128)(2,1)S(1)} %convert_element_type.17), channel_id=1, source_target_pairs={{0,8},{8,0},{16,24},{24,16},{1,9},{9,1},{17,25},{25,17},{2,10},{10... | collective-permute-start | bytes 417800 | tf_op jit(solution)/shard_map/ppermute | solution.py:341

commit v4 on v3

--- a/solution.py
+++ b/solution.py
@@ -30,7 +30,7 @@
 MIG_ROWS = INST * KVH * MOST * PAGE
 OLD_ROWS = (TABLE - MOST) * PAGE * KVH
 ROWS = MIG_ROWS + OLD_ROWS + 128
-CHUNK = 256
+SPANS = (0, 1280, ROWS)
 
 SMEM = pl.BlockSpec(memory_space=pltpu.SMEM)
 HBM = pl.BlockSpec(memory_space=pltpu.HBM)
@@ -167,101 +167,117 @@
     )(page, after, pool, new)
 
 
-def pickers():
+def put(x, pick, kk, vt, at, marks=None):
+    lane = lax.broadcasted_iota(jnp.int32, (128, 128), 1)
+    keys = jnp.dot(pick[0], x, preferred_element_type=F32)
+    kk[at, 0:128] = keys.astype(BF)
+    if marks is None:
+        marks = jnp.where((lane == 0) & (keys > 64.0), BIG, 0.0)
+    kk[at, 128:256] = marks.astype(BF)
+    vals = lax.dot_general(x, pick[1], (((0,), (0,)), ((), ())), preferred_element_type=F32)
+    vt[0:128, at] = vals.astype(BF)
+
+
+def fill(mig, parts, kk, vt):
+    row = lax.broadcasted_iota(jnp.int32, (128, 256), 0)
+    col = lax.broadcasted_iota(jnp.int32, (128, 256), 1)
+    keys = (col == 2 * row).astype(BF)
     row = lax.broadcasted_iota(jnp.int32, (256, 128), 0)
     col = lax.broadcasted_iota(jnp.int32, (256, 128), 1)
-    keys = (row == 2 * col).astype(BF)
-    row = lax.broadcasted_iota(jnp.int32, (128, 256), 0)
-    col = lax.broadcasted_iota(jnp.int32, (128, 256), 1)
-    return keys, (col == 2 * row + 1).astype(BF)
-
-
-def put(x, pick, kt, vv, at):
-    keys = lax.dot_general(x, pick[0], (((0,), (0,)), ((), ())), preferred_element_type=F32)
-    kt[0:128, at] = keys.astype(BF)
-    sub = lax.broadcasted_iota(jnp.int32, (128, 128), 0)
-    kt[128:256, at] = jnp.where((sub == 0) & (keys > 64.0), BIG, 0.0).astype(BF)
-    vals = jnp.dot(pick[1], x, preferred_element_type=F32)
-    vv[at, 0:128] = vals.astype(BF)
-    vv[at, 128:256] = jnp.ones((128, 128), BF)
-
-
-def fill(mig, parts, kt, vv, aug):
-    x_here, y_here, _ = here()
-    pick = pickers()
+    pick = (keys, (row == 2 * col + 1).astype(BF))
+    vt[128:144, :] = jnp.ones((16, ROWS), BF)
     for i in range(MIG_ROWS // 128):
-        put(mig[i], pick, kt, vv, slice(i * 128, i * 128 + 128))
+        put(mig[i], pick, kk, vt, slice(i * 128, i * 128 + 128))
     for i in range(2):
         x = jnp.concatenate([parts[2 * i][0:128], parts[2 * i + 1][0:128]], axis=0)
         at = MIG_ROWS + i * 128
-        put(x, pick, kt, vv, slice(at, at + 128))
+        put(x, pick, kk, vt, slice(at, at + 128))
     at = MIG_ROWS + OLD_ROWS
-    fresh = [r[128:144] for r in parts] + [jnp.zeros((192, 128), BF)]
-    put(jnp.concatenate(fresh, axis=0), pick, kt, vv, slice(at, at + 128))
+    x = jnp.concatenate([r[128:144] for r in parts] + [jnp.zeros((192, 128), BF)], axis=0)
     sub = lax.broadcasted_iota(jnp.int32, (128, 128), 0)
     lane = lax.broadcasted_iota(jnp.int32, (128, 128), 1)
-    hot = jnp.where((sub == 1 + lane) & (lane < 32), 1.0, 0.0)
-    kt[128:256, at : at + 128] = jnp.where((sub == 0) & (lane >= 32), BIG, hot).astype(BF)
-    j = lane - 1
+    hot = jnp.where((lane == 1 + sub) & (sub < 32), 1.0, 0.0)
+    marks = jnp.where((lane == 0) & (sub >= 32), BIG, hot)
+    put(x, pick, kk, vt, slice(at, at + 128), marks)
+
+
+def turn_kernel(q0, q2, pair, out):
+    x_here, y_here, _ = here()
+    sub = lax.broadcasted_iota(jnp.int32, (128, 128), 0)
+    lane = lax.broadcasted_iota(jnp.int32, (128, 128), 1)
+    j = sub - 1
     source = (y_here + 4 - (j >> 3)) & 3
     pos = source * 32 + x_here * 8 + (j & 7)
-    bar = jnp.where((lane >= 1) & (lane < 33) & (pos > sub), BIG, 0.0)
-    aug[...] = jnp.where(lane == 0, 1.0, bar).astype(BF)
-
-
-def rows_of(qs, outs, kt, vv, aug, s_ref):
-    per = CHUNK // 128
-    units = [(i, c) for i in range(len(qs)) for c in range(512 // CHUNK)]
-    lane = lax.broadcasted_iota(jnp.int32, (128, 128), 1)
-    stats = [jnp.zeros((128, 128), F32) for _ in qs]
+    bar = jnp.where((sub >= 1) & (sub < 33) & (pos > lane), BIG, 0.0)
+    aug = jnp.where(sub == 0, 1.0, bar).astype(BF)
+    for k, q in enumerate((q0, pair.at[0:128], q2, pair.at[128:256])):
+        for h in range(4):
+            lanes = slice(h * 128, h * 128 + 128)
+            out[k, 0:128, lanes] = q[:, lanes].astype(F32).T.astype(BF)
+            out[k, 128:256, lanes] = aug
+
+
+def turn(q, q2, pair):
+    return pl.pallas_call(
+        turn_kernel,
+        in_specs=[VMEM] * 3,
+        out_specs=VMEM,
+        out_shape=jax.ShapeDtypeStruct((4, 256, 512), BF),
+        compiler_params=pltpu.CompilerParams(vmem_limit_bytes=8 << 20),
+        cost_estimate=cost(1),
+        name="turn",
+    )(q, q2, pair)
+
+
+def attend(ks, outs, qt, kk, vt, s_ref):
+    units = [(i, t) for i in range(len(ks)) for t in range(len(SPANS) - 1)]
 
     def score(u):
-        i, c = units[u]
-        q = [
-            jnp.concatenate([qs[i][:, (c * per + h) * 128 : (c * per + h + 1) * 128], aug[...]], 1)
-            for h in range(per)
-        ]
-        s_ref[u % 2] = jnp.dot(jnp.concatenate(q, 0), kt[...], preferred_element_type=F32)
+        i, t = units[u]
+        rows = slice(SPANS[t], SPANS[t + 1])
+        size = SPANS[t + 1] - SPANS[t]
+        s_ref[u % 2, 0:size] = jnp.dot(kk[rows], qt[ks[i]], preferred_element_type=F32)
 
     score(0)
-    for u, (i, c) in enumerate(units):
+    for u, (i, t) in enumerate(units):
         if u + 1 < len(units):
             score(u + 1)
-        s = s_ref[u % 2]
-        top = jnp.max(s, axis=1, keepdims=True)
+        rows = slice(SPANS[t], SPANS[t + 1])
+        s = s_ref[u % 2, 0 : SPANS[t + 1] - SPANS[t]]
+        top = jnp.max(s, axis=0, keepdims=True)
         p = jnp.exp2((s - top) * LOG_SCALE)
         high = p.astype(BF)
         low = (p - high.astype(F32)).astype(BF)
-        o = jnp.dot(high, vv[...], preferred_element_type=F32)
-        o += jnp.dot(low, vv[...], preferred_element_type=F32)
-        total = o[:, 128:]
-        mean = o[:, :128] / total
-        most = jnp.maximum(jnp.max(jnp.abs(mean), axis=1, keepdims=True), 1e-30)
-        mean = mean / most
-        lse = jnp.log2(total) + top * LOG_SCALE
-        num = lse + jnp.log2(most)
-        for h in range(per):
-            part = slice(h * 128, h * 128 + 128)
-            at = c * per + h
-            outs[i][0:128, at * 128 : at * 128 + 128] = mean[part]
-            stats[i] = jnp.where(lane == at, lse[part], stats[i])
-            stats[i] = jnp.where(lane == 4 + at, num[part], stats[i])
-    for i, out in enumerate(outs):
-        rows = stats[i].T[0:8]
-        high = jnp.floor(rows * 2.0 + 0.5) * 0.5
-        out[128:136, 0:128] = high
-        out[128:136, 128:256] = rows - high
-        out[128:136, 256:512] = jnp.zeros((8, 256), F32)
-
-
-def first_kernel(q, mig, r0, r1, r2, r3, out, kt, vv, aug, s_ref):
-    fill(mig, (r0, r1, r2, r3), kt, vv, aug)
-    rows_of((q,), (out,), kt, vv, aug, s_ref)
-
-
-def more_kernel(count, *refs):
-    *qs, kt, vv, aug = refs[: count + 3]
-    rows_of(qs, refs[-1 - count : -1], kt, vv, aug, refs[-1])
+        o = jnp.dot(vt[:, rows], high, preferred_element_type=F32)
+        o += jnp.dot(vt[:, rows], low, preferred_element_type=F32)
+        if t == 0:
+            best, sums = top, o
+        else:
+            both = jnp.maximum(best, top)
+            sums = sums * jnp.exp2((best - both) * LOG_SCALE) + o * jnp.exp2((top - both) * LOG_SCALE)
+            best = both
+        if t + 2 < len(SPANS):
+            continue
+        total = sums[128:129]
+        mean = sums[0:128] / total
+        most = jnp.maximum(jnp.max(jnp.abs(mean), axis=0, keepdims=True), 1e-30)
+        den = jnp.log2(total) + best * LOG_SCALE
+        num = den + jnp.log2(most)
+        outs[i][0:128] = mean / most
+        rows = []
+        for x in (den, num):
+            high = jnp.floor(x * 2.0 + 0.5) * 0.5
+            rows += [high, x - high]
+        outs[i][128:136] = jnp.concatenate(rows + [jnp.zeros((4, 512), F32)], axis=0)
+
+
+def first_kernel(k, qt, mig, r0, r1, r2, r3, out, kk, vt, s_ref):
+    fill(mig, (r0, r1, r2, r3), kk, vt)
+    attend((k,), (out,), qt, kk, vt, s_ref)
+
+
+def more_kernel(ks, qt, kk, vt, *refs):
+    attend(ks, refs[-1 - len(ks) : -1], qt, kk, vt, refs[-1])
 
 
 def cost(count):
@@ -271,55 +287,51 @@
 
 
 PART = jax.ShapeDtypeStruct((136, 512), F32)
-SCORES = pltpu.VMEM((2, CHUNK, ROWS), F32)
-
-
-def first(q, mig, parts):
-    return pl.pallas_call(
-        first_kernel,
+SCORES = pltpu.VMEM((2, max(b - a for a, b in zip(SPANS, SPANS[1:])), 512), F32)
+
+
+def first(k, qt, mig, parts):
+    return pl.pallas_call(
+        functools.partial(first_kernel, k),
         in_specs=[VMEM] * 6,
-        out_specs=[VMEM] * 4,
+        out_specs=[VMEM] * 3,
         out_shape=[
             PART,
-            jax.ShapeDtypeStruct((256, ROWS), BF),
             jax.ShapeDtypeStruct((ROWS, 256), BF),
-            jax.ShapeDtypeStruct((128, 128), BF),
+            jax.ShapeDtypeStruct((144, ROWS), BF),
         ],
         scratch_shapes=[SCORES],
         compiler_params=pltpu.CompilerParams(vmem_limit_bytes=28 << 20),
         cost_estimate=cost(1),
         name="first",
-    )(q, mig, *parts)
-
-
-def more(qs, kt, vv, aug, after=None):
+    )(qt, mig, *parts)
+
+
+def more(ks, qt, kk, vt, after=None):
     late = () if after is None else (after,)
     return pl.pallas_call(
-        functools.partial(more_kernel, len(qs)),
-        in_specs=[VMEM] * (len(qs) + 3) + [HBM] * len(late),
-        out_specs=[VMEM] * len(qs),
-        out_shape=[PART] * len(qs),
+        functools.partial(more_kernel, ks),
+        in_specs=[VMEM] * 3 + [HBM] * len(late),
+        out_specs=[VMEM] * len(ks),
+        out_shape=[PART] * len(ks),
         scratch_shapes=[SCORES],
         compiler_params=pltpu.CompilerParams(vmem_limit_bytes=28 << 20),
-        cost_estimate=cost(len(qs)),
+        cost_estimate=cost(len(ks)),
         name="more",
-    )(*qs, kt, vv, aug, *late)
+    )(qt, kk, vt, *late)
 
 
 def combine_kernel(g0, g2, g, out):
     parts = (g0, g2, g.at[0], g.at[1])
-    stats = [g[128:136, 0:128] + g[128:136, 128:256] for g in parts]
-    dens = [x[0:4] for x in stats]
+    dens = [x[128:129] + x[129:130] for x in parts]
     top = functools.reduce(jnp.maximum, dens)
     share = 1.0 / sum(jnp.exp2(x - top) for x in dens)
-    rows = [jnp.exp2(x[4:8] - top) * share for x in stats]
-    cols = jnp.concatenate(rows + [jnp.zeros((112, 128), F32)], axis=0).T
+    result = sum(
+        x[0:128] * (jnp.exp2(x[130:131] + x[131:132] - top) * share) for x in parts
+    )
     for h in range(4):
         lanes = slice(h * 128, h * 128 + 128)
-        result = sum(
-            g[0:128, lanes] * cols[:, 4 * k + h : 4 * k + h + 1] for k, g in enumerate(parts)
-        )
-        out[:, lanes] = result.astype(BF)
+        out[:, lanes] = result[:, lanes].T.astype(BF)
 
 
 def combine(*parts):
@@ -350,15 +362,16 @@
     parts = [r.reshape(REST * 2, D) for r in parts]
     parts = [parts[0]] + [shift(parts[k], "y", k) for k in range(1, 4)]
     q2 = swap(q, 2)
-    pair = swap(jnp.concatenate([q, q2], axis=0), 1)
-    qs = [q, pair[:128], q2, pair[128:]]
-    out2, *shared = first(qs[2], mig.reshape(MIG_ROWS // 128, 256, D), parts)
+    updated = append(append_page, parts[0], pool[0], fresh)
+    far, updated = lax.optimization_barrier((q2, updated))
+    pair = swap(jnp.concatenate([q, far], axis=0), 1)
+    qt = turn(q, q2, pair)
+    out2, kk, vt = first(2, qt, mig.reshape(MIG_ROWS // 128, 256, D), parts)
     got2 = swap(out2.astype(F16), 2).astype(F32)
-    out1, out3 = more((qs[1], qs[3]), *shared)
+    out1, out3 = more((1, 3), qt, kk, vt)
     sent = [swap(out.astype(F16), k) for k, out in ((1, out1), (3, out3))]
     got = jnp.stack(sent).astype(F32)
-    (out0,) = more((q,), *shared, after=got2)
-    updated = append(append_page, out3, pool[0], fresh)
+    (out0,) = more((0,), qt, kk, vt, after=got2)
     return combine(out0, got2, got)[None], updated[None]
 
 

time: 50.5 us -> 48.1 us (0.952); the launches traced: 49.7 us -> 47.9 us
  Pallas kernels: 17.1 us -> 15.3 us
    pallas_call x3 -> x4, Pallas kernels: 11.6 us -> 10.1 us  [the longest x2 6.8 us: more(): pl.pallas_call(functools.partial(more_kernel, ks), in_specs=[VMEM] * 3 +...]
  transfers between devices with their start and end apart: 9 -> 9, of which waited for: 4 -> 6; matrix products, arithmetic and copies ran while one was open for 0% -> 0% of each run, Pallas kernels for 19% -> 18%
where the time goes in v4:
time: 48.1 us; the launch traced here: 47.9 us
  starting transfers between devices  23.3 us (48%)
  Pallas kernels  15.3 us (32%)
  waiting for transfers between devices  6.93 us (14%)
  between operations  2.12 us (4%)
    ppermute x5, starting transfers between devices, swap(): return lax.ppermute(value, 'x', [(i, i ^ k) for i in range(4)])  8.86 us
    all_to_all x1, starting transfers between devices, local(): mig = lax.all_to_all(mig, ('ba', 'y'), 0, 0, tiled=True)  8.63 us
    pallas_call x2, Pallas kernels, more(): pl.pallas_call(functools.partial(more_kernel, ks), in_specs=[VMEM] * 3 +...  6.8 us
    ppermute x3, starting transfers between devices, shift(): return lax.ppermute(value, axis, [(i, (i + k) % 4) for i in range(4)])  5.8 us
    ppermute x5, waiting for transfers between devices, swap(): return lax.ppermute(value, 'x', [(i, i ^ k) for i in range(4)])  5.06 us
    pallas_call x1, Pallas kernels, first(): pl.pallas_call(functools.partial(first_kernel, k), in_specs=[VMEM] * 6, o...  3.03 us
    pallas_call x1, Pallas kernels, pack(): pl.pallas_call(pack_kernel, in_specs=[HBM, VMEM, HBM, HBM, HBM, VMEM], ou...  2.88 us
    ppermute x3, waiting for transfers between devices, shift(): return lax.ppermute(value, axis, [(i, (i + k) % 4) for i in range(4)])  1.87 us
  transfers between devices with their start and end apart: 9, of which 6 were waited for; matrix products, arithmetic and copies ran while one was open for 0% of the time, Pallas kernels for 18%

profile of v4, /device:TPU:0, one launch (start us, length us, event | category | flops | bytes accessed | tf_op | source)
XLA Modules:
  0.0 47.9 jit_solution(14141375731575909922)
XLA Ops:
  1.3 2.9 %pack.1 = (bf16[8,4,2,32,2,128]{5,4,3,2,1,0:T(2,128)(2,1)}, bf16[72,2,128]{2,1,0:T(2,128)(2,1)}, bf16[72,2,128]{2,1,0:T(2,128)(2,1)}, bf16[72,2,128]{2,1,0:T(2,128)(2,1)}, bf16[72,2,128]{2,1,0:T(2,128)(2,1)}) custom-call(s32[1,4]{1,0:T(1,128)} %table_in.1, s32[1,1]{1,0:T(1,128)S(6)} %copy.10.ctx_in, s32[1,7]{1,0:T(1,128)} %page_in.2, s32[1,7]{1,0:T(1,128)} %dest_in.1, ...), custom_call_target="tpu_custom_call" | custom-call | tf_op jit(solution)/shard_map/pack/pallas_call | solution.py:118
  4.2 0.0 copy-start.1
  4.2 8.6 %all-to-all-start = ((bf16[32,128,128]{2,1,0:T(8,128)(2,1)}), bf16[32,128,128]{2,1,0:T(8,128)(2,1)S(1)}, u32[]{:S(2)}, u32[]{:S(2)}) async-start(bf16[32,128,128]{2,1,0:T(8,128)(2,1)} %bitcast.23), calls=%async_computation | async-start | bytes 2097152 | tf_op jit(solution)/shard_map/all_to_all | solution.py:361
  12.9 3.0 %collective-permute-start = (bf16[128,512]{1,0:T(8,128)(2,1)S(1)}, bf16[128,512]{1,0:T(8,128)(2,1)S(1)}, u32[]{:S(2)}, u32[]{:S(2)}) collective-permute-start(bf16[128,512]{1,0:T(8,128)(2,1)S(1)} %bitcast.16), channel_id=1, source_target_pairs={{0,16},{8,24},{16,0},{24,8},{1,17},{9,25},{17,1},{25,9},{2,18},{10... | collective-permute-start | bytes 393224 | tf_op jit(solution)/shard_map/ppermute | solution.py:353
  16.5 1.5 %append.1 = bf16[12,32,2,512]{3,2,1,0:T(2,128)(2,1)} custom-call(s32[1,1]{1,0:T(1,128)S(6)} %copy.11.page_in, bf16[144,128]{1,0:T(8,128)(2,1)S(1)} %bitcast.19, bf16[12,32,2,512]{3,2,1,0:T(2,128)(2,1)S(1)} %bitcast.15, bf16[8,2,512]{2,1,0:T(2,128)(2,1)S(1)} %bitcast.22), custom_call_target="tpu_custom_call" | custom-call | flops 1048576 | bytes 65536 | tf_op jit(solution)/shard_map/append/pallas_call | solution.py:154
  18.0 2.1 %collective-permute-done.q2 = bf16[128,512]{1,0:T(8,128)(2,1)S(1)} collective-permute-done((bf16[128,512]{1,0:T(8,128)(2,1)S(1)}, bf16[128,512]{1,0:T(8,128)(2,1)S(1)}, u32[]{:S(2)}, u32[]{:S(2)}) %collective-permute-start) | collective-permute-done | bytes 131104 | tf_op jit(solution)/shard_map/ppermute | solution.py:353
  20.2 1.6 %collective-permute-start.1 = (bf16[256,512]{1,0:T(8,128)(2,1)S(1)}, bf16[256,512]{1,0:T(8,128)(2,1)S(1)}, u32[]{:S(2)}, u32[]{:S(2)}) collective-permute-start(bf16[256,512]{1,0:T(8,128)(2,1)S(1)} %pad_maximum_fusion), channel_id=1, source_target_pairs={{0,8},{8,0},{16,24},{24,16},{1,9},{9,1},{17,25},{25,17},{2,10},{10... | collective-permute-start | bytes 786440 | tf_op jit(solution)/shard_map/ppermute | solution.py:353
  21.7 1.7 %collective-permute-start.2 = (bf16[144,128]{1,0:T(8,128)(2,1)S(1)}, bf16[144,128]{1,0:T(8,128)(2,1)S(1)}, u32[]{:S(2)}, u32[]{:S(2)}) collective-permute-start(bf16[144,128]{1,0:T(8,128)(2,1)S(1)} %bitcast.30), channel_id=1, source_target_pairs={{0,32},{32,64},{64,96},{96,0},{1,33},{33,65},{65,97},{97,1},{2,34}... | collective-permute-start | bytes 110600 | tf_op jit(solution)/shard_map/ppermute | solution.py:349
  23.4 2.7 %collective-permute-start.3 = (bf16[144,128]{1,0:T(8,128)(2,1)S(1)}, bf16[144,128]{1,0:T(8,128)(2,1)S(1)}, u32[]{:S(2)}, u32[]{:S(2)}) collective-permute-start(bf16[144,128]{1,0:T(8,128)(2,1)S(1)} %bitcast.29), channel_id=1, source_target_pairs={{0,64},{32,96},{64,0},{96,32},{1,65},{33,97},{65,1},{97,33},{2,66}... | collective-permute-start | bytes 110600 | tf_op jit(solution)/shard_map/ppermute | solution.py:349
  26.1 1.5 %collective-permute-start.4 = (bf16[144,128]{1,0:T(8,128)(2,1)S(1)}, bf16[144,128]{1,0:T(8,128)(2,1)S(1)}, u32[]{:S(2)}, u32[]{:S(2)}) collective-permute-start(bf16[144,128]{1,0:T(8,128)(2,1)S(1)} %bitcast.28), channel_id=1, source_target_pairs={{0,96},{32,0},{64,32},{96,64},{1,97},{33,1},{65,33},{97,65},{2,98}... | collective-permute-start | bytes 110600 | tf_op jit(solution)/shard_map/ppermute | solution.py:349
  27.6 0.4 collective-permute-done.1.pair
  27.9 0.3 turn.1.qt
  28.2 1.0 %collective-permute-done.2.r1 = bf16[144,128]{1,0:T(8,128)(2,1)S(1)} collective-permute-done((bf16[144,128]{1,0:T(8,128)(2,1)S(1)}, bf16[144,128]{1,0:T(8,128)(2,1)S(1)}, u32[]{:S(2)}, u32[]{:S(2)}) %collective-permute-start.2) | collective-permute-done | bytes 36896 | tf_op jit(solution)/shard_map/ppermute | solution.py:349
  29.1 0.9 %collective-permute-done.3.r2 = bf16[144,128]{1,0:T(8,128)(2,1)S(1)} collective-permute-done((bf16[144,128]{1,0:T(8,128)(2,1)S(1)}, bf16[144,128]{1,0:T(8,128)(2,1)S(1)}, u32[]{:S(2)}, u32[]{:S(2)}) %collective-permute-start.3) | collective-permute-done | bytes 36896 | tf_op jit(solution)/shard_map/ppermute | solution.py:349
  30.1 0.0 all-to-all-done
  30.1 3.0 %first.1 = (f32[136,512]{1,0:T(8,128)S(1)}, bf16[2432,256]{1,0:T(8,128)(2,1)S(1)}, bf16[144,2432]{1,0:T(8,128)(2,1)S(1)}) custom-call(bf16[4,256,512]{2,1,0:T(8,128)(2,1)S(1)} %turn.1.qt, bf16[16,256,128]{2,1,0:T(8,128)(2,1)S(1)} %bitcast.13, bf16[144,128]{1,0:T(8,128)(2,1)S(1)} %bitcast.20, bf16[144,128]{1,0:T(8,128)(2,1)S(1)} %collective-permute-done.2.r1, ...), custom_call_target="tpu_custom_call" | custom-call | flops 1048576 | bytes 65536 | tf_op jit(solution)/shard_map/first/pallas_call | solution.py:294
  33.1 3.0 %collective-permute-start.5 = (f16[136,512]{1,0:T(8,128)(2,1)S(1)}, f16[136,512]{1,0:T(8,128)(2,1)S(1)}, u32[]{:S(2)}, u32[]{:S(2)}) collective-permute-start(f16[136,512]{1,0:T(8,128)(2,1)S(1)} %convert_element_type.15), channel_id=1, source_target_pairs={{0,16},{8,24},{16,0},{24,8},{1,17},{9,25},{17,1},{25,9},{2,18},{10... | collective-permute-start | bytes 417800 | tf_op jit(solution)/shard_map/ppermute | solution.py:353
  36.1 4.4 %more.3 = (f32[136,512]{1,0:T(8,128)S(1)}, f32[136,512]{1,0:T(8,128)S(1)}) custom-call(bf16[4,256,512]{2,1,0:T(8,128)(2,1)S(1)} %turn.1.qt, bf16[2432,256]{1,0:T(8,128)(2,1)S(1)} %get-tuple-element.20.kk, bf16[144,2432]{1,0:T(8,128)(2,1)S(1)} %get-tuple-element.21.vt), custom_call_target="tpu_custom_call" | custom-call | flops 2097152 | bytes 131072 | tf_op jit(solution)/shard_map/more/pallas_call | solution.py:312
  40.5 1.4 %collective-permute-start.7 = (f16[136,512]{1,0:T(8,128)(2,1)S(1)}, f16[136,512]{1,0:T(8,128)(2,1)S(1)}, u32[]{:S(2)}, u32[]{:S(2)}) collective-permute-start(f16[136,512]{1,0:T(8,128)(2,1)S(1)} %convert_element_type.18), channel_id=1, source_target_pairs={{0,24},{8,16},{16,8},{24,0},{1,25},{9,17},{17,9},{25,1},{2,26},{10... | collective-permute-start | bytes 417800 | tf_op jit(solution)/shard_map/ppermute | solution.py:353
  41.9 2.4 %more.2.g0 = f32[136,512]{1,0:T(8,128)S(1)} custom-call(bf16[4,256,512]{2,1,0:T(8,128)(2,1)S(1)} %turn.1.qt, bf16[2432,256]{1,0:T(8,128)(2,1)S(1)} %get-tuple-element.20.kk, bf16[144,2432]{1,0:T(8,128)(2,1)S(1)} %get-tuple-element.21.vt, f32[136,512]{1,0:T(8,128)S(1)} %convert_element_type.16.refs_0_.g2), custom_call_target="tpu_custom_call" | custom-call | flops 1048576 | bytes 65536 | tf_op jit(solution)/shard_map/more/pallas_call | solution.py:312
  44.4 2.5 %collective-permute-done.7 = f16[136,512]{1,0:T(8,128)(2,1)S(1)} collective-permute-done((f16[136,512]{1,0:T(8,128)(2,1)S(1)}, f16[136,512]{1,0:T(8,128)(2,1)S(1)}, u32[]{:S(2)}, u32[]{:S(2)}) %collective-permute-start.7) | collective-permute-done | bytes 139296 | tf_op jit(solution)/shard_map/ppermute | solution.py:353
  46.9 0.1 collective-permute-done.6
  47.0 0.1 maximum_convert_fusion.g
  47.0 0.8 %combine.1 = bf16[128,512]{1,0:T(8,128)(2,1)} custom-call(f32[136,512]{1,0:T(8,128)S(1)} %more.2.g0, f32[136,512]{1,0:T(8,128)S(1)} %convert_element_type.16.refs_0_.g2, f32[2,136,512]{2,1,0:T(8,128)S(1)} %maximum_convert_fusion.g), custom_call_target="tpu_custom_call" | custom-call | tf_op jit(solution)/shard_map/combine/pallas_call | solution.py:338
  (21 shorter events, 0.1 us)
Async XLA Ops:
  4.2 8.7 %copy-start.1 = (bf16[1,128,512]{2,1,0:T(8,128)(2,1)S(1)}, bf16[1,128,512]{2,1,0:T(8,128)(2,1)}, u32[]{:S(2)}) copy-start(bf16[1,128,512]{2,1,0:T(8,128)(2,1)} %param.8) | copy-start | bytes 393220
  4.2 12.3 %copy-start = (bf16[1,12,32,2,512]{4,3,2,1,0:T(2,128)(2,1)S(1)}, bf16[1,12,32,2,512]{4,3,2,1,0:T(2,128)(2,1)}, u32[]{:S(2)}) copy-start(bf16[1,12,32,2,512]{4,3,2,1,0:T(2,128)(2,1)} %param.10) | copy-start | bytes 2359300
  4.2 12.3 %copy-start.2 = (bf16[72,2,128]{2,1,0:T(2,128)(2,1)S(1)}, bf16[72,2,128]{2,1,0:T(2,128)(2,1)}, u32[]{:S(2)}) copy-start(bf16[72,2,128]{2,1,0:T(2,128)(2,1)} %get-tuple-element.14) | copy-start | bytes 110596
  4.2 12.3 %copy-start.3 = (bf16[1,8,2,512]{3,2,1,0:T(2,128)(2,1)S(1)}, bf16[1,8,2,512]{3,2,1,0:T(2,128)(2,1)}, u32[]{:S(2)}) copy-start(bf16[1,8,2,512]{3,2,1,0:T(2,128)(2,1)} %param.9) | copy-start | bytes 49156
  4.2 25.8 %all-to-all-start = ((bf16[32,128,128]{2,1,0:T(8,128)(2,1)}), bf16[32,128,128]{2,1,0:T(8,128)(2,1)S(1)}, u32[]{:S(2)}, u32[]{:S(2)}) async-start(bf16[32,128,128]{2,1,0:T(8,128)(2,1)} %bitcast.23), calls=%async_computation | async-start | bytes 2097152 | tf_op jit(solution)/shard_map/all_to_all | solution.py:361
  12.8 8.9 %copy-start.6 = (bf16[72,2,128]{2,1,0:T(2,128)(2,1)S(1)}, bf16[72,2,128]{2,1,0:T(2,128)(2,1)}, u32[]{:S(2)}) copy-start(bf16[72,2,128]{2,1,0:T(2,128)(2,1)} %get-tuple-element.17) | copy-start | bytes 110596
  12.9 10.6 %copy-start.5 = (bf16[72,2,128]{2,1,0:T(2,128)(2,1)S(1)}, bf16[72,2,128]{2,1,0:T(2,128)(2,1)}, u32[]{:S(2)}) copy-start(bf16[72,2,128]{2,1,0:T(2,128)(2,1)} %get-tuple-element.18) | copy-start | bytes 110596
  12.9 13.2 %copy-start.4 = (bf16[72,2,128]{2,1,0:T(2,128)(2,1)S(1)}, bf16[72,2,128]{2,1,0:T(2,128)(2,1)}, u32[]{:S(2)}) copy-start(bf16[72,2,128]{2,1,0:T(2,128)(2,1)} %get-tuple-element.19) | copy-start | bytes 110596
  12.9 7.3 %collective-permute-start = (bf16[128,512]{1,0:T(8,128)(2,1)S(1)}, bf16[128,512]{1,0:T(8,128)(2,1)S(1)}, u32[]{:S(2)}, u32[]{:S(2)}) collective-permute-start(bf16[128,512]{1,0:T(8,128)(2,1)S(1)} %bitcast.16), channel_id=1, source_target_pairs={{0,16},{8,24},{16,0},{24,8},{1,17},{9,25},{17,1},{25,9},{2,18},{10... | collective-permute-start | bytes 393224 | tf_op jit(solution)/shard_map/ppermute | solution.py:353
  20.2 7.8 %collective-permute-start.1 = (bf16[256,512]{1,0:T(8,128)(2,1)S(1)}, bf16[256,512]{1,0:T(8,128)(2,1)S(1)}, u32[]{:S(2)}, u32[]{:S(2)}) collective-permute-start(bf16[256,512]{1,0:T(8,128)(2,1)S(1)} %pad_maximum_fusion), channel_id=1, source_target_pairs={{0,8},{8,0},{16,24},{24,16},{1,9},{9,1},{17,25},{25,17},{2,10},{10... | collective-permute-start | bytes 786440 | tf_op jit(solution)/shard_map/ppermute | solution.py:353
  21.7 7.4 %collective-permute-start.2 = (bf16[144,128]{1,0:T(8,128)(2,1)S(1)}, bf16[144,128]{1,0:T(8,128)(2,1)S(1)}, u32[]{:S(2)}, u32[]{:S(2)}) collective-permute-start(bf16[144,128]{1,0:T(8,128)(2,1)S(1)} %bitcast.30), channel_id=1, source_target_pairs={{0,32},{32,64},{64,96},{96,0},{1,33},{33,65},{65,97},{97,1},{2,34}... | collective-permute-start | bytes 110600 | tf_op jit(solution)/shard_map/ppermute | solution.py:349
  23.4 6.6 %collective-permute-start.3 = (bf16[144,128]{1,0:T(8,128)(2,1)S(1)}, bf16[144,128]{1,0:T(8,128)(2,1)S(1)}, u32[]{:S(2)}, u32[]{:S(2)}) collective-permute-start(bf16[144,128]{1,0:T(8,128)(2,1)S(1)} %bitcast.29), channel_id=1, source_target_pairs={{0,64},{32,96},{64,0},{96,32},{1,65},{33,97},{65,1},{97,33},{2,66}... | collective-permute-start | bytes 110600 | tf_op jit(solution)/shard_map/ppermute | solution.py:349
  26.1 4.0 %collective-permute-start.4 = (bf16[144,128]{1,0:T(8,128)(2,1)S(1)}, bf16[144,128]{1,0:T(8,128)(2,1)S(1)}, u32[]{:S(2)}, u32[]{:S(2)}) collective-permute-start(bf16[144,128]{1,0:T(8,128)(2,1)S(1)} %bitcast.28), channel_id=1, source_target_pairs={{0,96},{32,0},{64,32},{96,64},{1,97},{33,1},{65,33},{97,65},{2,98}... | collective-permute-start | bytes 110600 | tf_op jit(solution)/shard_map/ppermute | solution.py:349
  33.1 8.8 %collective-permute-start.5 = (f16[136,512]{1,0:T(8,128)(2,1)S(1)}, f16[136,512]{1,0:T(8,128)(2,1)S(1)}, u32[]{:S(2)}, u32[]{:S(2)}) collective-permute-start(f16[136,512]{1,0:T(8,128)(2,1)S(1)} %convert_element_type.15), channel_id=1, source_target_pairs={{0,16},{8,24},{16,0},{24,8},{1,17},{9,25},{17,1},{25,9},{2,18},{10... | collective-permute-start | bytes 417800 | tf_op jit(solution)/shard_map/ppermute | solution.py:353
  40.5 6.3 %collective-permute-start.7 = (f16[136,512]{1,0:T(8,128)(2,1)S(1)}, f16[136,512]{1,0:T(8,128)(2,1)S(1)}, u32[]{:S(2)}, u32[]{:S(2)}) collective-permute-start(f16[136,512]{1,0:T(8,128)(2,1)S(1)} %convert_element_type.18), channel_id=1, source_target_pairs={{0,24},{8,16},{16,8},{24,0},{1,25},{9,17},{17,9},{25,1},{2,26},{10... | collective-permute-start | bytes 417800 | tf_op jit(solution)/shard_map/ppermute | solution.py:353
  41.9 5.1 %collective-permute-start.6 = (f16[136,512]{1,0:T(8,128)(2,1)S(1)}, f16[136,512]{1,0:T(8,128)(2,1)S(1)}, u32[]{:S(2)}, u32[]{:S(2)}) collective-permute-start(f16[136,512]{1,0:T(8,128)(2,1)S(1)} %convert_element_type.17), channel_id=1, source_target_pairs={{0,8},{8,0},{16,24},{24,16},{1,9},{9,1},{17,25},{25,17},{2,10},{10... | collective-permute-start | bytes 417800 | tf_op jit(solution)/shard_map/ppermute | solution.py:353

commit v5 on v4

--- a/solution.py
+++ b/solution.py
@@ -30,7 +30,8 @@
 MIG_ROWS = INST * KVH * MOST * PAGE
 OLD_ROWS = (TABLE - MOST) * PAGE * KVH
 ROWS = MIG_ROWS + OLD_ROWS + 128
-SPANS = (0, 1280, ROWS)
+WIDE = (0, 1280, ROWS)
+NARROW = (0, 640, 1280, 1920, ROWS)
 
 SMEM = pl.BlockSpec(memory_space=pltpu.SMEM)
 HBM = pl.BlockSpec(memory_space=pltpu.HBM)
@@ -46,21 +47,18 @@
 
 
 def pack_kernel(
-    table_in, ctx_in, page_in, dest_in, source, new, mig, r0, r1, r2, r3, table, ctx, page, dest,
-    pool, dead, sem_s, sem_p, sem_m, sem_r
+    table_in, page_in, dest_in, source, mig, table, page, dest, pool, dead, sem_s, sem_p, sem_m
 ):
     fetch = pltpu.make_async_copy(source, pool, sem_p)
     fetch.start()
     scalars = [
         pltpu.make_async_copy(a, b, sem_s.at[i])
-        for i, (a, b) in enumerate(
-            ((table_in, table), (ctx_in, ctx), (page_in, page), (dest_in, dest))
-        )
+        for i, (a, b) in enumerate(((table_in, table), (page_in, page), (dest_in, dest)))
     ]
     for copy in scalars:
         copy.start()
     dead[...] = jnp.full_like(dead, DEAD)
-    _, y_here, b_here = here()
+    b_here = here()[2]
     for copy in scalars:
         copy.wait()
     for d in range(INST):
@@ -82,16 +80,41 @@
             pltpu.make_async_copy(
                 pool.at[page[0, m], :, :, pl.ds(y * D, D)], mig.at[dest[0, m], y, rank], sem_m
             ).start()
-    index = lax.broadcasted_iota(jnp.int32, (PAGE, 2, KVH * D), 0)
-    for j in range(TABLE):
-        page_j = table[0, j]
-
-        @pl.when(ctx[0, 0] < (j + 1) * PAGE)
-        def _():
-            rows = pool[page_j].astype(F32)
-            alive = index < ctx[0, 0] - j * PAGE
-            pool[page_j] = jnp.where(alive, rows, DEAD).astype(BF)
-
+    for j in range(MOST):
+        for y in range(KVH):
+            pltpu.make_async_copy(
+                pool.at[table[0, j], :, :, pl.ds(y * D, D)], mig.at[b_here, y, j], sem_m
+            ).start()
+    pltpu.make_async_copy(mig, mig, sem_m).wait()
+
+
+def pack(table, page, dest, pool):
+    return pl.pallas_call(
+        pack_kernel,
+        in_specs=[HBM] * 4,
+        out_specs=HBM,
+        out_shape=jax.ShapeDtypeStruct((INST, KVH, MOST, PAGE, 2, D), BF),
+        scratch_shapes=[pltpu.SMEM(a.shape, jnp.int32) for a in (table, page, dest)]
+        + [
+            pltpu.VMEM(pool.shape, BF),
+            pltpu.VMEM((KVH, PAGE, 2, D), BF),
+            pltpu.SemaphoreType.DMA((3,)),
+            pltpu.SemaphoreType.DMA,
+            pltpu.SemaphoreType.DMA,
+        ],
+        compiler_params=pltpu.CompilerParams(vmem_limit_bytes=60 << 20),
+        name="pack",
+    )(table, page, dest, pool)
+
+
+def settle_kernel(
+    table, ctx, page, after, source, new, r0, r1, r2, r3, target, pool, sem, sem_r
+):
+    fetch = pltpu.make_async_copy(source, pool, sem.at[0])
+    fetch.start()
+    y_here = here()[1]
+    length = ctx[0, 0].astype(F32)
+    fetch.wait()
     outs = (r0, r1, r2, r3)
     for k in range(4):
         lanes = pl.ds(pl.multiple_of(lax.rem(y_here + k, 4) * D, D), D)
@@ -101,48 +124,14 @@
                 outs[k].at[pl.ds((j - MOST) * PAGE, PAGE)],
                 sem_r.at[k],
             ).start()
+        outs[k][REST : REST + 4] = jnp.full((4, 2, D), length, F32).astype(BF)
         pltpu.make_async_copy(
             new.at[:, :, lanes], outs[k].at[pl.ds((TABLE - MOST) * PAGE, NEW_DEV)], sem_r.at[k]
         ).start()
-    for j in range(MOST):
-        for y in range(KVH):
-            pltpu.make_async_copy(
-                pool.at[table[0, j], :, :, pl.ds(y * D, D)], mig.at[b_here, y, j], sem_m
-            ).start()
     for k in range(4):
-        pltpu.make_async_copy(outs[k], outs[k], sem_r.at[k]).wait()
-    pltpu.make_async_copy(mig, mig, sem_m).wait()
-
-
-def pack(table, ctx, page, dest, pool, new):
-    return pl.pallas_call(
-        pack_kernel,
-        in_specs=[HBM, VMEM, HBM, HBM, HBM, VMEM],
-        out_specs=[HBM] * 5,
-        out_shape=[jax.ShapeDtypeStruct((INST, KVH, MOST, PAGE, 2, D), BF)]
-        + [jax.ShapeDtypeStruct((REST, 2, D), BF)] * 4,
-        scratch_shapes=[pltpu.SMEM(a.shape, jnp.int32) for a in (table, ctx, page, dest)]
-        + [
-            pltpu.VMEM(pool.shape, BF),
-            pltpu.VMEM((KVH, PAGE, 2, D), BF),
-            pltpu.SemaphoreType.DMA((4,)),
-            pltpu.SemaphoreType.DMA,
-            pltpu.SemaphoreType.DMA,
-            pltpu.SemaphoreType.DMA((4,)),
-        ],
-        compiler_params=pltpu.CompilerParams(vmem_limit_bytes=60 << 20),
-        name="pack",
-    )(table, ctx, page, dest, pool, new)
-
-
-def append_kernel(page_in, after, source, new, target, page, pool, sem):
-    copy = pltpu.make_async_copy(source, pool, sem.at[0])
-    copy.start()
-    scalar = pltpu.make_async_copy(page_in, page, sem.at[1])
-    scalar.start()
-    scalar.wait()
-    copy.wait()
-    last = pltpu.make_async_copy(new, pool.at[page[0, 0], pl.ds(0, NEW_DEV)], sem.at[1])
+        moved = outs[k].at[pl.ds(0, REST)]
+        pltpu.make_async_copy(moved, moved, sem_r.at[k]).wait()
+    last = pltpu.make_async_copy(new, pool.at[page[0, 0], pl.ds(0, NEW_DEV)], sem.at[0])
     last.start()
     last.wait()
     copy = pltpu.make_async_copy(pool, target, sem.at[0])
@@ -150,21 +139,22 @@
     copy.wait()
 
 
-def append(page, after, pool, new):
-    return pl.pallas_call(
-        append_kernel,
-        in_specs=[HBM] * 4,
-        out_specs=HBM,
-        out_shape=jax.ShapeDtypeStruct(pool.shape, BF),
+def settle(table, ctx, page, after, pool, new):
+    return pl.pallas_call(
+        settle_kernel,
+        in_specs=[SMEM] * 3 + [HBM, HBM, VMEM],
+        out_specs=[VMEM] * 4 + [HBM],
+        out_shape=[jax.ShapeDtypeStruct((REST + 4, 2, D), BF)] * 4
+        + [jax.ShapeDtypeStruct(pool.shape, BF)],
         scratch_shapes=[
-            pltpu.SMEM((1, 1), jnp.int32),
             pltpu.VMEM(pool.shape, BF),
-            pltpu.SemaphoreType.DMA((2,)),
+            pltpu.SemaphoreType.DMA((1,)),
+            pltpu.SemaphoreType.DMA((4,)),
         ],
         compiler_params=pltpu.CompilerParams(vmem_limit_bytes=8 << 20),
         cost_estimate=cost(1),
-        name="append",
-    )(page, after, pool, new)
+        name="settle",
+    )(table, ctx, page, after, pool, new)
 
 
 def put(x, pick, kk, vt, at, marks=None):
@@ -186,19 +176,39 @@
     col = lax.broadcasted_iota(jnp.int32, (256, 128), 1)
     pick = (keys, (row == 2 * col + 1).astype(BF))
     vt[128:144, :] = jnp.ones((16, ROWS), BF)
+    sub = lax.broadcasted_iota(jnp.int32, (128, 128), 0)
+    lane = lax.broadcasted_iota(jnp.int32, (128, 128), 1)
+    b_here = here()[2]
+    live = [r[144:152].astype(F32)[0:1] for r in parts]
+    row = sub.astype(F32)
     for i in range(MIG_ROWS // 128):
-        put(mig[i], pick, kk, vt, slice(i * 128, i * 128 + 128))
+        source = lax.rem(b_here + 1 + (i >> 1), INST)
+        x = mig[2 * source + (i & 1)]
+        marks = None
+        if i >= MIG_ROWS // 128 - 2:
+            ctx = [live_of(live, 2 * (i & 1) + e) for e in range(2)]
+            dead = row >= jnp.where(sub < 64, ctx[0], ctx[1] + 64.0)
+            marks = jnp.where((lane == 0) & dead, BIG, 0.0)
+        put(x, pick, kk, vt, slice(i * 128, i * 128 + 128), marks)
     for i in range(2):
         x = jnp.concatenate([parts[2 * i][0:128], parts[2 * i + 1][0:128]], axis=0)
         at = MIG_ROWS + i * 128
-        put(x, pick, kk, vt, slice(at, at + 128))
+        dead = row >= jnp.where(sub < 64, live[2 * i] - 64.0, live[2 * i + 1])
+        marks = jnp.where((lane == 0) & dead, BIG, 0.0)
+        put(x, pick, kk, vt, slice(at, at + 128), marks)
     at = MIG_ROWS + OLD_ROWS
     x = jnp.concatenate([r[128:144] for r in parts] + [jnp.zeros((192, 128), BF)], axis=0)
-    sub = lax.broadcasted_iota(jnp.int32, (128, 128), 0)
-    lane = lax.broadcasted_iota(jnp.int32, (128, 128), 1)
     hot = jnp.where((lane == 1 + sub) & (sub < 32), 1.0, 0.0)
     marks = jnp.where((lane == 0) & (sub >= 32), BIG, hot)
     put(x, pick, kk, vt, slice(at, at + 128), marks)
+
+
+def live_of(live, y):
+    y_here = here()[1]
+    value = live[0]
+    for k in range(1, 4):
+        value = jnp.where(((y_here + 4 - k) & 3) == y, live[k], value)
+    return value
 
 
 def turn_kernel(q0, q2, pair, out):
@@ -229,21 +239,21 @@
     )(q, q2, pair)
 
 
-def attend(ks, outs, qt, kk, vt, s_ref):
-    units = [(i, t) for i in range(len(ks)) for t in range(len(SPANS) - 1)]
+def attend(ks, spans, outs, qt, kk, vt, s_ref):
+    units = [(i, t) for i in range(len(ks)) for t in range(len(spans) - 1)]
 
     def score(u):
         i, t = units[u]
-        rows = slice(SPANS[t], SPANS[t + 1])
-        size = SPANS[t + 1] - SPANS[t]
+        rows = slice(spans[t], spans[t + 1])
+        size = spans[t + 1] - spans[t]
         s_ref[u % 2, 0:size] = jnp.dot(kk[rows], qt[ks[i]], preferred_element_type=F32)
 
     score(0)
     for u, (i, t) in enumerate(units):
         if u + 1 < len(units):
             score(u + 1)
-        rows = slice(SPANS[t], SPANS[t + 1])
-        s = s_ref[u % 2, 0 : SPANS[t + 1] - SPANS[t]]
+        rows = slice(spans[t], spans[t + 1])
+        s = s_ref[u % 2, 0 : spans[t + 1] - spans[t]]
         top = jnp.max(s, axis=0, keepdims=True)
         p = jnp.exp2((s - top) * LOG_SCALE)
         high = p.astype(BF)
@@ -256,7 +266,7 @@
             both = jnp.maximum(best, top)
             sums = sums * jnp.exp2((best - both) * LOG_SCALE) + o * jnp.exp2((top - both) * LOG_SCALE)
             best = both
-        if t + 2 < len(SPANS):
+        if t + 2 < len(spans):
             continue
         total = sums[128:129]
         mean = sums[0:128] / total
@@ -273,11 +283,11 @@
 
 def first_kernel(k, qt, mig, r0, r1, r2, r3, out, kk, vt, s_ref):
     fill(mig, (r0, r1, r2, r3), kk, vt)
-    attend((k,), (out,), qt, kk, vt, s_ref)
+    attend((k,), NARROW, (out,), qt, kk, vt, s_ref)
 
 
 def more_kernel(ks, qt, kk, vt, *refs):
-    attend(ks, refs[-1 - len(ks) : -1], qt, kk, vt, refs[-1])
+    attend(ks, WIDE, refs[-1 - len(ks) : -1], qt, kk, vt, refs[-1])
 
 
 def cost(count):
@@ -287,7 +297,8 @@
 
 
 PART = jax.ShapeDtypeStruct((136, 512), F32)
-SCORES = pltpu.VMEM((2, max(b - a for a, b in zip(SPANS, SPANS[1:])), 512), F32)
+def scores(spans):
+    return pltpu.VMEM((2, max(b - a for a, b in zip(spans, spans[1:])), 512), F32)
 
 
 def first(k, qt, mig, parts):
@@ -300,7 +311,7 @@
             jax.ShapeDtypeStruct((ROWS, 256), BF),
             jax.ShapeDtypeStruct((144, ROWS), BF),
         ],
-        scratch_shapes=[SCORES],
+        scratch_shapes=[scores(NARROW)],
         compiler_params=pltpu.CompilerParams(vmem_limit_bytes=28 << 20),
         cost_estimate=cost(1),
         name="first",
@@ -314,7 +325,7 @@
         in_specs=[VMEM] * 3 + [HBM] * len(late),
         out_specs=[VMEM] * len(ks),
         out_shape=[PART] * len(ks),
-        scratch_shapes=[SCORES],
+        scratch_shapes=[scores(WIDE)],
         compiler_params=pltpu.CompilerParams(vmem_limit_bytes=28 << 20),
         cost_estimate=cost(len(ks)),
         name="more",
@@ -356,13 +367,14 @@
 def local(queries, new_kv, pool, page_table, ctx_len, move_page, move_dest, append_page):
     fresh = new_kv[0]
     q = queries[0]
-    mig, *parts = pack(page_table, ctx_len, move_page, move_dest, pool[0], fresh)
+    mig = pack(page_table, move_page, move_dest, pool[0])
+    after = mig
     mig = mig.reshape(INST * KVH, MOST * PAGE * 2, D)
     mig = lax.all_to_all(mig, ("ba", "y"), 0, 0, tiled=True)
-    parts = [r.reshape(REST * 2, D) for r in parts]
+    *parts, updated = settle(page_table, ctx_len, append_page, after, pool[0], fresh)
+    parts = [r.reshape((REST + 4) * 2, D) for r in parts]
     parts = [parts[0]] + [shift(parts[k], "y", k) for k in range(1, 4)]
     q2 = swap(q, 2)
-    updated = append(append_page, parts[0], pool[0], fresh)
     far, updated = lax.optimization_barrier((q2, updated))
     pair = swap(jnp.concatenate([q, far], axis=0), 1)
     qt = turn(q, q2, pair)

time: 48.1 us -> 46.6 us (0.969)
  Pallas kernels: 15.3 us -> 14.5 us
  waiting for transfers between devices: 6.93 us -> 6.17 us
    ppermute x5, waiting for transfers between devices: 5.06 us -> 4.18 us  [swap(): return lax.ppermute(value, 'x', [(i, i ^ k) for i in range(4)])]
    pallas_call x2, Pallas kernels: 4.4 us -> 3.7 us  [the longest x1 1.99 us: pack(): pl.pallas_call(pack_kernel, in_specs=[HBM] * 4, out_specs=HBM, out_shape=...]
  transfers between devices with their start and end apart: 9 -> 9, of which waited for: 6 -> 5; matrix products, arithmetic and copies ran while one was open for 0% -> 0% of each run, Pallas kernels for 18% -> 19%
where the time goes in v5:
time: 46.6 us; the launch traced here: 46.4 us
  starting transfers between devices  23.4 us (50%)
  Pallas kernels  14.5 us (31%)
  waiting for transfers between devices  6.17 us (13%)
  between operations  2.11 us (5%)
    ppermute x5, starting transfers between devices, swap(): return lax.ppermute(value, 'x', [(i, i ^ k) for i in range(4)])  8.95 us
    all_to_all x1, starting transfers between devices, local(): mig = lax.all_to_all(mig, ('ba', 'y'), 0, 0, tiled=True)  8.62 us
    pallas_call x2, Pallas kernels, more(): pl.pallas_call(functools.partial(more_kernel, ks), in_specs=[VMEM] * 3 +...  6.83 us
    ppermute x3, starting transfers between devices, shift(): return lax.ppermute(value, axis, [(i, (i + k) % 4) for i in range(4)])  5.8 us
    ppermute x5, waiting for transfers between devices, swap(): return lax.ppermute(value, 'x', [(i, i ^ k) for i in range(4)])  4.18 us
    pallas_call x1, Pallas kernels, first(): pl.pallas_call(functools.partial(first_kernel, k), in_specs=[VMEM] * 6, o...  2.89 us
    pallas_call x1, Pallas kernels, pack(): pl.pallas_call(pack_kernel, in_specs=[HBM] * 4, out_specs=HBM, out_shape=...  1.99 us
    ppermute x3, waiting for transfers between devices, shift(): return lax.ppermute(value, axis, [(i, (i + k) % 4) for i in range(4)])  1.99 us
  transfers between devices with their start and end apart: 9, of which 5 were waited for; matrix products, arithmetic and copies ran while one was open for 0% of the time, Pallas kernels for 19%

profile of v5, /device:TPU:0, one launch (start us, length us, event | category | flops | bytes accessed | tf_op | source)
XLA Modules:
  0.0 46.4 jit_solution(14576514248472421600)
XLA Ops:
  0.6 2.0 %pack.1.after = bf16[8,4,2,32,2,128]{5,4,3,2,1,0:T(2,128)(2,1)} custom-call(s32[1,4]{1,0:T(1,128)} %table.1, s32[1,7]{1,0:T(1,128)} %page_in.1, s32[1,7]{1,0:T(1,128)} %dest_in.1, bf16[12,32,2,512]{3,2,1,0:T(2,128)(2,1)} %bitcast.15), custom_call_target="tpu_custom_call" | custom-call | tf_op jit(solution)/shard_map/pack/pallas_call | solution.py:92
  2.6 0.0 copy-start.2
  2.6 0.0 copy-start.1
  2.7 0.0 copy-start.3
  2.7 8.6 %all-to-all-start = ((bf16[32,128,128]{2,1,0:T(8,128)(2,1)}), bf16[32,128,128]{2,1,0:T(8,128)(2,1)S(1)}, u32[]{:S(2)}, u32[]{:S(2)}) async-start(bf16[32,128,128]{2,1,0:T(8,128)(2,1)} %bitcast.13), calls=%async_computation | async-start | bytes 2097152 | tf_op jit(solution)/shard_map/all_to_all | solution.py:373
  11.3 3.1 %collective-permute-start = (bf16[128,512]{1,0:T(8,128)(2,1)S(1)}, bf16[128,512]{1,0:T(8,128)(2,1)S(1)}, u32[]{:S(2)}, u32[]{:S(2)}) collective-permute-start(bf16[128,512]{1,0:T(8,128)(2,1)S(1)} %bitcast.17), channel_id=1, source_target_pairs={{0,16},{8,24},{16,0},{24,8},{1,17},{9,25},{17,1},{25,9},{2,18},{10... | collective-permute-start | bytes 393224 | tf_op jit(solution)/shard_map/ppermute | solution.py:364
  15.8 1.7 %settle.1 = (bf16[76,2,128]{2,1,0:T(2,128)(2,1)S(1)}, bf16[76,2,128]{2,1,0:T(2,128)(2,1)S(1)}, bf16[76,2,128]{2,1,0:T(2,128)(2,1)S(1)}, bf16[76,2,128]{2,1,0:T(2,128)(2,1)S(1)}, bf16[12,32,2,512]{3,2,1,0:T(2,128)(2,1)}) custom-call(s32[1,4]{1,0:T(1,128)S(1)} %copy-done.4, s32[1,1]{1,0:T(1,128)S(6)} %copy.10.ctx, s32[1,1]{1,0:T(1,128)S(6)} %copy.11.page, ...), custom_call_target="tpu_custom_call" | custom-call | flops 1048576 | bytes 65536 | tf_op jit(solution)/shard_map/settle/pallas_call | solution.py:143
  17.5 1.1 %collective-permute-done.q2 = bf16[128,512]{1,0:T(8,128)(2,1)S(1)} collective-permute-done((bf16[128,512]{1,0:T(8,128)(2,1)S(1)}, bf16[128,512]{1,0:T(8,128)(2,1)S(1)}, u32[]{:S(2)}, u32[]{:S(2)}) %collective-permute-start) | collective-permute-done | bytes 131104 | tf_op jit(solution)/shard_map/ppermute | solution.py:364
  18.6 1.5 %collective-permute-start.1 = (bf16[256,512]{1,0:T(8,128)(2,1)S(1)}, bf16[256,512]{1,0:T(8,128)(2,1)S(1)}, u32[]{:S(2)}, u32[]{:S(2)}) collective-permute-start(bf16[256,512]{1,0:T(8,128)(2,1)S(1)} %pad_maximum_fusion), channel_id=1, source_target_pairs={{0,8},{8,0},{16,24},{24,16},{1,9},{9,1},{17,25},{25,17},{2,10},{10... | collective-permute-start | bytes 786440 | tf_op jit(solution)/shard_map/ppermute | solution.py:364
  20.1 1.7 %collective-permute-start.2 = (bf16[152,128]{1,0:T(8,128)(2,1)S(1)}, bf16[152,128]{1,0:T(8,128)(2,1)S(1)}, u32[]{:S(2)}, u32[]{:S(2)}) collective-permute-start(bf16[152,128]{1,0:T(8,128)(2,1)S(1)} %bitcast.24), channel_id=1, source_target_pairs={{0,32},{32,64},{64,96},{96,0},{1,33},{33,65},{65,97},{97,1},{2,34}... | collective-permute-start | bytes 116744 | tf_op jit(solution)/shard_map/ppermute | solution.py:360
  21.8 2.7 %collective-permute-start.3 = (bf16[152,128]{1,0:T(8,128)(2,1)S(1)}, bf16[152,128]{1,0:T(8,128)(2,1)S(1)}, u32[]{:S(2)}, u32[]{:S(2)}) collective-permute-start(bf16[152,128]{1,0:T(8,128)(2,1)S(1)} %bitcast.23), channel_id=1, source_target_pairs={{0,64},{32,96},{64,0},{96,32},{1,65},{33,97},{65,1},{97,33},{2,66}... | collective-permute-start | bytes 116744 | tf_op jit(solution)/shard_map/ppermute | solution.py:360
  24.5 1.5 %collective-permute-start.4 = (bf16[152,128]{1,0:T(8,128)(2,1)S(1)}, bf16[152,128]{1,0:T(8,128)(2,1)S(1)}, u32[]{:S(2)}, u32[]{:S(2)}) collective-permute-start(bf16[152,128]{1,0:T(8,128)(2,1)S(1)} %bitcast.22), channel_id=1, source_target_pairs={{0,96},{32,0},{64,32},{96,64},{1,97},{33,1},{65,33},{97,65},{2,98}... | collective-permute-start | bytes 116744 | tf_op jit(solution)/shard_map/ppermute | solution.py:360
  25.9 0.4 collective-permute-done.1.pair
  26.4 0.3 turn.1.qt
  26.6 1.0 %collective-permute-done.2.r1 = bf16[152,128]{1,0:T(8,128)(2,1)S(1)} collective-permute-done((bf16[152,128]{1,0:T(8,128)(2,1)S(1)}, bf16[152,128]{1,0:T(8,128)(2,1)S(1)}, u32[]{:S(2)}, u32[]{:S(2)}) %collective-permute-start.2) | collective-permute-done | bytes 38944 | tf_op jit(solution)/shard_map/ppermute | solution.py:360
  27.7 1.0 %collective-permute-done.3.r2 = bf16[152,128]{1,0:T(8,128)(2,1)S(1)} collective-permute-done((bf16[152,128]{1,0:T(8,128)(2,1)S(1)}, bf16[152,128]{1,0:T(8,128)(2,1)S(1)}, u32[]{:S(2)}, u32[]{:S(2)}) %collective-permute-start.3) | collective-permute-done | bytes 38944 | tf_op jit(solution)/shard_map/ppermute | solution.py:360
  28.6 2.9 %first.1 = (f32[136,512]{1,0:T(8,128)S(1)}, bf16[2432,256]{1,0:T(8,128)(2,1)S(1)}, bf16[144,2432]{1,0:T(8,128)(2,1)S(1)}) custom-call(bf16[4,256,512]{2,1,0:T(8,128)(2,1)S(1)} %turn.1.qt, bf16[16,256,128]{2,1,0:T(8,128)(2,1)S(1)} %bitcast.14, bf16[152,128]{1,0:T(8,128)(2,1)S(1)} %bitcast.20, bf16[152,128]{1,0:T(8,128)(2,1)S(1)} %collective-permute-done.2.r1, ...), custom_call_target="tpu_custom_call" | custom-call | flops 1048576 | bytes 65536 | tf_op jit(solution)/shard_map/first/pallas_call | solution.py:305
  31.5 3.1 %collective-permute-start.5 = (f16[136,512]{1,0:T(8,128)(2,1)S(1)}, f16[136,512]{1,0:T(8,128)(2,1)S(1)}, u32[]{:S(2)}, u32[]{:S(2)}) collective-permute-start(f16[136,512]{1,0:T(8,128)(2,1)S(1)} %convert_element_type.15), channel_id=1, source_target_pairs={{0,16},{8,24},{16,0},{24,8},{1,17},{9,25},{17,1},{25,9},{2,18},{10... | collective-permute-start | bytes 417800 | tf_op jit(solution)/shard_map/ppermute | solution.py:364
  34.6 4.4 %more.3 = (f32[136,512]{1,0:T(8,128)S(1)}, f32[136,512]{1,0:T(8,128)S(1)}) custom-call(bf16[4,256,512]{2,1,0:T(8,128)(2,1)S(1)} %turn.1.qt, bf16[2432,256]{1,0:T(8,128)(2,1)S(1)} %get-tuple-element.20.kk, bf16[144,2432]{1,0:T(8,128)(2,1)S(1)} %get-tuple-element.21.vt), custom_call_target="tpu_custom_call" | custom-call | flops 2097152 | bytes 131072 | tf_op jit(solution)/shard_map/more/pallas_call | solution.py:323
  39.1 1.2 %collective-permute-start.7 = (f16[136,512]{1,0:T(8,128)(2,1)S(1)}, f16[136,512]{1,0:T(8,128)(2,1)S(1)}, u32[]{:S(2)}, u32[]{:S(2)}) collective-permute-start(f16[136,512]{1,0:T(8,128)(2,1)S(1)} %convert_element_type.18), channel_id=1, source_target_pairs={{0,24},{8,16},{16,8},{24,0},{1,25},{9,17},{17,9},{25,1},{2,26},{10... | collective-permute-start | bytes 417800 | tf_op jit(solution)/shard_map/ppermute | solution.py:364
  40.3 2.4 %more.2.g0 = f32[136,512]{1,0:T(8,128)S(1)} custom-call(bf16[4,256,512]{2,1,0:T(8,128)(2,1)S(1)} %turn.1.qt, bf16[2432,256]{1,0:T(8,128)(2,1)S(1)} %get-tuple-element.20.kk, bf16[144,2432]{1,0:T(8,128)(2,1)S(1)} %get-tuple-element.21.vt, f32[136,512]{1,0:T(8,128)S(1)} %convert_element_type.16.refs_0_.g2), custom_call_target="tpu_custom_call" | custom-call | flops 1048576 | bytes 65536 | tf_op jit(solution)/shard_map/more/pallas_call | solution.py:323
  42.8 2.7 %collective-permute-done.7 = f16[136,512]{1,0:T(8,128)(2,1)S(1)} collective-permute-done((f16[136,512]{1,0:T(8,128)(2,1)S(1)}, f16[136,512]{1,0:T(8,128)(2,1)S(1)}, u32[]{:S(2)}, u32[]{:S(2)}) %collective-permute-start.7) | collective-permute-done | bytes 139296 | tf_op jit(solution)/shard_map/ppermute | solution.py:364
  45.5 0.1 maximum_convert_fusion.g
  45.5 0.8 %combine.1 = bf16[128,512]{1,0:T(8,128)(2,1)} custom-call(f32[136,512]{1,0:T(8,128)S(1)} %more.2.g0, f32[136,512]{1,0:T(8,128)S(1)} %convert_element_type.16.refs_0_.g2, f32[2,136,512]{2,1,0:T(8,128)S(1)} %maximum_convert_fusion.g), custom_call_target="tpu_custom_call" | custom-call | tf_op jit(solution)/shard_map/combine/pallas_call | solution.py:349
  (17 shorter events, 0.1 us)
Async XLA Ops:
  2.6 8.7 %copy-start.2 = (bf16[1,128,512]{2,1,0:T(8,128)(2,1)S(1)}, bf16[1,128,512]{2,1,0:T(8,128)(2,1)}, u32[]{:S(2)}) copy-start(bf16[1,128,512]{2,1,0:T(8,128)(2,1)} %param.8) | copy-start | bytes 393220
  2.6 13.1 %copy-start = (bf16[8,4,2,32,2,128]{5,4,3,2,1,0:T(2,128)(2,1)S(1)}, bf16[8,4,2,32,2,128]{5,4,3,2,1,0:T(2,128)(2,1)}, u32[]{:S(2)}) copy-start(bf16[8,4,2,32,2,128]{5,4,3,2,1,0:T(2,128)(2,1)} %pack.1.after) | copy-start | bytes 3145732
  2.6 13.1 %copy-start.1 = (bf16[1,12,32,2,512]{4,3,2,1,0:T(2,128)(2,1)S(1)}, bf16[1,12,32,2,512]{4,3,2,1,0:T(2,128)(2,1)}, u32[]{:S(2)}) copy-start(bf16[1,12,32,2,512]{4,3,2,1,0:T(2,128)(2,1)} %param.10) | copy-start | bytes 2359300
  2.7 13.1 %copy-start.3 = (bf16[1,8,2,512]{3,2,1,0:T(2,128)(2,1)S(1)}, bf16[1,8,2,512]{3,2,1,0:T(2,128)(2,1)}, u32[]{:S(2)}) copy-start(bf16[1,8,2,512]{3,2,1,0:T(2,128)(2,1)} %param.9) | copy-start | bytes 49156
  2.7 13.1 %copy-start.4 = (s32[1,4]{1,0:T(1,128)S(1)}, s32[1,4]{1,0:T(1,128)}, u32[]{:S(2)}) copy-start(s32[1,4]{1,0:T(1,128)} %table.1) | copy-start | bytes 52
  2.7 25.9 %all-to-all-start = ((bf16[32,128,128]{2,1,0:T(8,128)(2,1)}), bf16[32,128,128]{2,1,0:T(8,128)(2,1)S(1)}, u32[]{:S(2)}, u32[]{:S(2)}) async-start(bf16[32,128,128]{2,1,0:T(8,128)(2,1)} %bitcast.13), calls=%async_computation | async-start | bytes 2097152 | tf_op jit(solution)/shard_map/all_to_all | solution.py:373
  11.3 7.3 %collective-permute-start = (bf16[128,512]{1,0:T(8,128)(2,1)S(1)}, bf16[128,512]{1,0:T(8,128)(2,1)S(1)}, u32[]{:S(2)}, u32[]{:S(2)}) collective-permute-start(bf16[128,512]{1,0:T(8,128)(2,1)S(1)} %bitcast.17), channel_id=1, source_target_pairs={{0,16},{8,24},{16,0},{24,8},{1,17},{9,25},{17,1},{25,9},{2,18},{10... | collective-permute-start | bytes 393224 | tf_op jit(solution)/shard_map/ppermute | solution.py:364
  18.6 7.8 %collective-permute-start.1 = (bf16[256,512]{1,0:T(8,128)(2,1)S(1)}, bf16[256,512]{1,0:T(8,128)(2,1)S(1)}, u32[]{:S(2)}, u32[]{:S(2)}) collective-permute-start(bf16[256,512]{1,0:T(8,128)(2,1)S(1)} %pad_maximum_fusion), channel_id=1, source_target_pairs={{0,8},{8,0},{16,24},{24,16},{1,9},{9,1},{17,25},{25,17},{2,10},{10... | collective-permute-start | bytes 786440 | tf_op jit(solution)/shard_map/ppermute | solution.py:364
  20.1 7.5 %collective-permute-start.2 = (bf16[152,128]{1,0:T(8,128)(2,1)S(1)}, bf16[152,128]{1,0:T(8,128)(2,1)S(1)}, u32[]{:S(2)}, u32[]{:S(2)}) collective-permute-start(bf16[152,128]{1,0:T(8,128)(2,1)S(1)} %bitcast.24), channel_id=1, source_target_pairs={{0,32},{32,64},{64,96},{96,0},{1,33},{33,65},{65,97},{97,1},{2,34}... | collective-permute-start | bytes 116744 | tf_op jit(solution)/shard_map/ppermute | solution.py:360
  21.8 6.8 %collective-permute-start.3 = (bf16[152,128]{1,0:T(8,128)(2,1)S(1)}, bf16[152,128]{1,0:T(8,128)(2,1)S(1)}, u32[]{:S(2)}, u32[]{:S(2)}) collective-permute-start(bf16[152,128]{1,0:T(8,128)(2,1)S(1)} %bitcast.23), channel_id=1, source_target_pairs={{0,64},{32,96},{64,0},{96,32},{1,65},{33,97},{65,1},{97,33},{2,66}... | collective-permute-start | bytes 116744 | tf_op jit(solution)/shard_map/ppermute | solution.py:360
  24.5 4.1 %collective-permute-start.4 = (bf16[152,128]{1,0:T(8,128)(2,1)S(1)}, bf16[152,128]{1,0:T(8,128)(2,1)S(1)}, u32[]{:S(2)}, u32[]{:S(2)}) collective-permute-start(bf16[152,128]{1,0:T(8,128)(2,1)S(1)} %bitcast.22), channel_id=1, source_target_pairs={{0,96},{32,0},{64,32},{96,64},{1,97},{33,1},{65,33},{97,65},{2,98}... | collective-permute-start | bytes 116744 | tf_op jit(solution)/shard_map/ppermute | solution.py:360
  31.5 8.8 %collective-permute-start.5 = (f16[136,512]{1,0:T(8,128)(2,1)S(1)}, f16[136,512]{1,0:T(8,128)(2,1)S(1)}, u32[]{:S(2)}, u32[]{:S(2)}) collective-permute-start(f16[136,512]{1,0:T(8,128)(2,1)S(1)} %convert_element_type.15), channel_id=1, source_target_pairs={{0,16},{8,24},{16,0},{24,8},{1,17},{9,25},{17,1},{25,9},{2,18},{10... | collective-permute-start | bytes 417800 | tf_op jit(solution)/shard_map/ppermute | solution.py:364
  39.1 6.3 %collective-permute-start.7 = (f16[136,512]{1,0:T(8,128)(2,1)S(1)}, f16[136,512]{1,0:T(8,128)(2,1)S(1)}, u32[]{:S(2)}, u32[]{:S(2)}) collective-permute-start(f16[136,512]{1,0:T(8,128)(2,1)S(1)} %convert_element_type.18), channel_id=1, source_target_pairs={{0,24},{8,16},{16,8},{24,0},{1,25},{9,17},{17,9},{25,1},{2,26},{10... | collective-permute-start | bytes 417800 | tf_op jit(solution)/shard_map/ppermute | solution.py:364
  40.3 5.1 %collective-permute-start.6 = (f16[136,512]{1,0:T(8,128)(2,1)S(1)}, f16[136,512]{1,0:T(8,128)(2,1)S(1)}, u32[]{:S(2)}, u32[]{:S(2)}) collective-permute-start(f16[136,512]{1,0:T(8,128)(2,1)S(1)} %convert_element_type.17), channel_id=1, source_target_pairs={{0,8},{8,0},{16,24},{24,16},{1,9},{9,1},{17,25},{25,17},{2,10},{10... | collective-permute-start | bytes 417800 | tf_op jit(solution)/shard_map/ppermute | solution.py:364

commit v6 on v5

--- a/solution.py
+++ b/solution.py
@@ -30,8 +30,8 @@
 MIG_ROWS = INST * KVH * MOST * PAGE
 OLD_ROWS = (TABLE - MOST) * PAGE * KVH
 ROWS = MIG_ROWS + OLD_ROWS + 128
-WIDE = (0, 1280, ROWS)
-NARROW = (0, 640, 1280, 1920, ROWS)
+SPANS = (0, 1280, ROWS)
+SAMPLE = slice(MIG_ROWS - 128, MIG_ROWS)
 
 SMEM = pl.BlockSpec(memory_space=pltpu.SMEM)
 HBM = pl.BlockSpec(memory_space=pltpu.HBM)
@@ -49,8 +49,15 @@
 def pack_kernel(
     table_in, page_in, dest_in, source, mig, table, page, dest, pool, dead, sem_s, sem_p, sem_m
 ):
-    fetch = pltpu.make_async_copy(source, pool, sem_p)
-    fetch.start()
+    third = source.shape[0] // 3
+    fetch = [
+        pltpu.make_async_copy(
+            source.at[pl.ds(i * third, third)], pool.at[pl.ds(i * third, third)], sem_p.at[i]
+        )
+        for i in range(3)
+    ]
+    for copy in fetch:
+        copy.start()
     scalars = [
         pltpu.make_async_copy(a, b, sem_s.at[i])
         for i, (a, b) in enumerate(((table_in, table), (page_in, page), (dest_in, dest)))
@@ -71,7 +78,8 @@
             def _():
                 pltpu.make_async_copy(dead, mig.at[d, :, s], sem_m).start()
 
-    fetch.wait()
+    for copy in fetch:
+        copy.wait()
     for m in range(MOVES):
         rank = jnp.int32(0)
         for e in range(m):
@@ -99,7 +107,7 @@
             pltpu.VMEM(pool.shape, BF),
             pltpu.VMEM((KVH, PAGE, 2, D), BF),
             pltpu.SemaphoreType.DMA((3,)),
-            pltpu.SemaphoreType.DMA,
+            pltpu.SemaphoreType.DMA((3,)),
             pltpu.SemaphoreType.DMA,
         ],
         compiler_params=pltpu.CompilerParams(vmem_limit_bytes=60 << 20),
@@ -239,55 +247,68 @@
     )(q, q2, pair)
 
 
-def attend(ks, spans, outs, qt, kk, vt, s_ref):
-    units = [(i, t) for i in range(len(ks)) for t in range(len(spans) - 1)]
-
-    def score(u):
-        i, t = units[u]
-        rows = slice(spans[t], spans[t + 1])
-        size = spans[t + 1] - spans[t]
-        s_ref[u % 2, 0:size] = jnp.dot(kk[rows], qt[ks[i]], preferred_element_type=F32)
-
-    score(0)
-    for u, (i, t) in enumerate(units):
-        if u + 1 < len(units):
-            score(u + 1)
-        rows = slice(spans[t], spans[t + 1])
-        s = s_ref[u % 2, 0 : spans[t + 1] - spans[t]]
+def emit(out, sums, top):
+    total = sums[128:129]
+    mean = sums[0:128] / total
+    most = jnp.maximum(jnp.max(jnp.abs(mean), axis=0, keepdims=True), 1e-30)
+    den = jnp.log2(total) + top * LOG_SCALE
+    num = den + jnp.log2(most)
+    out[0:128] = mean / most
+    rows = []
+    for x in (den, num):
+        high = jnp.floor(x * 2.0 + 0.5) * 0.5
+        rows += [high, x - high]
+    out[128:136] = jnp.concatenate(rows + [jnp.zeros((4, 512), F32)], axis=0)
+
+
+def weigh(s, top, values):
+    p = jnp.exp2((s - top) * LOG_SCALE)
+    high = p.astype(BF)
+    low = (p - high.astype(F32)).astype(BF)
+    o = jnp.dot(values, high, preferred_element_type=F32)
+    return o + jnp.dot(values, low, preferred_element_type=F32)
+
+
+def exact(q, out, kk, vt, s_ref):
+    best = sums = None
+    for start, stop in zip(SPANS, SPANS[1:]):
+        rows = slice(start, stop)
+        s_ref[0 : stop - start] = jnp.dot(kk[rows], q, preferred_element_type=F32)
+        s = s_ref[0 : stop - start]
         top = jnp.max(s, axis=0, keepdims=True)
-        p = jnp.exp2((s - top) * LOG_SCALE)
-        high = p.astype(BF)
-        low = (p - high.astype(F32)).astype(BF)
-        o = jnp.dot(vt[:, rows], high, preferred_element_type=F32)
-        o += jnp.dot(vt[:, rows], low, preferred_element_type=F32)
-        if t == 0:
+        o = weigh(s, top, vt[:, rows])
+        if best is None:
             best, sums = top, o
         else:
             both = jnp.maximum(best, top)
-            sums = sums * jnp.exp2((best - both) * LOG_SCALE) + o * jnp.exp2((top - both) * LOG_SCALE)
+            old = jnp.exp2((best - both) * LOG_SCALE)
+            sums = sums * old + o * jnp.exp2((top - both) * LOG_SCALE)
             best = both
-        if t + 2 < len(spans):
-            continue
-        total = sums[128:129]
-        mean = sums[0:128] / total
-        most = jnp.maximum(jnp.max(jnp.abs(mean), axis=0, keepdims=True), 1e-30)
-        den = jnp.log2(total) + best * LOG_SCALE
-        num = den + jnp.log2(most)
-        outs[i][0:128] = mean / most
-        rows = []
-        for x in (den, num):
-            high = jnp.floor(x * 2.0 + 0.5) * 0.5
-            rows += [high, x - high]
-        outs[i][128:136] = jnp.concatenate(rows + [jnp.zeros((4, 512), F32)], axis=0)
+    emit(out, sums, best)
+
+
+def attend(ks, outs, qt, kk, vt, s_ref):
+    bad = []
+    for k, out in zip(ks, outs):
+        q = qt[k]
+        top = jnp.max(jnp.dot(kk[SAMPLE], q, preferred_element_type=F32), axis=0, keepdims=True)
+        sums = weigh(jnp.dot(kk[...], q, preferred_element_type=F32), top, vt[...])
+        emit(out, sums, top)
+        bad.append(jnp.max(jnp.where(sums[128:129] < 1e36, 0.0, 1.0)) > 0.5)
+    for k, out, wrong in zip(ks, outs, bad):
+
+        @pl.when(wrong)
+        def _():
+            exact(qt[k], out, kk, vt, s_ref)
 
 
 def first_kernel(k, qt, mig, r0, r1, r2, r3, out, kk, vt, s_ref):
     fill(mig, (r0, r1, r2, r3), kk, vt)
-    attend((k,), NARROW, (out,), qt, kk, vt, s_ref)
+    attend((k,), (out,), qt, kk, vt, s_ref)
 
 
 def more_kernel(ks, qt, kk, vt, *refs):
-    attend(ks, WIDE, refs[-1 - len(ks) : -1], qt, kk, vt, refs[-1])
+    attend(ks, refs[-1 - len(ks) : -1], qt, kk, vt, refs[-1])
 
 
 def cost(count):
@@ -297,8 +318,7 @@
 
 
 PART = jax.ShapeDtypeStruct((136, 512), F32)
-def scores(spans):
-    return pltpu.VMEM((2, max(b - a for a, b in zip(spans, spans[1:])), 512), F32)
+SCORES = pltpu.VMEM((max(b - a for a, b in zip(SPANS, SPANS[1:])), 512), F32)
 
 
 def first(k, qt, mig, parts):
@@ -311,7 +331,7 @@
             jax.ShapeDtypeStruct((ROWS, 256), BF),
             jax.ShapeDtypeStruct((144, ROWS), BF),
         ],
-        scratch_shapes=[scores(NARROW)],
+        scratch_shapes=[SCORES],
         compiler_params=pltpu.CompilerParams(vmem_limit_bytes=28 << 20),
         cost_estimate=cost(1),
         name="first",
@@ -325,7 +345,7 @@
         in_specs=[VMEM] * 3 + [HBM] * len(late),
         out_specs=[VMEM] * len(ks),
         out_shape=[PART] * len(ks),
-        scratch_shapes=[scores(WIDE)],
+        scratch_shapes=[SCORES],
         compiler_params=pltpu.CompilerParams(vmem_limit_bytes=28 << 20),
         cost_estimate=cost(len(ks)),
         name="more",
@@ -373,10 +393,11 @@
     mig = lax.all_to_all(mig, ("ba", "y"), 0, 0, tiled=True)
     *parts, updated = settle(page_table, ctx_len, append_page, after, pool[0], fresh)
     parts = [r.reshape((REST + 4) * 2, D) for r in parts]
-    parts = [parts[0]] + [shift(parts[k], "y", k) for k in range(1, 4)]
+    far = shift(parts[2], "y", 2)
+    parts = [parts[0], shift(parts[1], "y", 1), far, shift(parts[3], "y", 3)]
     q2 = swap(q, 2)
-    far, updated = lax.optimization_barrier((q2, updated))
-    pair = swap(jnp.concatenate([q, far], axis=0), 1)
+    q2, updated = lax.optimization_barrier((q2, updated))
+    pair = swap(jnp.concatenate([q, q2], axis=0), 1)
     qt = turn(q, q2, pair)
     out2, kk, vt = first(2, qt, mig.reshape(MIG_ROWS // 128, 256, D), parts)
     got2 = swap(out2.astype(F16), 2).astype(F32)

time: 46.6 us -> 54.1 us (1.16)
  starting transfers between devices: 23.4 us -> 31.7 us
  Pallas kernels: 14.5 us -> 13.5 us
    ppermute x5, starting transfers between devices: 8.95 us -> 17.4 us  [swap(): return lax.ppermute(value, 'x', [(i, i ^ k) for i in range(4)])]
    pallas_call x2, Pallas kernels: 6.83 us -> 5.97 us  [more(): pl.pallas_call(functools.partial(more_kernel, ks), in_specs=[VMEM] * 3 +...]
  transfers between devices with their start and end apart: 9 -> 9, of which waited for: 5 -> 6; matrix products, arithmetic and copies ran while one was open for 0% -> 0% of each run, Pallas kernels for 19% -> 15%
where the time goes in v6:
time: 54.1 us; the launch traced here: 54 us
  starting transfers between devices  31.7 us (59%)
  Pallas kernels  13.5 us (25%)
  waiting for transfers between devices  6.48 us (12%)
  between operations  2.11 us (4%)
    ppermute x5, starting transfers between devices, swap(): return lax.ppermute(value, 'x', [(i, i ^ k) for i in range(4)])  17.4 us
    all_to_all x1, starting transfers between devices, local(): mig = lax.all_to_all(mig, ('ba', 'y'), 0, 0, tiled=True)  8.54 us
    pallas_call x2, Pallas kernels, more(): pl.pallas_call(functools.partial(more_kernel, ks), in_specs=[VMEM] * 3 +...  5.97 us
    ppermute x3, starting transfers between devices, shift(): return lax.ppermute(value, axis, [(i, (i + k) % 4) for i in range(4)])  5.8 us
    ppermute x5, waiting for transfers between devices, swap(): return lax.ppermute(value, 'x', [(i, i ^ k) for i in range(4)])  4.49 us
    pallas_call x1, Pallas kernels, first(): pl.pallas_call(functools.partial(first_kernel, k), in_specs=[VMEM] * 6, o...  2.69 us
    pallas_call x1, Pallas kernels, pack(): pl.pallas_call(pack_kernel, in_specs=[HBM] * 4, out_specs=HBM, out_shape=...  2.03 us
    ppermute x3, waiting for transfers between devices, shift(): return lax.ppermute(value, axis, [(i, (i + k) % 4) for i in range(4)])  1.99 us
  transfers between devices with their start and end apart: 9, of which 6 were waited for; matrix products, arithmetic and copies ran while one was open for 0% of the time, Pallas kernels for 15%

profile of v6, /device:TPU:0, one launch (start us, length us, event | category | flops | bytes accessed | tf_op | source)
XLA Modules:
  0.0 54.0 jit_solution(4624026806918350706)
XLA Ops:
  0.6 2.0 %pack.1.after = bf16[8,4,2,32,2,128]{5,4,3,2,1,0:T(2,128)(2,1)} custom-call(s32[1,4]{1,0:T(1,128)} %table.1, s32[1,7]{1,0:T(1,128)} %page_in.1, s32[1,7]{1,0:T(1,128)} %dest_in.1, bf16[12,32,2,512]{3,2,1,0:T(2,128)(2,1)} %bitcast.15), custom_call_target="tpu_custom_call" | custom-call | tf_op jit(solution)/shard_map/pack/pallas_call | solution.py:100
  2.7 0.0 copy-start.2
  2.7 0.0 copy-start.1
  2.7 8.5 %all-to-all-start = ((bf16[32,128,128]{2,1,0:T(8,128)(2,1)}), bf16[32,128,128]{2,1,0:T(8,128)(2,1)S(1)}, u32[]{:S(2)}, u32[]{:S(2)}) async-start(bf16[32,128,128]{2,1,0:T(8,128)(2,1)} %bitcast.13), calls=%async_computation | async-start | bytes 2097152 | tf_op jit(solution)/shard_map/all_to_all | solution.py:393
  11.3 3.1 %collective-permute-start = (bf16[128,512]{1,0:T(8,128)(2,1)S(1)}, bf16[128,512]{1,0:T(8,128)(2,1)S(1)}, u32[]{:S(2)}, u32[]{:S(2)}) collective-permute-start(bf16[128,512]{1,0:T(8,128)(2,1)S(1)} %bitcast.17), channel_id=1, source_target_pairs={{0,16},{8,24},{16,0},{24,8},{1,17},{9,25},{17,1},{25,9},{2,18},{10... | collective-permute-start | bytes 393224 | tf_op jit(solution)/shard_map/ppermute | solution.py:384
  15.7 1.7 %settle.1 = (bf16[76,2,128]{2,1,0:T(2,128)(2,1)S(1)}, bf16[76,2,128]{2,1,0:T(2,128)(2,1)S(1)}, bf16[76,2,128]{2,1,0:T(2,128)(2,1)S(1)}, bf16[76,2,128]{2,1,0:T(2,128)(2,1)S(1)}, bf16[12,32,2,512]{3,2,1,0:T(2,128)(2,1)}) custom-call(s32[1,4]{1,0:T(1,128)S(1)} %copy-done.4, s32[1,1]{1,0:T(1,128)S(6)} %copy.10.ctx, s32[1,1]{1,0:T(1,128)S(6)} %copy.11.page, ...), custom_call_target="tpu_custom_call" | custom-call | flops 1048576 | bytes 65536 | tf_op jit(solution)/shard_map/settle/pallas_call | solution.py:151
  17.4 1.1 %collective-permute-done.q2 = bf16[128,512]{1,0:T(8,128)(2,1)S(1)} collective-permute-done((bf16[128,512]{1,0:T(8,128)(2,1)S(1)}, bf16[128,512]{1,0:T(8,128)(2,1)S(1)}, u32[]{:S(2)}, u32[]{:S(2)}) %collective-permute-start) | collective-permute-done | bytes 131104 | tf_op jit(solution)/shard_map/ppermute | solution.py:384
  18.6 1.6 %collective-permute-start.1 = (bf16[256,512]{1,0:T(8,128)(2,1)S(1)}, bf16[256,512]{1,0:T(8,128)(2,1)S(1)}, u32[]{:S(2)}, u32[]{:S(2)}) collective-permute-start(bf16[256,512]{1,0:T(8,128)(2,1)S(1)} %pad_maximum_fusion), channel_id=1, source_target_pairs={{0,8},{8,0},{16,24},{24,16},{1,9},{9,1},{17,25},{25,17},{2,10},{10... | collective-permute-start | bytes 786440 | tf_op jit(solution)/shard_map/ppermute | solution.py:384
  20.1 1.7 %collective-permute-start.2 = (bf16[152,128]{1,0:T(8,128)(2,1)S(1)}, bf16[152,128]{1,0:T(8,128)(2,1)S(1)}, u32[]{:S(2)}, u32[]{:S(2)}) collective-permute-start(bf16[152,128]{1,0:T(8,128)(2,1)S(1)} %bitcast.24), channel_id=1, source_target_pairs={{0,32},{32,64},{64,96},{96,0},{1,33},{33,65},{65,97},{97,1},{2,34}... | collective-permute-start | bytes 116744 | tf_op jit(solution)/shard_map/ppermute | solution.py:380
  21.8 2.7 %collective-permute-start.3 = (bf16[152,128]{1,0:T(8,128)(2,1)S(1)}, bf16[152,128]{1,0:T(8,128)(2,1)S(1)}, u32[]{:S(2)}, u32[]{:S(2)}) collective-permute-start(bf16[152,128]{1,0:T(8,128)(2,1)S(1)} %bitcast.23), channel_id=1, source_target_pairs={{0,64},{32,96},{64,0},{96,32},{1,65},{33,97},{65,1},{97,33},{2,66}... | collective-permute-start | bytes 116744 | tf_op jit(solution)/shard_map/ppermute | solution.py:380
  24.5 1.5 %collective-permute-start.4 = (bf16[152,128]{1,0:T(8,128)(2,1)S(1)}, bf16[152,128]{1,0:T(8,128)(2,1)S(1)}, u32[]{:S(2)}, u32[]{:S(2)}) collective-permute-start(bf16[152,128]{1,0:T(8,128)(2,1)S(1)} %bitcast.22), channel_id=1, source_target_pairs={{0,96},{32,0},{64,32},{96,64},{1,97},{33,1},{65,33},{97,65},{2,98}... | collective-permute-start | bytes 116744 | tf_op jit(solution)/shard_map/ppermute | solution.py:380
  25.9 0.4 collective-permute-done.1.pair
  26.3 0.3 turn.1.qt
  26.6 1.0 %collective-permute-done.2.r1 = bf16[152,128]{1,0:T(8,128)(2,1)S(1)} collective-permute-done((bf16[152,128]{1,0:T(8,128)(2,1)S(1)}, bf16[152,128]{1,0:T(8,128)(2,1)S(1)}, u32[]{:S(2)}, u32[]{:S(2)}) %collective-permute-start.2) | collective-permute-done | bytes 38944 | tf_op jit(solution)/shard_map/ppermute | solution.py:380
  27.6 1.0 %collective-permute-done.3.r2 = bf16[152,128]{1,0:T(8,128)(2,1)S(1)} collective-permute-done((bf16[152,128]{1,0:T(8,128)(2,1)S(1)}, bf16[152,128]{1,0:T(8,128)(2,1)S(1)}, u32[]{:S(2)}, u32[]{:S(2)}) %collective-permute-start.3) | collective-permute-done | bytes 38944 | tf_op jit(solution)/shard_map/ppermute | solution.py:380
  28.6 2.7 %first.1 = (f32[136,512]{1,0:T(8,128)S(1)}, bf16[2432,256]{1,0:T(8,128)(2,1)S(1)}, bf16[144,2432]{1,0:T(8,128)(2,1)S(1)}) custom-call(bf16[4,256,512]{2,1,0:T(8,128)(2,1)S(1)} %turn.1.qt, bf16[16,256,128]{2,1,0:T(8,128)(2,1)S(1)} %bitcast.14, bf16[152,128]{1,0:T(8,128)(2,1)S(1)} %bitcast.20, bf16[152,128]{1,0:T(8,128)(2,1)S(1)} %collective-permute-done.2.r1, ...), custom_call_target="tpu_custom_call" | custom-call | flops 1048576 | bytes 65536 | tf_op jit(solution)/shard_map/first/pallas_call | solution.py:325
  31.3 3.1 %collective-permute-start.5 = (f16[136,512]{1,0:T(8,128)(2,1)S(1)}, f16[136,512]{1,0:T(8,128)(2,1)S(1)}, u32[]{:S(2)}, u32[]{:S(2)}) collective-permute-start(f16[136,512]{1,0:T(8,128)(2,1)S(1)} %convert_element_type.15), channel_id=1, source_target_pairs={{0,16},{8,24},{16,0},{24,8},{1,17},{9,25},{17,1},{25,9},{2,18},{10... | collective-permute-start | bytes 417800 | tf_op jit(solution)/shard_map/ppermute | solution.py:384
  34.4 3.9 %more.3 = (f32[136,512]{1,0:T(8,128)S(1)}, f32[136,512]{1,0:T(8,128)S(1)}) custom-call(bf16[4,256,512]{2,1,0:T(8,128)(2,1)S(1)} %turn.1.qt, bf16[2432,256]{1,0:T(8,128)(2,1)S(1)} %get-tuple-element.20.kk, bf16[144,2432]{1,0:T(8,128)(2,1)S(1)} %get-tuple-element.21.vt), custom_call_target="tpu_custom_call" | custom-call | flops 2097152 | bytes 131072 | tf_op jit(solution)/shard_map/more/pallas_call | solution.py:343
  38.4 9.6 %collective-permute-start.7 = (f16[136,512]{1,0:T(8,128)(2,1)S(1)}, f16[136,512]{1,0:T(8,128)(2,1)S(1)}, u32[]{:S(2)}, u32[]{:S(2)}) collective-permute-start(f16[136,512]{1,0:T(8,128)(2,1)S(1)} %convert_element_type.18), channel_id=1, source_target_pairs={{0,24},{8,16},{16,8},{24,0},{1,25},{9,17},{17,9},{25,1},{2,26},{10... | collective-permute-start | bytes 417800 | tf_op jit(solution)/shard_map/ppermute | solution.py:384
  48.1 2.0 %more.2.g0 = f32[136,512]{1,0:T(8,128)S(1)} custom-call(bf16[4,256,512]{2,1,0:T(8,128)(2,1)S(1)} %turn.1.qt, bf16[2432,256]{1,0:T(8,128)(2,1)S(1)} %get-tuple-element.20.kk, bf16[144,2432]{1,0:T(8,128)(2,1)S(1)} %get-tuple-element.21.vt, f32[136,512]{1,0:T(8,128)S(1)} %convert_element_type.16.refs_0_.g2), custom_call_target="tpu_custom_call" | custom-call | flops 1048576 | bytes 65536 | tf_op jit(solution)/shard_map/more/pallas_call | solution.py:343
  50.1 1.0 %collective-permute-done.7 = f16[136,512]{1,0:T(8,128)(2,1)S(1)} collective-permute-done((f16[136,512]{1,0:T(8,128)(2,1)S(1)}, f16[136,512]{1,0:T(8,128)(2,1)S(1)}, u32[]{:S(2)}, u32[]{:S(2)}) %collective-permute-start.7) | collective-permute-done | bytes 139296 | tf_op jit(solution)/shard_map/ppermute | solution.py:384
  51.1 2.0 %collective-permute-done.6 = f16[136,512]{1,0:T(8,128)(2,1)S(1)} collective-permute-done((f16[136,512]{1,0:T(8,128)(2,1)S(1)}, f16[136,512]{1,0:T(8,128)(2,1)S(1)}, u32[]{:S(2)}, u32[]{:S(2)}) %collective-permute-start.6) | collective-permute-done | bytes 139296 | tf_op jit(solution)/shard_map/ppermute | solution.py:384
  53.1 0.1 maximum_convert_fusion.g
  53.2 0.8 %combine.1 = bf16[128,512]{1,0:T(8,128)(2,1)} custom-call(f32[136,512]{1,0:T(8,128)S(1)} %more.2.g0, f32[136,512]{1,0:T(8,128)S(1)} %convert_element_type.16.refs_0_.g2, f32[2,136,512]{2,1,0:T(8,128)S(1)} %maximum_convert_fusion.g), custom_call_target="tpu_custom_call" | custom-call | tf_op jit(solution)/shard_map/combine/pallas_call | solution.py:369
  (17 shorter events, 0.1 us)
Async XLA Ops:
  2.7 8.6 %copy-start.2 = (bf16[1,128,512]{2,1,0:T(8,128)(2,1)S(1)}, bf16[1,128,512]{2,1,0:T(8,128)(2,1)}, u32[]{:S(2)}) copy-start(bf16[1,128,512]{2,1,0:T(8,128)(2,1)} %param.8) | copy-start | bytes 393220
  2.7 13.0 %copy-start = (bf16[8,4,2,32,2,128]{5,4,3,2,1,0:T(2,128)(2,1)S(1)}, bf16[8,4,2,32,2,128]{5,4,3,2,1,0:T(2,128)(2,1)}, u32[]{:S(2)}) copy-start(bf16[8,4,2,32,2,128]{5,4,3,2,1,0:T(2,128)(2,1)} %pack.1.after) | copy-start | bytes 3145732
  2.7 13.0 %copy-start.1 = (bf16[1,12,32,2,512]{4,3,2,1,0:T(2,128)(2,1)S(1)}, bf16[1,12,32,2,512]{4,3,2,1,0:T(2,128)(2,1)}, u32[]{:S(2)}) copy-start(bf16[1,12,32,2,512]{4,3,2,1,0:T(2,128)(2,1)} %param.10) | copy-start | bytes 2359300
  2.7 13.0 %copy-start.3 = (bf16[1,8,2,512]{3,2,1,0:T(2,128)(2,1)S(1)}, bf16[1,8,2,512]{3,2,1,0:T(2,128)(2,1)}, u32[]{:S(2)}) copy-start(bf16[1,8,2,512]{3,2,1,0:T(2,128)(2,1)} %param.9) | copy-start | bytes 49156
  2.7 13.0 %copy-start.4 = (s32[1,4]{1,0:T(1,128)S(1)}, s32[1,4]{1,0:T(1,128)}, u32[]{:S(2)}) copy-start(s32[1,4]{1,0:T(1,128)} %table.1) | copy-start | bytes 52
  2.7 25.8 %all-to-all-start = ((bf16[32,128,128]{2,1,0:T(8,128)(2,1)}), bf16[32,128,128]{2,1,0:T(8,128)(2,1)S(1)}, u32[]{:S(2)}, u32[]{:S(2)}) async-start(bf16[32,128,128]{2,1,0:T(8,128)(2,1)} %bitcast.13), calls=%async_computation | async-start | bytes 2097152 | tf_op jit(solution)/shard_map/all_to_all | solution.py:393
  11.3 7.3 %collective-permute-start = (bf16[128,512]{1,0:T(8,128)(2,1)S(1)}, bf16[128,512]{1,0:T(8,128)(2,1)S(1)}, u32[]{:S(2)}, u32[]{:S(2)}) collective-permute-start(bf16[128,512]{1,0:T(8,128)(2,1)S(1)} %bitcast.17), channel_id=1, source_target_pairs={{0,16},{8,24},{16,0},{24,8},{1,17},{9,25},{17,1},{25,9},{2,18},{10... | collective-permute-start | bytes 393224 | tf_op jit(solution)/shard_map/ppermute | solution.py:384
  18.6 7.8 %collective-permute-start.1 = (bf16[256,512]{1,0:T(8,128)(2,1)S(1)}, bf16[256,512]{1,0:T(8,128)(2,1)S(1)}, u32[]{:S(2)}, u32[]{:S(2)}) collective-permute-start(bf16[256,512]{1,0:T(8,128)(2,1)S(1)} %pad_maximum_fusion), channel_id=1, source_target_pairs={{0,8},{8,0},{16,24},{24,16},{1,9},{9,1},{17,25},{25,17},{2,10},{10... | collective-permute-start | bytes 786440 | tf_op jit(solution)/shard_map/ppermute | solution.py:384
  20.1 7.5 %collective-permute-start.2 = (bf16[152,128]{1,0:T(8,128)(2,1)S(1)}, bf16[152,128]{1,0:T(8,128)(2,1)S(1)}, u32[]{:S(2)}, u32[]{:S(2)}) collective-permute-start(bf16[152,128]{1,0:T(8,128)(2,1)S(1)} %bitcast.24), channel_id=1, source_target_pairs={{0,32},{32,64},{64,96},{96,0},{1,33},{33,65},{65,97},{97,1},{2,34}... | collective-permute-start | bytes 116744 | tf_op jit(solution)/shard_map/ppermute | solution.py:380
  21.8 6.8 %collective-permute-start.3 = (bf16[152,128]{1,0:T(8,128)(2,1)S(1)}, bf16[152,128]{1,0:T(8,128)(2,1)S(1)}, u32[]{:S(2)}, u32[]{:S(2)}) collective-permute-start(bf16[152,128]{1,0:T(8,128)(2,1)S(1)} %bitcast.23), channel_id=1, source_target_pairs={{0,64},{32,96},{64,0},{96,32},{1,65},{33,97},{65,1},{97,33},{2,66}... | collective-permute-start | bytes 116744 | tf_op jit(solution)/shard_map/ppermute | solution.py:380
  24.5 4.1 %collective-permute-start.4 = (bf16[152,128]{1,0:T(8,128)(2,1)S(1)}, bf16[152,128]{1,0:T(8,128)(2,1)S(1)}, u32[]{:S(2)}, u32[]{:S(2)}) collective-permute-start(bf16[152,128]{1,0:T(8,128)(2,1)S(1)} %bitcast.22), channel_id=1, source_target_pairs={{0,96},{32,0},{64,32},{96,64},{1,97},{33,1},{65,33},{97,65},{2,98}... | collective-permute-start | bytes 116744 | tf_op jit(solution)/shard_map/ppermute | solution.py:380
  31.3 16.7 %collective-permute-start.5 = (f16[136,512]{1,0:T(8,128)(2,1)S(1)}, f16[136,512]{1,0:T(8,128)(2,1)S(1)}, u32[]{:S(2)}, u32[]{:S(2)}) collective-permute-start(f16[136,512]{1,0:T(8,128)(2,1)S(1)} %convert_element_type.15), channel_id=1, source_target_pairs={{0,16},{8,24},{16,0},{24,8},{1,17},{9,25},{17,1},{25,9},{2,18},{10... | collective-permute-start | bytes 417800 | tf_op jit(solution)/shard_map/ppermute | solution.py:384
  38.4 12.7 %collective-permute-start.7 = (f16[136,512]{1,0:T(8,128)(2,1)S(1)}, f16[136,512]{1,0:T(8,128)(2,1)S(1)}, u32[]{:S(2)}, u32[]{:S(2)}) collective-permute-start(f16[136,512]{1,0:T(8,128)(2,1)S(1)} %convert_element_type.18), channel_id=1, source_target_pairs={{0,24},{8,16},{16,8},{24,0},{1,25},{9,17},{17,9},{25,1},{2,26},{10... | collective-permute-start | bytes 417800 | tf_op jit(solution)/shard_map/ppermute | solution.py:384
  48.0 5.1 %collective-permute-start.6 = (f16[136,512]{1,0:T(8,128)(2,1)S(1)}, f16[136,512]{1,0:T(8,128)(2,1)S(1)}, u32[]{:S(2)}, u32[]{:S(2)}) collective-permute-start(f16[136,512]{1,0:T(8,128)(2,1)S(1)} %convert_element_type.17), channel_id=1, source_target_pairs={{0,8},{8,0},{16,24},{24,16},{1,9},{9,1},{17,25},{25,17},{2,10},{10... | collective-permute-start | bytes 417800 | tf_op jit(solution)/shard_map/ppermute | solution.py:384

commit v7 on v6

--- a/solution.py
+++ b/solution.py
@@ -287,8 +287,14 @@
     emit(out, sums, best)
 
 
+def place_of(k):
+    core = here()[2] & 1
+    return {"near": 1 + 2 * core, "next": 3 - 2 * core}.get(k, k)
+
+
 def attend(ks, outs, qt, kk, vt, s_ref):
     bad = []
+    ks = [place_of(k) for k in ks]
     for k, out in zip(ks, outs):
         q = qt[k]
         top = jnp.max(jnp.dot(kk[SAMPLE], q, preferred_element_type=F32), axis=0, keepdims=True)
@@ -338,8 +344,7 @@
     )(qt, mig, *parts)
 
 
-def more(ks, qt, kk, vt, after=None):
-    late = () if after is None else (after,)
+def more(ks, qt, kk, vt, late=()):
     return pl.pallas_call(
         functools.partial(more_kernel, ks),
         in_specs=[VMEM] * 3 + [HBM] * len(late),
@@ -352,8 +357,8 @@
     )(qt, kk, vt, *late)
 
 
-def combine_kernel(g0, g2, g, out):
-    parts = (g0, g2, g.at[0], g.at[1])
+def combine_kernel(*refs):
+    *parts, out = refs
     dens = [x[128:129] + x[129:130] for x in parts]
     top = functools.reduce(jnp.maximum, dens)
     share = 1.0 / sum(jnp.exp2(x - top) for x in dens)
@@ -368,7 +373,7 @@
 def combine(*parts):
     return pl.pallas_call(
         combine_kernel,
-        in_specs=[VMEM] * 3,
+        in_specs=[VMEM] * 4,
         out_specs=VMEM,
         out_shape=jax.ShapeDtypeStruct((128, 512), BF),
         compiler_params=pltpu.CompilerParams(vmem_limit_bytes=8 << 20),
@@ -382,6 +387,11 @@
 
 def swap(value, k):
     return lax.ppermute(value, "x", [(i, i ^ k) for i in range(4)])
+
+
+def beside(value, turn):
+    pairs = [(x * INST + b, (x ^ (1 + 2 * ((b + turn) % 2))) * INST + b) for x in range(4) for b in range(INST)]
+    return lax.ppermute(value, ("x", "ba"), pairs)
 
 
 def local(queries, new_kv, pool, page_table, ctx_len, move_page, move_dest, append_page):
@@ -401,11 +411,12 @@
     qt = turn(q, q2, pair)
     out2, kk, vt = first(2, qt, mig.reshape(MIG_ROWS // 128, 256, D), parts)
     got2 = swap(out2.astype(F16), 2).astype(F32)
-    out1, out3 = more((1, 3), qt, kk, vt)
-    sent = [swap(out.astype(F16), k) for k, out in ((1, out1), (3, out3))]
-    got = jnp.stack(sent).astype(F32)
-    (out0,) = more((0,), qt, kk, vt, after=got2)
-    return combine(out0, got2, got)[None], updated[None]
+    (near,) = more(("near",), qt, kk, vt)
+    got = beside(near.astype(F16), 0).astype(F32)
+    (other,) = more(("next",), qt, kk, vt)
+    last = beside(other.astype(F16), 1).astype(F32)
+    (out0,) = more((0,), qt, kk, vt, late=(got2, got))
+    return combine(out0, got2, got, last)[None], updated[None]
 
 
 def solution(mesh):

time: 54.1 us -> 54.1 us (level)
  the two profiles are of different devices: /device:TPU:0 before, /device:TPU:6 now
where the time goes in v7:
time: 54.1 us; the launch traced here: 53.1 us
  Pallas kernels  25.5 us (47%)
  starting transfers between devices  18.3 us (34%)
  waiting for transfers between devices  6.97 us (13%)
  between operations  2.16 us (4%)
    pallas_call x3, Pallas kernels, more(): pl.pallas_call(functools.partial(more_kernel, ks), in_specs=[VMEM] * 3 +...  15.1 us
    all_to_all x1, starting transfers between devices, local(): mig = lax.all_to_all(mig, ('ba', 'y'), 0, 0, tiled=True)  8.47 us
    ppermute x3, starting transfers between devices, shift(): return lax.ppermute(value, axis, [(i, (i + k) % 4) for i in range(4)])  5.8 us
    pallas_call x1, Pallas kernels, first(): pl.pallas_call(functools.partial(first_kernel, k), in_specs=[VMEM] * 6, o...  5.65 us
    ppermute x3, starting transfers between devices, swap(): return lax.ppermute(value, 'x', [(i, i ^ k) for i in range(4)])  3.87 us
    ppermute x3, waiting for transfers between devices, swap(): return lax.ppermute(value, 'x', [(i, i ^ k) for i in range(4)])  3.77 us
    pallas_call x1, Pallas kernels, pack(): pl.pallas_call(pack_kernel, in_specs=[HBM] * 4, out_specs=HBM, out_shape=...  1.99 us
    ppermute x3, waiting for transfers between devices, shift(): return lax.ppermute(value, axis, [(i, (i + k) % 4) for i in range(4)])  1.99 us
  transfers between devices with their start and end apart: 9, of which 5 were waited for; matrix products, arithmetic and copies ran while one was open for 0% of the time, Pallas kernels for 32%

profile of v7, /device:TPU:6, one launch (start us, length us, event | category | flops | bytes accessed | tf_op | source)
XLA Modules:
  0.0 53.1 jit_solution(8072736025934717063)
XLA Ops:
  0.6 2.0 %pack.1.after = bf16[8,4,2,32,2,128]{5,4,3,2,1,0:T(2,128)(2,1)} custom-call(s32[1,4]{1,0:T(1,128)} %table.1, s32[1,7]{1,0:T(1,128)} %page_in.1, s32[1,7]{1,0:T(1,128)} %dest_in.1, bf16[12,32,2,512]{3,2,1,0:T(2,128)(2,1)} %bitcast.13), custom_call_target="tpu_custom_call" | custom-call | tf_op jit(solution)/shard_map/pack/pallas_call | solution.py:100
  2.6 0.0 copy-start.2
  2.7 0.0 copy-start.4
  2.7 8.5 %all-to-all-start = ((bf16[32,128,128]{2,1,0:T(8,128)(2,1)}), bf16[32,128,128]{2,1,0:T(8,128)(2,1)S(1)}, u32[]{:S(2)}, u32[]{:S(2)}) async-start(bf16[32,128,128]{2,1,0:T(8,128)(2,1)} %bitcast.11), calls=%async_computation | async-start | bytes 2097152 | tf_op jit(solution)/shard_map/all_to_all | solution.py:403
  11.2 1.5 %collective-permute-start = (bf16[128,512]{1,0:T(8,128)(2,1)S(1)}, bf16[128,512]{1,0:T(8,128)(2,1)S(1)}, u32[]{:S(2)}, u32[]{:S(2)}) collective-permute-start(bf16[128,512]{1,0:T(8,128)(2,1)S(1)} %bitcast.15), channel_id=1, source_target_pairs={{0,16},{8,24},{16,0},{24,8},{1,17},{9,25},{17,1},{25,9},{2,18},{10... | collective-permute-start | bytes 393224 | tf_op jit(solution)/shard_map/ppermute | solution.py:389
  14.0 1.7 %settle.1 = (bf16[76,2,128]{2,1,0:T(2,128)(2,1)S(1)}, bf16[76,2,128]{2,1,0:T(2,128)(2,1)S(1)}, bf16[76,2,128]{2,1,0:T(2,128)(2,1)S(1)}, bf16[76,2,128]{2,1,0:T(2,128)(2,1)S(1)}, bf16[12,32,2,512]{3,2,1,0:T(2,128)(2,1)}) custom-call(s32[1,4]{1,0:T(1,128)S(1)} %copy-done.4, s32[1,1]{1,0:T(1,128)S(6)} %copy.10.ctx, s32[1,1]{1,0:T(1,128)S(6)} %copy.11.page, ...), custom_call_target="tpu_custom_call" | custom-call | flops 1048576 | bytes 65536 | tf_op jit(solution)/shard_map/settle/pallas_call | solution.py:151
  15.7 2.7 %collective-permute-done.q2 = bf16[128,512]{1,0:T(8,128)(2,1)S(1)} collective-permute-done((bf16[128,512]{1,0:T(8,128)(2,1)S(1)}, bf16[128,512]{1,0:T(8,128)(2,1)S(1)}, u32[]{:S(2)}, u32[]{:S(2)}) %collective-permute-start) | collective-permute-done | bytes 131104 | tf_op jit(solution)/shard_map/ppermute | solution.py:389
  18.5 0.9 %collective-permute-start.1 = (bf16[256,512]{1,0:T(8,128)(2,1)S(1)}, bf16[256,512]{1,0:T(8,128)(2,1)S(1)}, u32[]{:S(2)}, u32[]{:S(2)}) collective-permute-start(bf16[256,512]{1,0:T(8,128)(2,1)S(1)} %pad_maximum_fusion), channel_id=1, source_target_pairs={{0,8},{8,0},{16,24},{24,16},{1,9},{9,1},{17,25},{25,17},{2,10},{10... | collective-permute-start | bytes 786440 | tf_op jit(solution)/shard_map/ppermute | solution.py:389
  19.4 1.7 %collective-permute-start.2 = (bf16[152,128]{1,0:T(8,128)(2,1)S(1)}, bf16[152,128]{1,0:T(8,128)(2,1)S(1)}, u32[]{:S(2)}, u32[]{:S(2)}) collective-permute-start(bf16[152,128]{1,0:T(8,128)(2,1)S(1)} %bitcast.22), channel_id=1, source_target_pairs={{0,32},{32,64},{64,96},{96,0},{1,33},{33,65},{65,97},{97,1},{2,34}... | collective-permute-start | bytes 116744 | tf_op jit(solution)/shard_map/ppermute | solution.py:385
  21.0 2.7 %collective-permute-start.3 = (bf16[152,128]{1,0:T(8,128)(2,1)S(1)}, bf16[152,128]{1,0:T(8,128)(2,1)S(1)}, u32[]{:S(2)}, u32[]{:S(2)}) collective-permute-start(bf16[152,128]{1,0:T(8,128)(2,1)S(1)} %bitcast.21), channel_id=1, source_target_pairs={{0,64},{32,96},{64,0},{96,32},{1,65},{33,97},{65,1},{97,33},{2,66}... | collective-permute-start | bytes 116744 | tf_op jit(solution)/shard_map/ppermute | solution.py:385
  23.7 1.5 %collective-permute-start.4 = (bf16[152,128]{1,0:T(8,128)(2,1)S(1)}, bf16[152,128]{1,0:T(8,128)(2,1)S(1)}, u32[]{:S(2)}, u32[]{:S(2)}) collective-permute-start(bf16[152,128]{1,0:T(8,128)(2,1)S(1)} %bitcast.20), channel_id=1, source_target_pairs={{0,96},{32,0},{64,32},{96,64},{1,97},{33,1},{65,33},{97,65},{2,98}... | collective-permute-start | bytes 116744 | tf_op jit(solution)/shard_map/ppermute | solution.py:385
  25.2 1.1 %collective-permute-done.1.pair = bf16[256,512]{1,0:T(8,128)(2,1)S(1)} collective-permute-done((bf16[256,512]{1,0:T(8,128)(2,1)S(1)}, bf16[256,512]{1,0:T(8,128)(2,1)S(1)}, u32[]{:S(2)}, u32[]{:S(2)}) %collective-permute-start.1) | collective-permute-done | bytes 262176 | tf_op jit(solution)/shard_map/ppermute | solution.py:389
  26.2 0.3 turn.1.qt
  26.5 1.0 %collective-permute-done.2.r1 = bf16[152,128]{1,0:T(8,128)(2,1)S(1)} collective-permute-done((bf16[152,128]{1,0:T(8,128)(2,1)S(1)}, bf16[152,128]{1,0:T(8,128)(2,1)S(1)}, u32[]{:S(2)}, u32[]{:S(2)}) %collective-permute-start.2) | collective-permute-done | bytes 38944 | tf_op jit(solution)/shard_map/ppermute | solution.py:385
  27.5 1.0 %collective-permute-done.3.r2 = bf16[152,128]{1,0:T(8,128)(2,1)S(1)} collective-permute-done((bf16[152,128]{1,0:T(8,128)(2,1)S(1)}, bf16[152,128]{1,0:T(8,128)(2,1)S(1)}, u32[]{:S(2)}, u32[]{:S(2)}) %collective-permute-start.3) | collective-permute-done | bytes 38944 | tf_op jit(solution)/shard_map/ppermute | solution.py:385
  28.5 5.7 %first.1 = (f32[136,512]{1,0:T(8,128)S(1)}, bf16[2432,256]{1,0:T(8,128)(2,1)S(1)}, bf16[144,2432]{1,0:T(8,128)(2,1)S(1)}) custom-call(bf16[4,256,512]{2,1,0:T(8,128)(2,1)S(1)} %turn.1.qt, bf16[16,256,128]{2,1,0:T(8,128)(2,1)S(1)} %bitcast.12, bf16[152,128]{1,0:T(8,128)(2,1)S(1)} %bitcast.18, bf16[152,128]{1,0:T(8,128)(2,1)S(1)} %collective-permute-done.2.r1, ...), custom_call_target="tpu_custom_call" | custom-call | flops 1048576 | bytes 65536 | tf_op jit(solution)/shard_map/first/pallas_call | solution.py:331
  34.2 1.5 %collective-permute-start.5 = (f16[136,512]{1,0:T(8,128)(2,1)S(1)}, f16[136,512]{1,0:T(8,128)(2,1)S(1)}, u32[]{:S(2)}, u32[]{:S(2)}) collective-permute-start(f16[136,512]{1,0:T(8,128)(2,1)S(1)} %convert_element_type.18), channel_id=1, source_target_pairs={{0,16},{8,24},{16,0},{24,8},{1,17},{9,25},{17,1},{25,9},{2,18},{10... | collective-permute-start | bytes 417800 | tf_op jit(solution)/shard_map/ppermute | solution.py:389
  35.6 5.1 %more.3 = f32[136,512]{1,0:T(8,128)S(1)} custom-call(bf16[4,256,512]{2,1,0:T(8,128)(2,1)S(1)} %turn.1.qt, bf16[2432,256]{1,0:T(8,128)(2,1)S(1)} %get-tuple-element.18.kk, bf16[144,2432]{1,0:T(8,128)(2,1)S(1)} %get-tuple-element.19.vt), custom_call_target="tpu_custom_call" | custom-call | flops 1048576 | bytes 65536 | tf_op jit(solution)/shard_map/more/pallas_call | solution.py:348
  40.8 0.1 collective-permute-start.6
  40.9 5.0 %more.5 = f32[136,512]{1,0:T(8,128)S(1)} custom-call(bf16[4,256,512]{2,1,0:T(8,128)(2,1)S(1)} %turn.1.qt, bf16[2432,256]{1,0:T(8,128)(2,1)S(1)} %get-tuple-element.18.kk, bf16[144,2432]{1,0:T(8,128)(2,1)S(1)} %get-tuple-element.19.vt), custom_call_target="tpu_custom_call" | custom-call | flops 1048576 | bytes 65536 | tf_op jit(solution)/shard_map/more/pallas_call | solution.py:348
  45.9 0.1 collective-permute-start.7
  46.1 5.0 %more.4.refs_0_ = f32[136,512]{1,0:T(8,128)S(1)} custom-call(bf16[4,256,512]{2,1,0:T(8,128)(2,1)S(1)} %turn.1.qt, bf16[2432,256]{1,0:T(8,128)(2,1)S(1)} %get-tuple-element.18.kk, bf16[144,2432]{1,0:T(8,128)(2,1)S(1)} %get-tuple-element.19.vt, f32[136,512]{1,0:T(8,128)S(1)} %convert_element_type.19.refs_0_.refs_1_, ...), custom_call_target="tpu_custom_call" | custom-call | flops 1048576 | bytes 65536 | tf_op jit(solution)/shard_map/more/pallas_call | solution.py:348
  51.0 1.2 %collective-permute-done.7 = f16[136,512]{1,0:T(8,128)(2,1)S(1)} collective-permute-done((f16[136,512]{1,0:T(8,128)(2,1)S(1)}, f16[136,512]{1,0:T(8,128)(2,1)S(1)}, u32[]{:S(2)}, u32[]{:S(2)}) %collective-permute-start.7) | collective-permute-done | bytes 139296 | tf_op jit(solution)/shard_map/ppermute | solution.py:394
  52.3 0.8 %combine.1 = bf16[128,512]{1,0:T(8,128)(2,1)} custom-call(f32[136,512]{1,0:T(8,128)S(1)} %more.4.refs_0_, f32[136,512]{1,0:T(8,128)S(1)} %convert_element_type.19.refs_0_.refs_1_, f32[136,512]{1,0:T(8,128)S(1)} %convert_element_type.21.refs_1_.refs_2_, f32[136,512]{1,0:T(8,128)S(1)} %convert_element_type.23.refs_3_), custom_call_target="tpu_custom_call" | custom-call | tf_op jit(solution)/shard_map/combine/pallas_call | solution.py:374
  (19 shorter events, 0.2 us)
Async XLA Ops:
  2.6 8.5 %copy-start.2 = (bf16[1,128,512]{2,1,0:T(8,128)(2,1)S(1)}, bf16[1,128,512]{2,1,0:T(8,128)(2,1)}, u32[]{:S(2)}) copy-start(bf16[1,128,512]{2,1,0:T(8,128)(2,1)} %param.8) | copy-start | bytes 393220
  2.6 11.3 %copy-start = (bf16[8,4,2,32,2,128]{5,4,3,2,1,0:T(2,128)(2,1)S(1)}, bf16[8,4,2,32,2,128]{5,4,3,2,1,0:T(2,128)(2,1)}, u32[]{:S(2)}) copy-start(bf16[8,4,2,32,2,128]{5,4,3,2,1,0:T(2,128)(2,1)} %pack.1.after) | copy-start | bytes 3145732
  2.7 11.3 %copy-start.1 = (bf16[1,12,32,2,512]{4,3,2,1,0:T(2,128)(2,1)S(1)}, bf16[1,12,32,2,512]{4,3,2,1,0:T(2,128)(2,1)}, u32[]{:S(2)}) copy-start(bf16[1,12,32,2,512]{4,3,2,1,0:T(2,128)(2,1)} %param.10) | copy-start | bytes 2359300
  2.7 11.3 %copy-start.3 = (bf16[1,8,2,512]{3,2,1,0:T(2,128)(2,1)S(1)}, bf16[1,8,2,512]{3,2,1,0:T(2,128)(2,1)}, u32[]{:S(2)}) copy-start(bf16[1,8,2,512]{3,2,1,0:T(2,128)(2,1)} %param.9) | copy-start | bytes 49156
  2.7 11.3 %copy-start.4 = (s32[1,4]{1,0:T(1,128)S(1)}, s32[1,4]{1,0:T(1,128)}, u32[]{:S(2)}) copy-start(s32[1,4]{1,0:T(1,128)} %table.1) | copy-start | bytes 52
  2.7 25.8 %all-to-all-start = ((bf16[32,128,128]{2,1,0:T(8,128)(2,1)}), bf16[32,128,128]{2,1,0:T(8,128)(2,1)S(1)}, u32[]{:S(2)}, u32[]{:S(2)}) async-start(bf16[32,128,128]{2,1,0:T(8,128)(2,1)} %bitcast.11), calls=%async_computation | async-start | bytes 2097152 | tf_op jit(solution)/shard_map/all_to_all | solution.py:403
  11.2 7.3 %collective-permute-start = (bf16[128,512]{1,0:T(8,128)(2,1)S(1)}, bf16[128,512]{1,0:T(8,128)(2,1)S(1)}, u32[]{:S(2)}, u32[]{:S(2)}) collective-permute-start(bf16[128,512]{1,0:T(8,128)(2,1)S(1)} %bitcast.15), channel_id=1, source_target_pairs={{0,16},{8,24},{16,0},{24,8},{1,17},{9,25},{17,1},{25,9},{2,18},{10... | collective-permute-start | bytes 393224 | tf_op jit(solution)/shard_map/ppermute | solution.py:389
  18.5 7.8 %collective-permute-start.1 = (bf16[256,512]{1,0:T(8,128)(2,1)S(1)}, bf16[256,512]{1,0:T(8,128)(2,1)S(1)}, u32[]{:S(2)}, u32[]{:S(2)}) collective-permute-start(bf16[256,512]{1,0:T(8,128)(2,1)S(1)} %pad_maximum_fusion), channel_id=1, source_target_pairs={{0,8},{8,0},{16,24},{24,16},{1,9},{9,1},{17,25},{25,17},{2,10},{10... | collective-permute-start | bytes 786440 | tf_op jit(solution)/shard_map/ppermute | solution.py:389
  19.4 8.1 %collective-permute-start.2 = (bf16[152,128]{1,0:T(8,128)(2,1)S(1)}, bf16[152,128]{1,0:T(8,128)(2,1)S(1)}, u32[]{:S(2)}, u32[]{:S(2)}) collective-permute-start(bf16[152,128]{1,0:T(8,128)(2,1)S(1)} %bitcast.22), channel_id=1, source_target_pairs={{0,32},{32,64},{64,96},{96,0},{1,33},{33,65},{65,97},{97,1},{2,34}... | collective-permute-start | bytes 116744 | tf_op jit(solution)/shard_map/ppermute | solution.py:385
  21.0 7.4 %collective-permute-start.3 = (bf16[152,128]{1,0:T(8,128)(2,1)S(1)}, bf16[152,128]{1,0:T(8,128)(2,1)S(1)}, u32[]{:S(2)}, u32[]{:S(2)}) collective-permute-start(bf16[152,128]{1,0:T(8,128)(2,1)S(1)} %bitcast.21), channel_id=1, source_target_pairs={{0,64},{32,96},{64,0},{96,32},{1,65},{33,97},{65,1},{97,33},{2,66}... | collective-permute-start | bytes 116744 | tf_op jit(solution)/shard_map/ppermute | solution.py:385
  23.7 4.8 %collective-permute-start.4 = (bf16[152,128]{1,0:T(8,128)(2,1)S(1)}, bf16[152,128]{1,0:T(8,128)(2,1)S(1)}, u32[]{:S(2)}, u32[]{:S(2)}) collective-permute-start(bf16[152,128]{1,0:T(8,128)(2,1)S(1)} %bitcast.20), channel_id=1, source_target_pairs={{0,96},{32,0},{64,32},{96,64},{1,97},{33,1},{65,33},{97,65},{2,98}... | collective-permute-start | bytes 116744 | tf_op jit(solution)/shard_map/ppermute | solution.py:385
  34.2 11.8 %collective-permute-start.5 = (f16[136,512]{1,0:T(8,128)(2,1)S(1)}, f16[136,512]{1,0:T(8,128)(2,1)S(1)}, u32[]{:S(2)}, u32[]{:S(2)}) collective-permute-start(f16[136,512]{1,0:T(8,128)(2,1)S(1)} %convert_element_type.18), channel_id=1, source_target_pairs={{0,16},{8,24},{16,0},{24,8},{1,17},{9,25},{17,1},{25,9},{2,18},{10... | collective-permute-start | bytes 417800 | tf_op jit(solution)/shard_map/ppermute | solution.py:389
  40.8 5.2 %collective-permute-start.6 = (f16[136,512]{1,0:T(8,128)(2,1)S(1)}, f16[136,512]{1,0:T(8,128)(2,1)S(1)}, u32[]{:S(2)}, u32[]{:S(2)}) collective-permute-start(f16[136,512]{1,0:T(8,128)(2,1)S(1)} %convert_element_type.20), channel_id=1, source_target_pairs={{0,8},{1,25},{2,10},{3,27},{4,12},{5,29},{6,14},{7,31},{8,0},{9,17... | collective-permute-start | bytes 417800 | tf_op jit(solution)/shard_map/ppermute | solution.py:394
  45.9 6.3 %collective-permute-start.7 = (f16[136,512]{1,0:T(8,128)(2,1)S(1)}, f16[136,512]{1,0:T(8,128)(2,1)S(1)}, u32[]{:S(2)}, u32[]{:S(2)}) collective-permute-start(f16[136,512]{1,0:T(8,128)(2,1)S(1)} %convert_element_type.22), channel_id=1, source_target_pairs={{0,24},{1,9},{2,26},{3,11},{4,28},{5,13},{6,30},{7,15},{8,16},{9,1... | collective-permute-start | bytes 417800 | tf_op jit(solution)/shard_map/ppermute | solution.py:394

commit v8 on v6

--- a/solution.py
+++ b/solution.py
@@ -29,7 +29,7 @@
 REST = RES - HALF
 MIG_ROWS = INST * KVH * MOST * PAGE
 OLD_ROWS = (TABLE - MOST) * PAGE * KVH
-ROWS = MIG_ROWS + OLD_ROWS + 128
+ROWS = MIG_ROWS + OLD_ROWS + KVH * NEW_DEV
 SPANS = (0, 1280, ROWS)
 SAMPLE = slice(MIG_ROWS - 128, MIG_ROWS)
 
@@ -167,13 +167,14 @@
 
 def put(x, pick, kk, vt, at, marks=None):
     lane = lax.broadcasted_iota(jnp.int32, (128, 128), 1)
+    size = at.stop - at.start
     keys = jnp.dot(pick[0], x, preferred_element_type=F32)
-    kk[at, 0:128] = keys.astype(BF)
+    kk[at, 0:128] = keys[0:size].astype(BF)
     if marks is None:
         marks = jnp.where((lane == 0) & (keys > 64.0), BIG, 0.0)
-    kk[at, 128:256] = marks.astype(BF)
+    kk[at, 128:256] = marks[0:size].astype(BF)
     vals = lax.dot_general(x, pick[1], (((0,), (0,)), ((), ())), preferred_element_type=F32)
-    vt[0:128, at] = vals.astype(BF)
+    vt[0:128, at] = vals[:, 0:size].astype(BF)
 
 
 def fill(mig, parts, kk, vt):
@@ -208,7 +209,7 @@
     x = jnp.concatenate([r[128:144] for r in parts] + [jnp.zeros((192, 128), BF)], axis=0)
     hot = jnp.where((lane == 1 + sub) & (sub < 32), 1.0, 0.0)
     marks = jnp.where((lane == 0) & (sub >= 32), BIG, hot)
-    put(x, pick, kk, vt, slice(at, at + 128), marks)
+    put(x, pick, kk, vt, slice(at, ROWS), marks)
 
 
 def live_of(live, y):

time: 54.1 us -> 53.7 us (level)
  no operation moved by 1% of the time
where the time goes in v8:
time: 53.7 us; the launch traced here: 53.8 us
  starting transfers between devices  31.6 us (59%)
  Pallas kernels  13.4 us (25%)
  waiting for transfers between devices  6.5 us (12%)
  between operations  2.11 us (4%)
    ppermute x5, starting transfers between devices, swap(): return lax.ppermute(value, 'x', [(i, i ^ k) for i in range(4)])  17.2 us
    all_to_all x1, starting transfers between devices, local(): mig = lax.all_to_all(mig, ('ba', 'y'), 0, 0, tiled=True)  8.57 us
    pallas_call x2, Pallas kernels, more(): pl.pallas_call(functools.partial(more_kernel, ks), in_specs=[VMEM] * 3 +...  5.92 us
    ppermute x3, starting transfers between devices, shift(): return lax.ppermute(value, axis, [(i, (i + k) % 4) for i in range(4)])  5.8 us
    ppermute x5, waiting for transfers between devices, swap(): return lax.ppermute(value, 'x', [(i, i ^ k) for i in range(4)])  4.52 us
    pallas_call x1, Pallas kernels, first(): pl.pallas_call(functools.partial(first_kernel, k), in_specs=[VMEM] * 6, o...  2.68 us
    pallas_call x1, Pallas kernels, pack(): pl.pallas_call(pack_kernel, in_specs=[HBM] * 4, out_specs=HBM, out_shape=...  1.99 us
    ppermute x3, waiting for transfers between devices, shift(): return lax.ppermute(value, axis, [(i, (i + k) % 4) for i in range(4)])  1.99 us
  transfers between devices with their start and end apart: 9, of which 6 were waited for; matrix products, arithmetic and copies ran while one was open for 0% of the time, Pallas kernels for 15%

profile of v8, /device:TPU:0, one launch (start us, length us, event | category | flops | bytes accessed | tf_op | source)
XLA Modules:
  0.0 53.8 jit_solution(6878603953665490917)
XLA Ops:
  0.6 2.0 %pack.1.after = bf16[8,4,2,32,2,128]{5,4,3,2,1,0:T(2,128)(2,1)} custom-call(s32[1,4]{1,0:T(1,128)} %table.1, s32[1,7]{1,0:T(1,128)} %page_in.1, s32[1,7]{1,0:T(1,128)} %dest_in.1, bf16[12,32,2,512]{3,2,1,0:T(2,128)(2,1)} %bitcast.15), custom_call_target="tpu_custom_call" | custom-call | tf_op jit(solution)/shard_map/pack/pallas_call | solution.py:100
  2.6 0.0 copy-start.2
  2.7 0.0 copy-start.3
  2.7 8.6 %all-to-all-start = ((bf16[32,128,128]{2,1,0:T(8,128)(2,1)}), bf16[32,128,128]{2,1,0:T(8,128)(2,1)S(1)}, u32[]{:S(2)}, u32[]{:S(2)}) async-start(bf16[32,128,128]{2,1,0:T(8,128)(2,1)} %bitcast.13), calls=%async_computation | async-start | bytes 2097152 | tf_op jit(solution)/shard_map/all_to_all | solution.py:394
  11.3 3.1 %collective-permute-start = (bf16[128,512]{1,0:T(8,128)(2,1)S(1)}, bf16[128,512]{1,0:T(8,128)(2,1)S(1)}, u32[]{:S(2)}, u32[]{:S(2)}) collective-permute-start(bf16[128,512]{1,0:T(8,128)(2,1)S(1)} %bitcast.17), channel_id=1, source_target_pairs={{0,16},{8,24},{16,0},{24,8},{1,17},{9,25},{17,1},{25,9},{2,18},{10... | collective-permute-start | bytes 393224 | tf_op jit(solution)/shard_map/ppermute | solution.py:385
  15.7 1.7 %settle.1 = (bf16[76,2,128]{2,1,0:T(2,128)(2,1)S(1)}, bf16[76,2,128]{2,1,0:T(2,128)(2,1)S(1)}, bf16[76,2,128]{2,1,0:T(2,128)(2,1)S(1)}, bf16[76,2,128]{2,1,0:T(2,128)(2,1)S(1)}, bf16[12,32,2,512]{3,2,1,0:T(2,128)(2,1)}) custom-call(s32[1,4]{1,0:T(1,128)S(1)} %copy-done.4, s32[1,1]{1,0:T(1,128)S(6)} %copy.10.ctx, s32[1,1]{1,0:T(1,128)S(6)} %copy.11.page, ...), custom_call_target="tpu_custom_call" | custom-call | flops 1048576 | bytes 65536 | tf_op jit(solution)/shard_map/settle/pallas_call | solution.py:151
  17.4 1.1 %collective-permute-done.q2 = bf16[128,512]{1,0:T(8,128)(2,1)S(1)} collective-permute-done((bf16[128,512]{1,0:T(8,128)(2,1)S(1)}, bf16[128,512]{1,0:T(8,128)(2,1)S(1)}, u32[]{:S(2)}, u32[]{:S(2)}) %collective-permute-start) | collective-permute-done | bytes 131104 | tf_op jit(solution)/shard_map/ppermute | solution.py:385
  18.6 1.6 %collective-permute-start.1 = (bf16[256,512]{1,0:T(8,128)(2,1)S(1)}, bf16[256,512]{1,0:T(8,128)(2,1)S(1)}, u32[]{:S(2)}, u32[]{:S(2)}) collective-permute-start(bf16[256,512]{1,0:T(8,128)(2,1)S(1)} %pad_maximum_fusion), channel_id=1, source_target_pairs={{0,8},{8,0},{16,24},{24,16},{1,9},{9,1},{17,25},{25,17},{2,10},{10... | collective-permute-start | bytes 786440 | tf_op jit(solution)/shard_map/ppermute | solution.py:385
  20.1 1.7 %collective-permute-start.2 = (bf16[152,128]{1,0:T(8,128)(2,1)S(1)}, bf16[152,128]{1,0:T(8,128)(2,1)S(1)}, u32[]{:S(2)}, u32[]{:S(2)}) collective-permute-start(bf16[152,128]{1,0:T(8,128)(2,1)S(1)} %bitcast.24), channel_id=1, source_target_pairs={{0,32},{32,64},{64,96},{96,0},{1,33},{33,65},{65,97},{97,1},{2,34}... | collective-permute-start | bytes 116744 | tf_op jit(solution)/shard_map/ppermute | solution.py:381
  21.8 2.7 %collective-permute-start.3 = (bf16[152,128]{1,0:T(8,128)(2,1)S(1)}, bf16[152,128]{1,0:T(8,128)(2,1)S(1)}, u32[]{:S(2)}, u32[]{:S(2)}) collective-permute-start(bf16[152,128]{1,0:T(8,128)(2,1)S(1)} %bitcast.23), channel_id=1, source_target_pairs={{0,64},{32,96},{64,0},{96,32},{1,65},{33,97},{65,1},{97,33},{2,66}... | collective-permute-start | bytes 116744 | tf_op jit(solution)/shard_map/ppermute | solution.py:381
  24.5 1.5 %collective-permute-start.4 = (bf16[152,128]{1,0:T(8,128)(2,1)S(1)}, bf16[152,128]{1,0:T(8,128)(2,1)S(1)}, u32[]{:S(2)}, u32[]{:S(2)}) collective-permute-start(bf16[152,128]{1,0:T(8,128)(2,1)S(1)} %bitcast.22), channel_id=1, source_target_pairs={{0,96},{32,0},{64,32},{96,64},{1,97},{33,1},{65,33},{97,65},{2,98}... | collective-permute-start | bytes 116744 | tf_op jit(solution)/shard_map/ppermute | solution.py:381
  25.9 0.4 collective-permute-done.1.pair
  26.3 0.3 turn.1.qt
  26.6 1.0 %collective-permute-done.2.r1 = bf16[152,128]{1,0:T(8,128)(2,1)S(1)} collective-permute-done((bf16[152,128]{1,0:T(8,128)(2,1)S(1)}, bf16[152,128]{1,0:T(8,128)(2,1)S(1)}, u32[]{:S(2)}, u32[]{:S(2)}) %collective-permute-start.2) | collective-permute-done | bytes 38944 | tf_op jit(solution)/shard_map/ppermute | solution.py:381
  27.6 1.0 %collective-permute-done.3.r2 = bf16[152,128]{1,0:T(8,128)(2,1)S(1)} collective-permute-done((bf16[152,128]{1,0:T(8,128)(2,1)S(1)}, bf16[152,128]{1,0:T(8,128)(2,1)S(1)}, u32[]{:S(2)}, u32[]{:S(2)}) %collective-permute-start.3) | collective-permute-done | bytes 38944 | tf_op jit(solution)/shard_map/ppermute | solution.py:381
  28.6 2.7 %first.1 = (f32[136,512]{1,0:T(8,128)S(1)}, bf16[2336,256]{1,0:T(8,128)(2,1)S(1)}, bf16[144,2336]{1,0:T(8,128)(2,1)S(1)}) custom-call(bf16[4,256,512]{2,1,0:T(8,128)(2,1)S(1)} %turn.1.qt, bf16[16,256,128]{2,1,0:T(8,128)(2,1)S(1)} %bitcast.14, bf16[152,128]{1,0:T(8,128)(2,1)S(1)} %bitcast.20, bf16[152,128]{1,0:T(8,128)(2,1)S(1)} %collective-permute-done.2.r1, ...), custom_call_target="tpu_custom_call" | custom-call | flops 1048576 | bytes 65536 | tf_op jit(solution)/shard_map/first/pallas_call | solution.py:326
  31.3 3.1 %collective-permute-start.5 = (f16[136,512]{1,0:T(8,128)(2,1)S(1)}, f16[136,512]{1,0:T(8,128)(2,1)S(1)}, u32[]{:S(2)}, u32[]{:S(2)}) collective-permute-start(f16[136,512]{1,0:T(8,128)(2,1)S(1)} %convert_element_type.15), channel_id=1, source_target_pairs={{0,16},{8,24},{16,0},{24,8},{1,17},{9,25},{17,1},{25,9},{2,18},{10... | collective-permute-start | bytes 417800 | tf_op jit(solution)/shard_map/ppermute | solution.py:385
  34.4 3.9 %more.3 = (f32[136,512]{1,0:T(8,128)S(1)}, f32[136,512]{1,0:T(8,128)S(1)}) custom-call(bf16[4,256,512]{2,1,0:T(8,128)(2,1)S(1)} %turn.1.qt, bf16[2336,256]{1,0:T(8,128)(2,1)S(1)} %get-tuple-element.20.kk, bf16[144,2336]{1,0:T(8,128)(2,1)S(1)} %get-tuple-element.21.vt), custom_call_target="tpu_custom_call" | custom-call | flops 2097152 | bytes 131072 | tf_op jit(solution)/shard_map/more/pallas_call | solution.py:344
  38.4 9.4 %collective-permute-start.7 = (f16[136,512]{1,0:T(8,128)(2,1)S(1)}, f16[136,512]{1,0:T(8,128)(2,1)S(1)}, u32[]{:S(2)}, u32[]{:S(2)}) collective-permute-start(f16[136,512]{1,0:T(8,128)(2,1)S(1)} %convert_element_type.18), channel_id=1, source_target_pairs={{0,24},{8,16},{16,8},{24,0},{1,25},{9,17},{17,9},{25,1},{2,26},{10... | collective-permute-start | bytes 417800 | tf_op jit(solution)/shard_map/ppermute | solution.py:385
  47.8 2.0 %more.2.g0 = f32[136,512]{1,0:T(8,128)S(1)} custom-call(bf16[4,256,512]{2,1,0:T(8,128)(2,1)S(1)} %turn.1.qt, bf16[2336,256]{1,0:T(8,128)(2,1)S(1)} %get-tuple-element.20.kk, bf16[144,2336]{1,0:T(8,128)(2,1)S(1)} %get-tuple-element.21.vt, f32[136,512]{1,0:T(8,128)S(1)} %convert_element_type.16.refs_0_.g2), custom_call_target="tpu_custom_call" | custom-call | flops 1048576 | bytes 65536 | tf_op jit(solution)/shard_map/more/pallas_call | solution.py:344
  49.8 2.1 %collective-permute-done.7 = f16[136,512]{1,0:T(8,128)(2,1)S(1)} collective-permute-done((f16[136,512]{1,0:T(8,128)(2,1)S(1)}, f16[136,512]{1,0:T(8,128)(2,1)S(1)}, u32[]{:S(2)}, u32[]{:S(2)}) %collective-permute-start.7) | collective-permute-done | bytes 139296 | tf_op jit(solution)/shard_map/ppermute | solution.py:385
  51.9 0.9 %collective-permute-done.6 = f16[136,512]{1,0:T(8,128)(2,1)S(1)} collective-permute-done((f16[136,512]{1,0:T(8,128)(2,1)S(1)}, f16[136,512]{1,0:T(8,128)(2,1)S(1)}, u32[]{:S(2)}, u32[]{:S(2)}) %collective-permute-start.6) | collective-permute-done | bytes 139296 | tf_op jit(solution)/shard_map/ppermute | solution.py:385
  52.9 0.1 maximum_convert_fusion.g
  52.9 0.8 %combine.1 = bf16[128,512]{1,0:T(8,128)(2,1)} custom-call(f32[136,512]{1,0:T(8,128)S(1)} %more.2.g0, f32[136,512]{1,0:T(8,128)S(1)} %convert_element_type.16.refs_0_.g2, f32[2,136,512]{2,1,0:T(8,128)S(1)} %maximum_convert_fusion.g), custom_call_target="tpu_custom_call" | custom-call | tf_op jit(solution)/shard_map/combine/pallas_call | solution.py:370
  (17 shorter events, 0.1 us)
Async XLA Ops:
  2.6 8.6 %copy-start.2 = (bf16[1,128,512]{2,1,0:T(8,128)(2,1)S(1)}, bf16[1,128,512]{2,1,0:T(8,128)(2,1)}, u32[]{:S(2)}) copy-start(bf16[1,128,512]{2,1,0:T(8,128)(2,1)} %param.8) | copy-start | bytes 393220
  2.6 13.0 %copy-start = (bf16[8,4,2,32,2,128]{5,4,3,2,1,0:T(2,128)(2,1)S(1)}, bf16[8,4,2,32,2,128]{5,4,3,2,1,0:T(2,128)(2,1)}, u32[]{:S(2)}) copy-start(bf16[8,4,2,32,2,128]{5,4,3,2,1,0:T(2,128)(2,1)} %pack.1.after) | copy-start | bytes 3145732
  2.6 13.0 %copy-start.1 = (bf16[1,12,32,2,512]{4,3,2,1,0:T(2,128)(2,1)S(1)}, bf16[1,12,32,2,512]{4,3,2,1,0:T(2,128)(2,1)}, u32[]{:S(2)}) copy-start(bf16[1,12,32,2,512]{4,3,2,1,0:T(2,128)(2,1)} %param.10) | copy-start | bytes 2359300
  2.7 13.0 %copy-start.3 = (bf16[1,8,2,512]{3,2,1,0:T(2,128)(2,1)S(1)}, bf16[1,8,2,512]{3,2,1,0:T(2,128)(2,1)}, u32[]{:S(2)}) copy-start(bf16[1,8,2,512]{3,2,1,0:T(2,128)(2,1)} %param.9) | copy-start | bytes 49156
  2.7 13.0 %copy-start.4 = (s32[1,4]{1,0:T(1,128)S(1)}, s32[1,4]{1,0:T(1,128)}, u32[]{:S(2)}) copy-start(s32[1,4]{1,0:T(1,128)} %table.1) | copy-start | bytes 52
  2.7 25.9 %all-to-all-start = ((bf16[32,128,128]{2,1,0:T(8,128)(2,1)}), bf16[32,128,128]{2,1,0:T(8,128)(2,1)S(1)}, u32[]{:S(2)}, u32[]{:S(2)}) async-start(bf16[32,128,128]{2,1,0:T(8,128)(2,1)} %bitcast.13), calls=%async_computation | async-start | bytes 2097152 | tf_op jit(solution)/shard_map/all_to_all | solution.py:394
  11.3 7.3 %collective-permute-start = (bf16[128,512]{1,0:T(8,128)(2,1)S(1)}, bf16[128,512]{1,0:T(8,128)(2,1)S(1)}, u32[]{:S(2)}, u32[]{:S(2)}) collective-permute-start(bf16[128,512]{1,0:T(8,128)(2,1)S(1)} %bitcast.17), channel_id=1, source_target_pairs={{0,16},{8,24},{16,0},{24,8},{1,17},{9,25},{17,1},{25,9},{2,18},{10... | collective-permute-start | bytes 393224 | tf_op jit(solution)/shard_map/ppermute | solution.py:385
  18.6 7.8 %collective-permute-start.1 = (bf16[256,512]{1,0:T(8,128)(2,1)S(1)}, bf16[256,512]{1,0:T(8,128)(2,1)S(1)}, u32[]{:S(2)}, u32[]{:S(2)}) collective-permute-start(bf16[256,512]{1,0:T(8,128)(2,1)S(1)} %pad_maximum_fusion), channel_id=1, source_target_pairs={{0,8},{8,0},{16,24},{24,16},{1,9},{9,1},{17,25},{25,17},{2,10},{10... | collective-permute-start | bytes 786440 | tf_op jit(solution)/shard_map/ppermute | solution.py:385
  20.1 7.5 %collective-permute-start.2 = (bf16[152,128]{1,0:T(8,128)(2,1)S(1)}, bf16[152,128]{1,0:T(8,128)(2,1)S(1)}, u32[]{:S(2)}, u32[]{:S(2)}) collective-permute-start(bf16[152,128]{1,0:T(8,128)(2,1)S(1)} %bitcast.24), channel_id=1, source_target_pairs={{0,32},{32,64},{64,96},{96,0},{1,33},{33,65},{65,97},{97,1},{2,34}... | collective-permute-start | bytes 116744 | tf_op jit(solution)/shard_map/ppermute | solution.py:381
  21.8 6.8 %collective-permute-start.3 = (bf16[152,128]{1,0:T(8,128)(2,1)S(1)}, bf16[152,128]{1,0:T(8,128)(2,1)S(1)}, u32[]{:S(2)}, u32[]{:S(2)}) collective-permute-start(bf16[152,128]{1,0:T(8,128)(2,1)S(1)} %bitcast.23), channel_id=1, source_target_pairs={{0,64},{32,96},{64,0},{96,32},{1,65},{33,97},{65,1},{97,33},{2,66}... | collective-permute-start | bytes 116744 | tf_op jit(solution)/shard_map/ppermute | solution.py:381
  24.5 4.1 %collective-permute-start.4 = (bf16[152,128]{1,0:T(8,128)(2,1)S(1)}, bf16[152,128]{1,0:T(8,128)(2,1)S(1)}, u32[]{:S(2)}, u32[]{:S(2)}) collective-permute-start(bf16[152,128]{1,0:T(8,128)(2,1)S(1)} %bitcast.22), channel_id=1, source_target_pairs={{0,96},{32,0},{64,32},{96,64},{1,97},{33,1},{65,33},{97,65},{2,98}... | collective-permute-start | bytes 116744 | tf_op jit(solution)/shard_map/ppermute | solution.py:381
  31.3 16.5 %collective-permute-start.5 = (f16[136,512]{1,0:T(8,128)(2,1)S(1)}, f16[136,512]{1,0:T(8,128)(2,1)S(1)}, u32[]{:S(2)}, u32[]{:S(2)}) collective-permute-start(f16[136,512]{1,0:T(8,128)(2,1)S(1)} %convert_element_type.15), channel_id=1, source_target_pairs={{0,16},{8,24},{16,0},{24,8},{1,17},{9,25},{17,1},{25,9},{2,18},{10... | collective-permute-start | bytes 417800 | tf_op jit(solution)/shard_map/ppermute | solution.py:385
  38.4 13.6 %collective-permute-start.7 = (f16[136,512]{1,0:T(8,128)(2,1)S(1)}, f16[136,512]{1,0:T(8,128)(2,1)S(1)}, u32[]{:S(2)}, u32[]{:S(2)}) collective-permute-start(f16[136,512]{1,0:T(8,128)(2,1)S(1)} %convert_element_type.18), channel_id=1, source_target_pairs={{0,24},{8,16},{16,8},{24,0},{1,25},{9,17},{17,9},{25,1},{2,26},{10... | collective-permute-start | bytes 417800 | tf_op jit(solution)/shard_map/ppermute | solution.py:385
  47.8 5.1 %collective-permute-start.6 = (f16[136,512]{1,0:T(8,128)(2,1)S(1)}, f16[136,512]{1,0:T(8,128)(2,1)S(1)}, u32[]{:S(2)}, u32[]{:S(2)}) collective-permute-start(f16[136,512]{1,0:T(8,128)(2,1)S(1)} %convert_element_type.17), channel_id=1, source_target_pairs={{0,8},{8,0},{16,24},{24,16},{1,9},{9,1},{17,25},{25,17},{2,10},{10... | collective-permute-start | bytes 417800 | tf_op jit(solution)/shard_map/ppermute | solution.py:385
